TPU v7x, 512 devices: a whole 4x8x8 slice. The times are simulated.
512 devices in a mesh: gx: 16 (over z, core), yz: 8 (over y), body: 4 (over x).
Axes of the slice: x: 4, y: 8, z: 8, core: 2. Of those that a mesh axis runs over, the one named last changes fastest.
Arguments:
- fluid_pos: float32 [3, 32, 16, 8, 128], P(None, 'gx', 'yz', 'body'), may hold values from 0 to 1
- fluid_count: int32 [32, 16, 8], P('gx', 'yz', 'body'), may hold values from 64 to 128
- body_shape: float32 [3, 12288, 128], P(None, ('gx', 'yz', 'body')), may hold values from -2.5 to 2.5
- body_anchor: float32 [3, 12288, 8], P(None, ('gx', 'yz', 'body')), may hold values from -0.5 to 1.5
- body_dest: int32 [12288, 1], P(('gx', 'yz', 'body')), may hold values from 0 to 15; in each aligned block of 24 rows (0 to 23, 24 to 47, ...) at most 3 rows name the same one
- body_cell: int32 [12288, 8], P(('gx', 'yz', 'body')), may hold values from 0 to 7, as said below
Outputs:
- fluid_density: float32 [32, 16, 8, 128], P('gx', 'yz', 'body')
- fluid_accel: float32 [3, 32, 16, 8, 128], P(None, 'gx', 'yz', 'body')
- body_load: float32 [6, 12288], P(None, ('gx', 'yz', 'body'))
Inputs may be any that keep to these rules, and one draw needn't show every extreme that they name: `fluid_count`: slots at or past a cell's count are padding. `body_dest`: the rows of one device name any index at most 3 times, a bound that some block reaches. `body_cell`: a row lists the local cells ((a0 + a) % 2, (e0 + e) % 2, (f0 + f) % 2), entry k having a = k // 4, e = (k // 2) % 2, f = k % 2.
All inputs are finite; a program needn't handle non-finite values.
Results may differ from a plain program's by a relative error of at most 0.0003.
Values sent between devices are 32-bit elements; how exact they have to be, the bound alone decides.
No kernel may reach another device: no remote copies, remote signals or barrier semaphores. Data moves between devices by JAX's collectives and lax.ppermute only.
A program may use at most 64 MiB of HBM per device.

v0:
```python
import jax
import jax.numpy as jnp
from jax import lax
from jax.sharding import PartitionSpec as P

SLOTS = 128
BODY_PARTS = 128
CAPACITY = 3


stencil_steps = [(a, b, c) for a in (-1, 0, 1) for b in (-1, 0, 1) for c in (-1, 0, 1)]


def with_halo(cells, sides, width):
    for axis, dim in sides:
        count = lax.axis_size(axis)
        ends = count - 1
        head = lax.slice_in_dim(cells, 0, width, axis=dim)
        tail = lax.slice_in_dim(cells, cells.shape[dim] - width, cells.shape[dim], axis=dim)
        cells = jnp.concatenate(
            [
                lax.ppermute(tail, axis, [(i, (i + 1) % count) for i in range(ends)]),
                cells,
                lax.ppermute(head, axis, [((i + 1) % count, i) for i in range(ends)]),
            ],
            axis=dim,
        )
    return cells


def pair_terms(own_tile, near_tile, stencil):
    gap_parts = [
        own_tile[m][..., :, None] - near_tile[m][..., None, :] - float(stencil[m]) for m in range(3)
    ]
    spread = jnp.maximum(
        1.0
        - (gap_parts[0] * gap_parts[0] + gap_parts[1] * gap_parts[1] + gap_parts[2] * gap_parts[2]),
        0.0,
    )
    return (gap_parts, spread)


def pressure_of(density, live_mask):
    safe_den = jnp.where(live_mask > 0, density, 1.0)
    return jnp.where(live_mask > 0, (density - 1.0) / (safe_den * safe_den), 0.0)


def cross_arms(arm_vecs, forces):
    return jnp.stack(
        [
            arm_vecs[:, 1] * forces[:, 2] - arm_vecs[:, 2] * forces[:, 1],
            arm_vecs[:, 2] * forces[:, 0] - arm_vecs[:, 0] * forces[:, 2],
            arm_vecs[:, 0] * forces[:, 1] - arm_vecs[:, 1] * forces[:, 0],
        ],
        axis=1,
    )


def interact(positions, fluid_tiles):
    deltas = positions[:, :, :, None] - fluid_tiles[:, :3, None, :]
    spread = jnp.maximum(1.0 - jnp.sum(deltas * deltas, axis=1), 0.0)
    weight = 24.0 / SLOTS * (fluid_tiles[:, 3] * fluid_tiles[:, 4])[:, None, :] * spread * spread
    pushed = weight[:, None] * deltas
    return (jnp.sum(pushed, axis=3), -jnp.sum(pushed, axis=2))


def blocked_interact(positions, fluid_tiles):
    count_rows = positions.shape[0]
    block_rows = 32
    forces, reaction = lax.map(
        lambda pair: interact(pair[0], pair[1]),
        (
            positions.reshape((count_rows // block_rows, block_rows) + positions.shape[1:]),
            fluid_tiles.reshape((count_rows // block_rows, block_rows) + fluid_tiles.shape[1:]),
        ),
    )
    return (
        forces.reshape((count_rows,) + forces.shape[2:]),
        reaction.reshape((count_rows,) + reaction.shape[2:]),
    )


def local_density(own_tile, cycle_tiles):
    ext_x, ext_y, ext_z = own_tile.shape[1:4]
    summed = jnp.zeros(own_tile.shape[1:], jnp.float32)
    for stencil in stencil_steps:
        near_tile = cycle_tiles[
            :,
            1 + stencil[0] : 1 + stencil[0] + ext_x,
            1 + stencil[1] : 1 + stencil[1] + ext_y,
            1 + stencil[2] : 1 + stencil[2] + ext_z,
        ]
        gap_parts, spread = pair_terms(own_tile, near_tile, stencil)
        summed = summed + jnp.sum(near_tile[3][..., None, :] * spread * spread * spread, axis=-1)
    return own_tile[3] * summed / (SLOTS / 2.0)


def local_accel(own_tile, cycle_tiles):
    ext_x, ext_y, ext_z = own_tile.shape[1:4]
    summed = jnp.zeros((3,) + own_tile.shape[1:], jnp.float32)
    for stencil in stencil_steps:
        near_tile = cycle_tiles[
            :,
            1 + stencil[0] : 1 + stencil[0] + ext_x,
            1 + stencil[1] : 1 + stencil[1] + ext_y,
            1 + stencil[2] : 1 + stencil[2] + ext_z,
        ]
        gap_parts, spread = pair_terms(own_tile, near_tile, stencil)
        weight = (
            own_tile[3][..., :, None]
            * near_tile[3][..., None, :]
            * (own_tile[4][..., :, None] + near_tile[4][..., None, :])
            * spread
            * spread
        )
        summed = summed + jnp.stack([jnp.sum(weight * g, axis=-1) for g in gap_parts])
    return 12.0 / SLOTS * summed


def scatter_cells(reaction, cell_ids, cells_here):
    onehot = (cell_ids[None, :] == jnp.arange(cells_here, dtype=jnp.int32)[:, None]).astype(
        jnp.float32
    )
    return jnp.einsum("cr,rxs->xcs", onehot, reaction, precision=lax.Precision.HIGHEST)


def body_totals(arm_vecs, forces):
    return jnp.concatenate(
        [jnp.sum(forces, axis=2), jnp.sum(cross_arms(arm_vecs, forces), axis=2)], axis=1
    )


def local(fluid_pos, fluid_count, body_shape, body_anchor, body_dest, body_cell):
    tile_slots = fluid_pos.shape[4]
    ext_x, ext_y, ext_z = fluid_pos.shape[1:4]
    live_mask = (
        jnp.arange(tile_slots, dtype=jnp.int32)[None, None, None, :] < fluid_count[..., None]
    ).astype(jnp.float32)
    packed = jnp.concatenate([fluid_pos, live_mask[None]], axis=0)
    cycle_tiles = with_halo(packed, (("gx", 1), ("yz", 2), ("body", 3)), 1)
    density = local_density(packed, cycle_tiles)
    pressure = pressure_of(density, live_mask)
    cycle_press = with_halo(pressure, (("gx", 0), ("yz", 1), ("body", 2)), 1)
    cycle_full = jnp.concatenate([cycle_tiles, cycle_press[None]], axis=0)
    own_full = jnp.concatenate([packed, pressure[None]], axis=0)
    accel_grid = local_accel(own_full, cycle_full)
    cells_here = ext_x * ext_y * ext_z
    tile_table = jnp.transpose(own_full.reshape(5, cells_here, tile_slots), (1, 0, 2))
    groups = lax.axis_size("gx")
    body_rows, covered = body_cell.shape
    body_parts = body_shape.shape[2]
    dest_group = body_dest[:, 0]
    row_order = jnp.arange(body_rows, dtype=jnp.int32)
    earlier = (dest_group[:, None] == dest_group[None, :]) & (
        row_order[None, :] < row_order[:, None]
    )
    slot_rank = jnp.sum(earlier.astype(jnp.int32), axis=1)
    shapes = jnp.transpose(body_shape, (1, 0, 2))
    anchors = jnp.transpose(body_anchor, (1, 0, 2))
    send_cell = (
        jnp.full((groups, CAPACITY, covered), -1, jnp.int32)
        .at[dest_group, slot_rank]
        .set(body_cell)
    )
    got_cell = lax.all_to_all(send_cell, "gx", split_axis=0, concat_axis=0, tiled=True).reshape(-1)
    used_slots = (got_cell >= 0).astype(jnp.float32)
    served = jnp.take(tile_table, jnp.maximum(got_cell, 0), axis=0)
    served = served.at[:, 3].multiply(used_slots[:, None])
    fetched = lax.all_to_all(
        served.reshape(groups, CAPACITY, covered, 5, tile_slots),
        "gx",
        split_axis=0,
        concat_axis=0,
        tiled=True,
    )
    entry_tiles = fetched[dest_group, slot_rank].reshape(body_rows * covered, 5, tile_slots)
    positions = jnp.transpose(anchors, (0, 2, 1))[:, :, :, None] + shapes[:, None]
    forces, reaction = blocked_interact(
        positions.reshape(body_rows * covered, 3, body_parts), entry_tiles
    )
    body_force = jnp.sum(forces.reshape(body_rows, covered, 3, body_parts), axis=1)
    body_loads = body_totals(shapes, body_force)
    send_back = (
        jnp.zeros((groups, CAPACITY, covered, 3, tile_slots), jnp.float32)
        .at[dest_group, slot_rank]
        .set(reaction.reshape(body_rows, covered, 3, tile_slots))
    )
    got_back = lax.all_to_all(send_back, "gx", split_axis=0, concat_axis=0, tiled=True).reshape(
        -1, 3, tile_slots
    )
    fluid_extra = scatter_cells(got_back, got_cell, cells_here)
    fluid_accel = accel_grid + fluid_extra.reshape(3, ext_x, ext_y, ext_z, tile_slots)
    body_load = jnp.transpose(body_loads / BODY_PARTS)
    return (density, fluid_accel, body_load)


def solution(mesh):
    in_specs = (
        P(None, "gx", "yz", "body", None),
        P("gx", "yz", "body"),
        P(None, ("gx", "yz", "body"), None),
        P(None, ("gx", "yz", "body"), None),
        P(("gx", "yz", "body"), None),
        P(("gx", "yz", "body"), None),
    )
    out_specs = (
        P("gx", "yz", "body", None),
        P(None, "gx", "yz", "body", None),
        P(None, ("gx", "yz", "body")),
    )
    return jax.shard_map(local, mesh=mesh, in_specs=in_specs, out_specs=out_specs, check_vma=False)
```

profile of v0, /device:TPU:19, one launch (start us, length us, event | category | flops | bytes accessed | tf_op | source)
XLA Modules:
  0.0 212.7 jit_solution(1855192453176335963)
XLA Ops:
  2.1 4.6 %collective-permute-start = (f32[4,1,2,2,128]{4,3,2,1,0:T(2,128)S(1)}, f32[4,1,2,2,128]{4,3,2,1,0:T(2,128)S(1)}, u32[]{:S(2)}, u32[]{:S(2)}) collective-permute-start(f32[4,1,2,2,128]{4,3,2,1,0:T(2,128)S(1)} %get-tuple-element.396), channel_id=1, source_target_pairs={{0,32},{32,64},{64,96},{96,128},{128,160},{160,192},{192,224},{224... | collective-permute-start | bytes 24584 | tf_op jit(solution)/shard_map/ppermute | solution.py:22
  14.3 11.3 %all-to-all-start = ((s32[16,3,8]{2,1,0:T(4,128)}), s32[16,3,8]{2,1,0:T(4,128)S(1)}, u32[]{:S(2)}, u32[]{:S(2)}) async-start(s32[16,3,8]{2,1,0:T(4,128)} %copy.99), calls=%async_computation | async-start | bytes 65536 | tf_op jit(solution)/shard_map/all_to_all | solution.py:165
  33.8 3.2 %collective-permute-start.2 = (f32[4,4,1,2,128]{4,3,2,1,0:T(2,128)S(1)}, f32[4,4,1,2,128]{4,3,2,1,0:T(2,128)S(1)}, u32[]{:S(2)}, u32[]{:S(2)}) collective-permute-start(f32[4,4,1,2,128]{4,3,2,1,0:T(2,128)S(1)} %get-tuple-element.384), channel_id=1, source_target_pairs={{0,4},{4,8},{8,12},{12,16},{16,20},{20,24},{24,28},{1,5},{5,9},{9,... | collective-permute-start | bytes 49160 | tf_op jit(solution)/shard_map/ppermute | solution.py:22
  39.3 3.3 %collective-permute-done.3 = f32[4,4,1,2,128]{4,3,2,1,0:T(2,128)S(1)} collective-permute-done((f32[4,4,1,2,128]{4,3,2,1,0:T(2,128)S(1)}, f32[4,4,1,2,128]{4,3,2,1,0:T(2,128)S(1)}, u32[]{:S(2)}, u32[]{:S(2)}) %collective-permute-start.3) | collective-permute-done | bytes 16416 | tf_op jit(solution)/shard_map/ppermute | solution.py:24
  42.7 3.1 %collective-permute-start.4 = (f32[4,4,4,1,128]{4,3,2,1,0:T(1,128)S(1)}, f32[4,4,4,1,128]{4,3,2,1,0:T(1,128)S(1)}, u32[]{:S(2)}, u32[]{:S(2)}) collective-permute-start(f32[4,4,4,1,128]{4,3,2,1,0:T(1,128)S(1)} %get-tuple-element.330), channel_id=1, source_target_pairs={{0,1},{1,2},{2,3},{4,5},{5,6},{6,7},{8,9},{9,10},{10,11},{12,13},{... | collective-permute-start | bytes 98312 | tf_op jit(solution)/shard_map/ppermute | solution.py:22
  56.9 2.3 %fusion.104 = (f32[2,2,2,128]{3,2,1,0:T(2,128)S(1)}, f32[2,2,2,128]{3,2,1,0:T(2,128)S(1)}, f32[2,2,2,128]{3,2,1,0:T(2,128)S(1)}, f32[2,2,2,128]{3,2,1,0:T(2,128)S(1)}) fusion(f32[2,2,2,128]{3,2,1,0:T(2,128)} %get-tuple-element.284, f32[2,2,2,128]{3,2,1,0:T(2,128)S(1)} %get-tuple-element.400, f32[2,2,2,128]{3,2,1,0:T(2,128)} %get-tuple-element.285, ...), kind=kLoop, calls=%fused_computation.225 | loop fusion | flops 8515584 | bytes 94208 | tf_op jit(solution)/shard_map/reduce_sum | solution.py:94
  63.9 2.3 %fusion.121 = (f32[2,2,2,128]{3,2,1,0:T(2,128)S(1)}, f32[2,2,2,128]{3,2,1,0:T(2,128)S(1)}, f32[2,2,2,128]{3,2,1,0:T(2,128)S(1)}, f32[2,2,2,128]{3,2,1,0:T(2,128)S(1)}) fusion(f32[2,2,2,128]{3,2,1,0:T(2,128)} %get-tuple-element.301, f32[2,2,2,128]{3,2,1,0:T(2,128)} %get-tuple-element.302, f32[2,2,2,128]{3,2,1,0:T(2,128)} %get-tuple-element.303, ...), kind=kLoop, calls=%fused_computation.242 | loop fusion | flops 8515584 | bytes 94208 | tf_op jit(solution)/shard_map/reduce_sum | solution.py:94
  69.3 5.0 %collective-permute-start.6 = (f32[1,2,2,128]{3,2,1,0:T(2,128)S(1)}, f32[1,2,2,128]{3,2,1,0:T(2,128)S(1)}, u32[]{:S(2)}, u32[]{:S(2)}) collective-permute-start(f32[1,2,2,128]{3,2,1,0:T(2,128)S(1)} %get-tuple-element.403), channel_id=1, source_target_pairs={{0,32},{32,64},{64,96},{96,128},{128,160},{160,192},{192,224},{224... | collective-permute-start | bytes 6152 | tf_op jit(solution)/shard_map/ppermute | solution.py:22
  79.3 4.9 %collective-permute-start.8 = (f32[4,1,2,128]{3,2,1,0:T(2,128)S(1)}, f32[4,1,2,128]{3,2,1,0:T(2,128)S(1)}, u32[]{:S(2)}, u32[]{:S(2)}) collective-permute-start(f32[4,1,2,128]{3,2,1,0:T(2,128)S(1)} %get-tuple-element.401), channel_id=1, source_target_pairs={{0,4},{4,8},{8,12},{12,16},{16,20},{20,24},{24,28},{1,5},{5,9},{9,... | collective-permute-start | bytes 12296 | tf_op jit(solution)/shard_map/ppermute | solution.py:22
  88.5 2.8 %collective-permute-start.10 = (f32[4,4,1,128]{3,2,1,0:T(1,128)S(1)}, f32[4,4,1,128]{3,2,1,0:T(1,128)S(1)}, u32[]{:S(2)}, u32[]{:S(2)}) collective-permute-start(f32[4,4,1,128]{3,2,1,0:T(1,128)S(1)} %get-tuple-element.394), channel_id=1, source_target_pairs={{0,1},{1,2},{2,3},{4,5},{5,6},{6,7},{8,9},{9,10},{10,11},{12,13},{... | collective-permute-start | bytes 24584 | tf_op jit(solution)/shard_map/ppermute | solution.py:22
  91.3 2.5 %collective-permute-start.11 = (f32[4,4,1,128]{3,2,1,0:T(1,128)S(1)}, f32[4,4,1,128]{3,2,1,0:T(1,128)S(1)}, u32[]{:S(2)}, u32[]{:S(2)}) collective-permute-start(f32[4,4,1,128]{3,2,1,0:T(1,128)S(1)} %get-tuple-element.395), channel_id=1, source_target_pairs={{1,0},{2,1},{3,2},{5,4},{6,5},{7,6},{9,8},{10,9},{11,10},{13,12},{... | collective-permute-start | bytes 24584 | tf_op jit(solution)/shard_map/ppermute | solution.py:24
  94.3 4.2 %scatter-mul.4 = f32[384,5,128]{2,1,0:T(8,128)S(1)} dynamic-update-slice(f32[384,5,128]{2,1,0:T(8,128)S(1)} %broadcast_select_fusion, f32[384,1,128]{2,1,0:T(1,128)S(1)} %slice_multiply_fusion.1, s32[]{:T(128)} %copy.137, s32[]{:T(128)} %constant.197.clone.1, s32[]{:T(128)} %copy.137) | dynamic-update-slice | bytes 393220 | tf_op jit(solution)/shard_map/scatter-mul | solution.py:168
  100.0 8.7 %all-to-all-start.1 = ((f32[16,3,8,5,128]{4,2,3,1,0:T(8,128)}), f32[16,3,8,5,128]{4,2,3,1,0:T(8,128)S(1)}, u32[]{:S(2)}, u32[]{:S(2)}) async-start(f32[16,3,8,5,128]{4,2,3,1,0:T(8,128)} %copy.101), calls=%async_computation.1 | async-start | bytes 1966080 | tf_op jit(solution)/shard_map/all_to_all | solution.py:169
  108.9 2.5 %multiply_reduce_fusion.37 = (f32[2,2,2,128]{3,2,1,0:T(2,128)S(1)}, f32[2,2,2,128]{3,2,1,0:T(2,128)S(1)}, f32[2,2,2,128]{3,2,1,0:T(2,128)S(1)}, f32[2,2,2,128]{3...) fusion(f32[2,2,2,128]{3,2,1,0:T(2,128)} %get-tuple-element.354, ...), kind=kLoop, calls=%fused_computation.289 | loop fusion | flops 6023168 | bytes 86016 | tf_op jit(solution)/shard_map/reduce_sum | solution.py:116
  111.4 2.6 %multiply_reduce_fusion.45 = (f32[2,2,2,128]{3,2,1,0:T(2,128)S(1)}, f32[2,2,2,128]{3,2,1,0:T(2,128)S(1)}, f32[2,2,2,128]{3,2,1,0:T(2,128)S(1)}, f32[2,2,2,128]{3...) fusion(f32[2,2,2,128]{3,2,1,0:T(2,128)} %get-tuple-element.282, ...), kind=kLoop, calls=%fused_computation.297 | loop fusion | flops 5892096 | bytes 86016 | tf_op jit(solution)/shard_map/reduce_sum | solution.py:116
  114.0 2.5 %multiply_reduce_fusion.50 = (f32[2,2,2,128]{3,2,1,0:T(2,128)S(1)}, f32[2,2,2,128]{3,2,1,0:T(2,128)S(1)}, f32[2,2,2,128]{3,2,1,0:T(2,128)S(1)}, f32[2,2,2,128]{3...) fusion(f32[2,2,2,128]{3,2,1,0:T(2,128)} %get-tuple-element.341, ...), kind=kLoop, calls=%fused_computation.302 | loop fusion | flops 5892096 | bytes 86016 | tf_op jit(solution)/shard_map/reduce_sum | solution.py:116
  116.6 2.5 %multiply_reduce_fusion.12 = (f32[2,2,2,128]{3,2,1,0:T(2,128)S(1)}, f32[2,2,2,128]{3,2,1,0:T(2,128)S(1)}, f32[2,2,2,128]{3,2,1,0:T(2,128)S(1)}, f32[2,2,2,128]{3...) fusion(f32[2,2,2,128]{3,2,1,0:T(2,128)} %get-tuple-element.259, ...), kind=kLoop, calls=%fused_computation.264 | loop fusion | flops 5892096 | bytes 86016 | tf_op jit(solution)/shard_map/reduce_sum | solution.py:116
  119.1 2.5 %multiply_reduce_fusion.40 = (f32[2,2,2,128]{3,2,1,0:T(2,128)S(1)}, f32[2,2,2,128]{3,2,1,0:T(2,128)S(1)}, f32[2,2,2,128]{3,2,1,0:T(2,128)S(1)}, f32[2,2,2,128]{3...) fusion(f32[2,2,2,128]{3,2,1,0:T(2,128)} %get-tuple-element.271, ...), kind=kLoop, calls=%fused_computation.292 | loop fusion | flops 6023168 | bytes 86016 | tf_op jit(solution)/shard_map/reduce_sum | solution.py:116
  121.6 2.5 %multiply_reduce_fusion.42 = (f32[2,2,2,128]{3,2,1,0:T(2,128)S(1)}, f32[2,2,2,128]{3,2,1,0:T(2,128)S(1)}, f32[2,2,2,128]{3,2,1,0:T(2,128)S(1)}, f32[2,2,2,128]{3...) fusion(f32[2,2,2,128]{3,2,1,0:T(2,128)} %get-tuple-element.307, ...), kind=kLoop, calls=%fused_computation.294 | loop fusion | flops 6023168 | bytes 86016 | tf_op jit(solution)/shard_map/reduce_sum | solution.py:116
  124.2 2.5 %multiply_reduce_fusion.48 = (f32[2,2,2,128]{3,2,1,0:T(2,128)S(1)}, f32[2,2,2,128]{3,2,1,0:T(2,128)S(1)}, f32[2,2,2,128]{3,2,1,0:T(2,128)S(1)}, f32[2,2,2,128]{3...) fusion(f32[2,2,2,128]{3,2,1,0:T(2,128)} %get-tuple-element.322, ...), kind=kLoop, calls=%fused_computation.300 | loop fusion | flops 6154240 | bytes 86016 | tf_op jit(solution)/shard_map/reduce_sum | solution.py:116
  126.7 2.5 %multiply_reduce_fusion.15 = (f32[2,2,2,128]{3,2,1,0:T(2,128)S(1)}, f32[2,2,2,128]{3,2,1,0:T(2,128)S(1)}, f32[2,2,2,128]{3,2,1,0:T(2,128)S(1)}, f32[2,2,2,128]{3...) fusion(f32[2,2,2,128]{3,2,1,0:T(2,128)} %get-tuple-element.299, ...), kind=kLoop, calls=%fused_computation.267 | loop fusion | flops 6154240 | bytes 86016 | tf_op jit(solution)/shard_map/reduce_sum | solution.py:116
  136.1 45.5 %while.13 = (s32[]{:T(128)}, f32[6,32,3,128]{3,2,1,0:T(4,128)S(1)}, f32[6,32,3,128]{3,2,1,0:T(4,128)S(1)}, f32[6,32,5,128]{3,1,0,2:T(8,128)S(1)}, f32[6,32,3,128]{3,2,1,0:T(4,128)}, /*index=5*/s32[]{:T(128)}) while((s32[]{:T(128)}, f32[6,32,3,128]{3,2,1,0:T(4,128)S(1)}, f32[6,32,3,128]{3,2,1,0:T(4,128)S(1)}, ...), condition=%wide.region_114.115_spmd, body=%wide.region_110.114_spmd.sunk | while | flops 12578818 | bytes 9470033 | solution.py:70
  139.5 4.1 %fusion.182 = (f32[32,3,128]{2,1,0:T(4,128)S(1)}, f32[32,3,128]{2,1,0:T(4,128)S(1)}) fusion(f32[32,128,128]{2,1,0:T(8,128)S(1)} %multiply_multiply_fusion.56, f32[32,3,128]{2,1,0:T(4,128)S(1)} %copy.121, f32[32,3,128]{2,1,0:T(4,128)S(1)} %dynamic-slice_bitcast_fusion.5), kind=kLoop, calls=%fused_computation.6.clone.1 | loop fusion | flops 6266880 | bytes 2293760 | tf_op jit(solution)/shard_map/while/body/eval_jaxpr/reduce_sum | solution.py:64
  147.1 4.1 %fusion.182 = (f32[32,3,128]{2,1,0:T(4,128)S(1)}, f32[32,3,128]{2,1,0:T(4,128)S(1)}) fusion(f32[32,128,128]{2,1,0:T(8,128)S(1)} %multiply_multiply_fusion.56, f32[32,3,128]{2,1,0:T(4,128)S(1)} %copy.121, f32[32,3,128]{2,1,0:T(4,128)S(1)} %dynamic-slice_bitcast_fusion.5), kind=kLoop, calls=%fused_computation.6.clone.1 | loop fusion | flops 6266880 | bytes 2293760 | tf_op jit(solution)/shard_map/while/body/eval_jaxpr/reduce_sum | solution.py:64
  154.7 4.1 %fusion.182 = (f32[32,3,128]{2,1,0:T(4,128)S(1)}, f32[32,3,128]{2,1,0:T(4,128)S(1)}) fusion(f32[32,128,128]{2,1,0:T(8,128)S(1)} %multiply_multiply_fusion.56, f32[32,3,128]{2,1,0:T(4,128)S(1)} %copy.121, f32[32,3,128]{2,1,0:T(4,128)S(1)} %dynamic-slice_bitcast_fusion.5), kind=kLoop, calls=%fused_computation.6.clone.1 | loop fusion | flops 6266880 | bytes 2293760 | tf_op jit(solution)/shard_map/while/body/eval_jaxpr/reduce_sum | solution.py:64
  162.3 4.1 %fusion.182 = (f32[32,3,128]{2,1,0:T(4,128)S(1)}, f32[32,3,128]{2,1,0:T(4,128)S(1)}) fusion(f32[32,128,128]{2,1,0:T(8,128)S(1)} %multiply_multiply_fusion.56, f32[32,3,128]{2,1,0:T(4,128)S(1)} %copy.121, f32[32,3,128]{2,1,0:T(4,128)S(1)} %dynamic-slice_bitcast_fusion.5), kind=kLoop, calls=%fused_computation.6.clone.1 | loop fusion | flops 6266880 | bytes 2293760 | tf_op jit(solution)/shard_map/while/body/eval_jaxpr/reduce_sum | solution.py:64
  169.9 4.1 %fusion.182 = (f32[32,3,128]{2,1,0:T(4,128)S(1)}, f32[32,3,128]{2,1,0:T(4,128)S(1)}) fusion(f32[32,128,128]{2,1,0:T(8,128)S(1)} %multiply_multiply_fusion.56, f32[32,3,128]{2,1,0:T(4,128)S(1)} %copy.121, f32[32,3,128]{2,1,0:T(4,128)S(1)} %dynamic-slice_bitcast_fusion.5), kind=kLoop, calls=%fused_computation.6.clone.1 | loop fusion | flops 6266880 | bytes 2293760 | tf_op jit(solution)/shard_map/while/body/eval_jaxpr/reduce_sum | solution.py:64
  177.4 4.1 %fusion.182 = (f32[32,3,128]{2,1,0:T(4,128)S(1)}, f32[32,3,128]{2,1,0:T(4,128)S(1)}) fusion(f32[32,128,128]{2,1,0:T(8,128)S(1)} %multiply_multiply_fusion.56, f32[32,3,128]{2,1,0:T(4,128)S(1)} %copy.121, f32[32,3,128]{2,1,0:T(4,128)S(1)} %dynamic-slice_bitcast_fusion.5), kind=kLoop, calls=%fused_computation.6.clone.1 | loop fusion | flops 6266880 | bytes 2293760 | tf_op jit(solution)/shard_map/while/body/eval_jaxpr/reduce_sum | solution.py:64
  182.7 4.9 %scatter_fusion.1 = f32[16,3,8,3,128]{4,2,3,1,0:T(8,128)} fusion(f32[16,3,8,3,128]{4,2,3,1,0:T(8,128)} %broadcast_in_dim.24, s32[24]{0:T(128)S(1)} %copy-done.1, f32[24,8,3,128]{3,1,2,0:T(8,128)S(1)} %copy.107), kind=kCustom, calls=%fused_computation.3 | custom fusion | bytes 884928 | tf_op jit(solution)/shard_map/scatter | solution.py:186
  187.6 5.2 %all-to-all-start.2 = ((f32[16,3,8,3,128]{4,2,3,1,0:T(8,128)}), f32[16,3,8,3,128]{4,2,3,1,0:T(8,128)S(1)}, u32[]{:S(2)}, u32[]{:S(2)}) async-start(f32[16,3,8,3,128]{4,2,3,1,0:T(8,128)} %scatter_fusion.1), calls=%async_computation.2 | async-start | bytes 1179648 | tf_op jit(solution)/shard_map/all_to_all | solution.py:188
  196.6 3.2 %multiply_reduce_fusion.53 = (f32[2,2,2,128]{3,2,1,0:T(2,128)S(1)}, f32[2,2,2,128]{3,2,1,0:T(2,128)S(1)}, f32[2,2,2,128]{3,2,1,0:T(2,128)S(1)}, f32[2,2,2,128]{3...) fusion(f32[2,2,2,128]{3,2,1,0:T(2,128)} %get-tuple-element.286,, ...), kind=kLoop, calls=%fused_computation.305 | loop fusion | flops 8903680 | bytes 102400 | tf_op jit(solution)/shard_map/reduce_sum | solution.py:116
  201.2 10.3 %all-to-all-done.2 = f32[16,3,8,3,128]{4,2,3,1,0:T(8,128)S(1)} async-done(((f32[16,3,8,3,128]{4,2,3,1,0:T(8,128)}), f32[16,3,8,3,128]{4,2,3,1,0:T(8,128)S(1)}, u32[]{:S(2)}, u32[]{:S(2)}) %all-to-all-start.2) | async-done | bytes 589856 | tf_op jit(solution)/shard_map/all_to_all | solution.py:188
  (336 shorter events, 83.0 us)
Async XLA Ops:
  0.6 33.1 %copy-start.4 = (f32[3,2,2,2,128]{4,3,2,1,0:T(2,128)S(1)}, f32[3,2,2,2,128]{4,3,2,1,0:T(2,128)}, u32[]{:S(2)}) copy-start(f32[3,2,2,2,128]{4,3,2,1,0:T(2,128)} %param.10) | copy-start | bytes 36868
  2.1 31.6 %collective-permute-start = (f32[4,1,2,2,128]{4,3,2,1,0:T(2,128)S(1)}, f32[4,1,2,2,128]{4,3,2,1,0:T(2,128)S(1)}, u32[]{:S(2)}, u32[]{:S(2)}) collective-permute-start(f32[4,1,2,2,128]{4,3,2,1,0:T(2,128)S(1)} %get-tuple-element.396), channel_id=1, source_target_pairs={{0,32},{32,64},{64,96},{96,128},{128,160},{160,192},{192,224},{224... | collective-permute-start | bytes 24584 | tf_op jit(solution)/shard_map/ppermute | solution.py:22
  6.7 27.1 %collective-permute-start.1 = (f32[4,1,2,2,128]{4,3,2,1,0:T(2,128)S(1)}, f32[4,1,2,2,128]{4,3,2,1,0:T(2,128)S(1)}, u32[]{:S(2)}, u32[]{:S(2)}) collective-permute-start(f32[4,1,2,2,128]{4,3,2,1,0:T(2,128)S(1)} %get-tuple-element.397), channel_id=1, source_target_pairs={{32,0},{64,32},{96,64},{128,96},{160,128},{192,160},{224,192},{256... | collective-permute-start | bytes 24584 | tf_op jit(solution)/shard_map/ppermute | solution.py:24
  10.7 46.2 %copy-start = (s32[24]{0:T(128)}, s32[24]{0:T(128)S(1)}, u32[]{:S(2)}) copy-start(s32[24]{0:T(128)S(1)} %get-tuple-element.248) | copy-start | bytes 292
  14.3 18.7 %all-to-all-start = ((s32[16,3,8]{2,1,0:T(4,128)}), s32[16,3,8]{2,1,0:T(4,128)S(1)}, u32[]{:S(2)}, u32[]{:S(2)}) async-start(s32[16,3,8]{2,1,0:T(4,128)} %copy.99), calls=%async_computation | async-start | bytes 65536 | tf_op jit(solution)/shard_map/all_to_all | solution.py:165
  26.3 37.6 %copy-start.2 = (f32[2,2,2,128]{3,2,1,0:T(2,128)}, f32[2,2,2,128]{3,2,1,0:T(2,128)S(1)}, u32[]{:S(2)}) copy-start(f32[2,2,2,128]{3,2,1,0:T(2,128)S(1)} %fusion.167) | copy-start | bytes 12292
  28.7 39.9 %copy-start.83 = (s32[2,2,2]{2,1,0:T(2,128)S(1)}, s32[2,2,2]{2,1,0:T(2,128)}, u32[]{:S(2)}) copy-start(s32[2,2,2]{2,1,0:T(2,128)} %param.11) | copy-start | bytes 100
  33.8 5.4 %collective-permute-start.2 = (f32[4,4,1,2,128]{4,3,2,1,0:T(2,128)S(1)}, f32[4,4,1,2,128]{4,3,2,1,0:T(2,128)S(1)}, u32[]{:S(2)}, u32[]{:S(2)}) collective-permute-start(f32[4,4,1,2,128]{4,3,2,1,0:T(2,128)S(1)} %get-tuple-element.384), channel_id=1, source_target_pairs={{0,4},{4,8},{8,12},{12,16},{16,20},{20,24},{24,28},{1,5},{5,9},{9,... | collective-permute-start | bytes 49160 | tf_op jit(solution)/shard_map/ppermute | solution.py:22
  37.0 5.5 %collective-permute-start.3 = (f32[4,4,1,2,128]{4,3,2,1,0:T(2,128)S(1)}, f32[4,4,1,2,128]{4,3,2,1,0:T(2,128)S(1)}, u32[]{:S(2)}, u32[]{:S(2)}) collective-permute-start(f32[4,4,1,2,128]{4,3,2,1,0:T(2,128)S(1)} %get-tuple-element.385), channel_id=1, source_target_pairs={{4,0},{8,4},{12,8},{16,12},{20,16},{24,20},{28,24},{5,1},{9,5},{13... | collective-permute-start | bytes 49160 | tf_op jit(solution)/shard_map/ppermute | solution.py:24
  39.1 39.1 %copy-start.9 = (f32[2,2,2,128]{3,2,1,0:T(2,128)}, f32[2,2,2,128]{3,2,1,0:T(2,128)S(1)}, u32[]{:S(2)}) copy-start(f32[2,2,2,128]{3,2,1,0:T(2,128)S(1)} %get-tuple-element.386) | copy-start | bytes 12292
  39.2 39.1 %copy-start.11 = (f32[2,2,2,128]{3,2,1,0:T(2,128)}, f32[2,2,2,128]{3,2,1,0:T(2,128)S(1)}, u32[]{:S(2)}) copy-start(f32[2,2,2,128]{3,2,1,0:T(2,128)S(1)} %get-tuple-element.387) | copy-start | bytes 12292
  39.2 39.1 %copy-start.13 = (f32[2,2,2,128]{3,2,1,0:T(2,128)}, f32[2,2,2,128]{3,2,1,0:T(2,128)S(1)}, u32[]{:S(2)}) copy-start(f32[2,2,2,128]{3,2,1,0:T(2,128)S(1)} %get-tuple-element.388) | copy-start | bytes 12292
  39.2 39.1 %copy-start.15 = (f32[2,2,2,128]{3,2,1,0:T(2,128)}, f32[2,2,2,128]{3,2,1,0:T(2,128)S(1)}, u32[]{:S(2)}) copy-start(f32[2,2,2,128]{3,2,1,0:T(2,128)S(1)} %get-tuple-element.389) | copy-start | bytes 12292
  39.2 39.1 %copy-start.73 = (f32[2,2,2,128]{3,2,1,0:T(2,128)}, f32[2,2,2,128]{3,2,1,0:T(2,128)S(1)}, u32[]{:S(2)}) copy-start(f32[2,2,2,128]{3,2,1,0:T(2,128)S(1)} %get-tuple-element.390) | copy-start | bytes 12292
  39.2 39.1 %copy-start.75 = (f32[2,2,2,128]{3,2,1,0:T(2,128)}, f32[2,2,2,128]{3,2,1,0:T(2,128)S(1)}, u32[]{:S(2)}) copy-start(f32[2,2,2,128]{3,2,1,0:T(2,128)S(1)} %get-tuple-element.391) | copy-start | bytes 12292
  39.2 39.1 %copy-start.77 = (f32[2,2,2,128]{3,2,1,0:T(2,128)}, f32[2,2,2,128]{3,2,1,0:T(2,128)S(1)}, u32[]{:S(2)}) copy-start(f32[2,2,2,128]{3,2,1,0:T(2,128)S(1)} %get-tuple-element.392) | copy-start | bytes 12292
  39.2 39.1 %copy-start.79 = (f32[2,2,2,128]{3,2,1,0:T(2,128)}, f32[2,2,2,128]{3,2,1,0:T(2,128)S(1)}, u32[]{:S(2)}) copy-start(f32[2,2,2,128]{3,2,1,0:T(2,128)S(1)} %get-tuple-element.393) | copy-start | bytes 12292
  42.7 6.6 %collective-permute-start.4 = (f32[4,4,4,1,128]{4,3,2,1,0:T(1,128)S(1)}, f32[4,4,4,1,128]{4,3,2,1,0:T(1,128)S(1)}, u32[]{:S(2)}, u32[]{:S(2)}) collective-permute-start(f32[4,4,4,1,128]{4,3,2,1,0:T(1,128)S(1)} %get-tuple-element.330), channel_id=1, source_target_pairs={{0,1},{1,2},{2,3},{4,5},{5,6},{6,7},{8,9},{9,10},{10,11},{12,13},{... | collective-permute-start | bytes 98312 | tf_op jit(solution)/shard_map/ppermute | solution.py:22
  45.8 4.7 %collective-permute-start.5 = (f32[4,4,4,1,128]{4,3,2,1,0:T(1,128)S(1)}, f32[4,4,4,1,128]{4,3,2,1,0:T(1,128)S(1)}, u32[]{:S(2)}, u32[]{:S(2)}) collective-permute-start(f32[4,4,4,1,128]{4,3,2,1,0:T(1,128)S(1)} %get-tuple-element.329), channel_id=1, source_target_pairs={{1,0},{2,1},{3,2},{5,4},{6,5},{7,6},{9,8},{10,9},{11,10},{13,12},{... | collective-permute-start | bytes 98312 | tf_op jit(solution)/shard_map/ppermute | solution.py:24
  69.3 9.3 %collective-permute-start.6 = (f32[1,2,2,128]{3,2,1,0:T(2,128)S(1)}, f32[1,2,2,128]{3,2,1,0:T(2,128)S(1)}, u32[]{:S(2)}, u32[]{:S(2)}) collective-permute-start(f32[1,2,2,128]{3,2,1,0:T(2,128)S(1)} %get-tuple-element.403), channel_id=1, source_target_pairs={{0,32},{32,64},{64,96},{96,128},{128,160},{160,192},{192,224},{224... | collective-permute-start | bytes 6152 | tf_op jit(solution)/shard_map/ppermute | solution.py:22
  74.3 4.9 %collective-permute-start.7 = (f32[1,2,2,128]{3,2,1,0:T(2,128)S(1)}, f32[1,2,2,128]{3,2,1,0:T(2,128)S(1)}, u32[]{:S(2)}, u32[]{:S(2)}) collective-permute-start(f32[1,2,2,128]{3,2,1,0:T(2,128)S(1)} %get-tuple-element.404), channel_id=1, source_target_pairs={{32,0},{64,32},{96,64},{128,96},{160,128},{192,160},{224,192},{256... | collective-permute-start | bytes 6152 | tf_op jit(solution)/shard_map/ppermute | solution.py:24
  79.3 8.6 %collective-permute-start.8 = (f32[4,1,2,128]{3,2,1,0:T(2,128)S(1)}, f32[4,1,2,128]{3,2,1,0:T(2,128)S(1)}, u32[]{:S(2)}, u32[]{:S(2)}) collective-permute-start(f32[4,1,2,128]{3,2,1,0:T(2,128)S(1)} %get-tuple-element.401), channel_id=1, source_target_pairs={{0,4},{4,8},{8,12},{12,16},{16,20},{20,24},{24,28},{1,5},{5,9},{9,... | collective-permute-start | bytes 12296 | tf_op jit(solution)/shard_map/ppermute | solution.py:22
  84.1 4.4 %collective-permute-start.9 = (f32[4,1,2,128]{3,2,1,0:T(2,128)S(1)}, f32[4,1,2,128]{3,2,1,0:T(2,128)S(1)}, u32[]{:S(2)}, u32[]{:S(2)}) collective-permute-start(f32[4,1,2,128]{3,2,1,0:T(2,128)S(1)} %get-tuple-element.402), channel_id=1, source_target_pairs={{4,0},{8,4},{12,8},{16,12},{20,16},{24,20},{28,24},{5,1},{9,5},{13... | collective-permute-start | bytes 12296 | tf_op jit(solution)/shard_map/ppermute | solution.py:24
  88.5 20.2 %collective-permute-start.10 = (f32[4,4,1,128]{3,2,1,0:T(1,128)S(1)}, f32[4,4,1,128]{3,2,1,0:T(1,128)S(1)}, u32[]{:S(2)}, u32[]{:S(2)}) collective-permute-start(f32[4,4,1,128]{3,2,1,0:T(1,128)S(1)} %get-tuple-element.394), channel_id=1, source_target_pairs={{0,1},{1,2},{2,3},{4,5},{5,6},{6,7},{8,9},{9,10},{10,11},{12,13},{... | collective-permute-start | bytes 24584 | tf_op jit(solution)/shard_map/ppermute | solution.py:22
  91.3 17.4 %collective-permute-start.11 = (f32[4,4,1,128]{3,2,1,0:T(1,128)S(1)}, f32[4,4,1,128]{3,2,1,0:T(1,128)S(1)}, u32[]{:S(2)}, u32[]{:S(2)}) collective-permute-start(f32[4,4,1,128]{3,2,1,0:T(1,128)S(1)} %get-tuple-element.395), channel_id=1, source_target_pairs={{1,0},{2,1},{3,2},{5,4},{6,5},{7,6},{9,8},{10,9},{11,10},{13,12},{... | collective-permute-start | bytes 24584 | tf_op jit(solution)/shard_map/ppermute | solution.py:24
  99.9 31.3 %copy-start.42 = (f32[2,2,2,128]{3,2,1,0:T(2,128)S(1)}, f32[2,2,2,128]{3,2,1,0:T(2,128)}, u32[]{:S(2)}) copy-start(f32[2,2,2,128]{3,2,1,0:T(2,128)} %copy-done.41) | copy-start | bytes 12292
  99.9 31.3 %copy-start.44 = (f32[2,2,2,128]{3,2,1,0:T(2,128)S(1)}, f32[2,2,2,128]{3,2,1,0:T(2,128)}, u32[]{:S(2)}) copy-start(f32[2,2,2,128]{3,2,1,0:T(2,128)} %copy-done.43) | copy-start | bytes 12292
  99.9 31.3 %copy-start.46 = (f32[2,2,2,128]{3,2,1,0:T(2,128)S(1)}, f32[2,2,2,128]{3,2,1,0:T(2,128)}, u32[]{:S(2)}) copy-start(f32[2,2,2,128]{3,2,1,0:T(2,128)} %copy-done.45) | copy-start | bytes 12292
  99.9 35.4 %copy-start.8 = (s32[24,1]{0,1:T(1,128)S(1)}, s32[24,1]{0,1:T(1,128)}, u32[]{:S(2)}) copy-start(s32[24,1]{0,1:T(1,128)} %get-tuple-element.249) | copy-start | bytes 292
  100.0 35.4 %all-to-all-start.1 = ((f32[16,3,8,5,128]{4,2,3,1,0:T(8,128)}), f32[16,3,8,5,128]{4,2,3,1,0:T(8,128)S(1)}, u32[]{:S(2)}, u32[]{:S(2)}) async-start(f32[16,3,8,5,128]{4,2,3,1,0:T(8,128)} %copy.101), calls=%async_computation.1 | async-start | bytes 1966080 | tf_op jit(solution)/shard_map/all_to_all | solution.py:169
  136.1 46.6 %copy-start.1 = (s32[24]{0:T(128)S(1)}, s32[24]{0:T(128)}, u32[]{:S(2)}) copy-start(s32[24]{0:T(128)} %copy-done) | copy-start | bytes 292
  187.6 23.9 %all-to-all-start.2 = ((f32[16,3,8,3,128]{4,2,3,1,0:T(8,128)}), f32[16,3,8,3,128]{4,2,3,1,0:T(8,128)S(1)}, u32[]{:S(2)}, u32[]{:S(2)}) async-start(f32[16,3,8,3,128]{4,2,3,1,0:T(8,128)} %scatter_fusion.1), calls=%async_computation.2 | async-start | bytes 1179648 | tf_op jit(solution)/shard_map/all_to_all | solution.py:188
  (80 other events, 1663.1 us)
where the time goes:
time: 215 us; the launch traced here: 213 us
  other arithmetic  96.9 us (45%)
  starting transfers between devices  61.2 us (28%)
  local copies, waits for them, and re-layouts  30.8 us (14%)
  waiting for transfers between devices  20.5 us (10%)
  between operations  2.52 us (1%)
    reduce_sum x13, other arithmetic, local_accel(): jnp.sum(weight * g, axis=-1)  30.7 us
    reduce_sum x6, other arithmetic, interact(): return (jnp.sum(pushed, axis=3), -jnp.sum(pushed, axis=2))  24.6 us
    ppermute x6, starting transfers between devices, with_halo(): lax.ppermute(tail, axis, [(i, (i + 1) % count) for i in range(ends)])  23.6 us
    reduce_sum x7, other arithmetic, local_density(): jnp.sum(near_tile[3][..., None, :] * spread * spread * spread, axis=-1)  15.1 us
    ppermute x6, starting transfers between devices, with_halo(): lax.ppermute(head, axis, [((i + 1) % count, i) for i in range(ends)])  12.4 us
    reduce_sum x6, other arithmetic, interact(): spread = jnp.maximum(1.0 - jnp.sum(deltas * deltas, axis=1), 0.0)  12.4 us
    all_to_all x1, starting transfers between devices, local(): lax.all_to_all(send_cell, 'gx', split_axis=0, concat_axis=0, tiled=True)  11.3 us
    all_to_all x1, waiting for transfers between devices, local(): lax.all_to_all(send_back, 'gx', split_axis=0, concat_axis=0, tiled=True)  10.3 us
  transfers between devices with their start and end apart: 15, of which 7 were waited for; matrix products, arithmetic and copies ran while one was open for 26% of the time, Pallas kernels for 0%

commit v1 on v0

v1 whole, which is shorter than its diff:
```python
import jax
import jax.numpy as jnp
from jax import lax
from jax.experimental import pallas as pl
from jax.experimental.pallas import tpu as pltpu
from jax.sharding import PartitionSpec as P

SLOTS = 128
BODY_PARTS = 128
CAPACITY = 3
FAR = 64.0
ROWS = 32
F32 = jnp.float32
BF16 = jnp.bfloat16


def split3(v):
    high = v.astype(BF16).astype(F32)
    rest = v - high
    mid = rest.astype(BF16).astype(F32)
    return high, mid, rest - mid


def near_rows(coords):
    rows = []
    norm = 0.0
    for v in coords:
        h, m, l = split3(v)
        rows += [h, m, h, l, h, m]
        norm = norm + v * v
    one = jnp.ones_like(norm)
    return rows + list(split3(-norm)) + [one, one, one]


def own_rows(coords):
    rows = []
    norm = 0.0
    for v in coords:
        h, m, l = split3(2.0 * v)
        rows += [h, h, m, h, l, m]
        norm = norm + v * v
    one = jnp.ones_like(norm)
    return rows + [one, one, one] + list(split3(1.0 - norm))


def pack_kernel(pos_ref, count_ref, shape_ref, anchor_ref, dest_ref, cell_ref, out_ref, send_ref, slot_ref, extra_ref, tally_ref):
    bodies = shape_ref.shape[1]
    groups = tally_ref.shape[0]
    lane = lax.broadcasted_iota(jnp.int32, (2, SLOTS), 1)
    row = lax.broadcasted_iota(jnp.int32, (2, SLOTS), 0)
    for a in range(2):
        for e in range(2):
            count = jnp.where(row == 0, count_ref[a, e, 0], count_ref[a, e, 1])
            live = lane < count
            base = 4 * a + 2 * e
            out_ref[0, base:base + 2, :] = jnp.where(live, pos_ref[0, a, e], FAR)
            out_ref[1, base:base + 2, :] = pos_ref[1, a, e]
            out_ref[2, base:base + 2, :] = pos_ref[2, a, e]
    send_ref[...] = jnp.zeros_like(send_ref)
    extra_ref[...] = jnp.concatenate(
        [
            anchor_ref[0],
            anchor_ref[1],
            anchor_ref[2],
            cell_ref[...].astype(F32),
            jnp.ones((bodies, 8), F32),
            jnp.zeros((bodies, SLOTS - 40), F32),
        ],
        axis=1,
    )
    for g in range(groups):
        tally_ref[g] = 0
    for b in range(bodies):
        dest = dest_ref[b, 0]
        rank = tally_ref[dest]
        tally_ref[dest] = rank + 1
        slot = dest * CAPACITY + rank
        slot_ref[b] = slot
        send_ref[slot, 0:3, :] = shape_ref[:, b, :]
        send_ref[slot, 3:4, :] = extra_ref[b:b + 1, :]


def density_kernel(left_ref, mid_ref, right_ref, rho_ref, press_ref, near_ref, coord_ref, own_ref, fb_ref, fa_ref, fr_ref, live_ref, col_ref):
    index = [lax.axis_index(n) for n in ("gx", "yz", "body")]
    size = [lax.axis_size(n) for n in ("gx", "yz", "body")]
    sub = lax.broadcasted_iota(jnp.int32, (8, SLOTS), 0)
    part = [sub // 4, sub // 2 % 2, sub % 2]
    fb_ref[...] = jnp.zeros_like(fb_ref)
    fa_ref[...] = jnp.zeros_like(fa_ref)
    fr_ref[...] = jnp.zeros_like(fr_ref)

    def block(t, carry):
        by = t // 3
        bz = t % 3
        ny = index[1] + by - 1
        nz = index[2] + bz - 1
        inside = (ny >= 0) & (ny < size[1]) & (nz >= 0) & (nz < size[2])
        off_y = (part[1] + 2 * by - 3).astype(F32)
        off_z = (part[2] + 2 * bz - 3).astype(F32)
        for kind in range(2):
            if kind == 0:
                raw = [mid_ref[t, m] for m in range(3)]
                wx = part[0] + 1
                ok = jnp.full((8, SLOTS), inside)
            else:
                raw = [jnp.where(sub >= 4, left_ref[t, m], right_ref[t, m]) for m in range(3)]
                wx = 3 - 3 * part[0]
                ok = jnp.where(sub >= 4, index[0], size[0] - 1 - index[0]) > 0
                ok = ok & inside
            coords = [
                jnp.where(ok, raw[0], FAR) + (wx - 2).astype(F32),
                raw[1] + off_y,
                raw[2] + off_z,
            ]
            for r, v in enumerate(near_rows(coords)):
                fb_ref[8 * r:8 * r + 8, :] = v
            for m in range(3):
                fr_ref[8 * m:8 * m + 8, :] = coords[m]
            if kind == 0:
                for r, v in enumerate(own_rows(coords)):
                    fa_ref[t, 8 * r:8 * r + 8, :] = v
            for c in range(8):
                a, e, f = c // 4, c // 2 % 2, c % 2
                at_x = 1 + a if kind == 0 else 3 - 3 * a
                w = (at_x * 6 + 2 * by + e) * 6 + 2 * bz + f
                near_ref[w] = fb_ref[pl.ds(c, ROWS, stride=8), :].astype(BF16)
                coord_ref[w] = fr_ref[pl.ds(c, 8, stride=8), :]
        return carry

    lax.fori_loop(0, 9, block, 0)

    def turn(r, carry):
        wy = r // 4 % 4 + 1
        wz = r % 4 + 1
        t = wy // 2 * 3 + wz // 2
        c = r // 16 * 4 + wy % 2 * 2 + wz % 2
        own_ref[r] = fa_ref[t, pl.ds(c, ROWS, stride=8), :].T.astype(BF16)
        w = ((r // 16 + 1) * 6 + wy) * 6 + wz
        live_ref[pl.ds(r, 1), :] = coord_ref[w, 0:1, :]
        return carry

    lax.fori_loop(0, 32, turn, 0, unroll=4)
    col_ref[...] = jnp.zeros_like(col_ref)
    lane = lax.broadcasted_iota(jnp.int32, (SLOTS, SLOTS), 1)

    def cell(r, carry):
        w = ((r // 16 + 1) * 6 + r // 4 % 4 + 1) * 6 + r % 4 + 1
        lhs = own_ref[r]
        acc = jnp.zeros((SLOTS, SLOTS), F32)
        steps = [(dx * 6 + dy) * 6 + dz for dx in (-1, 0, 1) for dy in (-1, 0, 1) for dz in (-1, 0, 1)]
        for g in range(0, 27, 2):
            pair = steps[g:g + 2]
            rhs = [near_ref[w + s] for s in pair]
            rhs = jnp.concatenate(rhs, axis=1) if len(rhs) == 2 else rhs[0]
            q = jnp.maximum(jnp.dot(lhs, rhs, preferred_element_type=F32), 0.0)
            q = q * q * q
            for h in range(len(pair)):
                acc = acc + q[:, h * SLOTS:(h + 1) * SLOTS]
        total = jnp.sum(acc, axis=1, keepdims=True)
        col_ref[...] = jnp.where(lane == r, total, col_ref[...])
        return carry

    lax.fori_loop(0, 32, cell, 0)
    live = live_ref[...] < 32.0
    density = jnp.where(live, col_ref[...].T[0:32, :] / (SLOTS / 2.0), 0.0)
    safe = jnp.where(live, density, 1.0)
    press_ref[...] = jnp.where(live, (density - 1.0) / (safe * safe), 0.0)
    for a in range(2):
        for e in range(2):
            r = (a * 4 + 1 + e) * 4 + 1
            rho_ref[a, e] = density[r:r + 2, :]


def body_kernel(recv_ref, pos_ref, press_ref, force_ref, load_ref, flag_ref, list_ref, fa_ref, fb_ref, side_ref, shape_ref, react_ref, sums_ref, sem):
    slots = recv_ref.shape[0]
    copy = pltpu.make_async_copy(recv_ref, flag_ref, sem)
    copy.start()
    fa_ref[...] = jnp.zeros_like(fa_ref)
    fb_ref[...] = jnp.zeros_like(fb_ref)
    react_ref[...] = jnp.zeros_like(react_ref)
    sums_ref[...] = jnp.zeros_like(sums_ref)
    copy.wait()
    shapes = [flag_ref[:, m, :] for m in range(3)]
    for r, v in enumerate(own_rows(shapes) + shapes):
        fa_ref[r * slots:(r + 1) * slots, :] = v
    press = jnp.concatenate([press_ref[(a * 4 + 1 + e) * 4 + 1:(a * 4 + 1 + e) * 4 + 3, :] for a in range(2) for e in range(2)], axis=0)
    press = press * (24.0 / SLOTS)
    list_ref[...] = press
    sub = lax.broadcasted_iota(jnp.int32, (8, SLOTS), 0)
    lane = lax.broadcasted_iota(jnp.int32, (8, SLOTS), 1)
    coords = [pos_ref[m] for m in range(3)]

    def one(t, carry):
        extra = jnp.broadcast_to(flag_ref[t, 3:4, :], (8, SLOTS))
        used = jnp.max(jnp.where(lane == 32, extra, 0.0)) > 0.0

        @pl.when(used)
        def _():
            first = jnp.sum(jnp.where(lane == 24, extra, 0.0), axis=1, keepdims=True).astype(jnp.int32)
            k = jnp.bitwise_xor(sub, first)
            gaps = []
            for m in range(3):
                anchor = jnp.sum(jnp.where(lane == 8 * m + k, extra, 0.0), axis=1, keepdims=True)
                gaps.append(coords[m] - anchor)
            for r, v in enumerate(near_rows(gaps)):
                fb_ref[8 * r:8 * r + 8, :] = v
            for m in range(3):
                side_ref[8 * m:8 * m + 8, :] = -gaps[m]
            turned = fa_ref[pl.ds(t, ROWS, stride=slots), :].T
            lhs = turned.astype(BF16)
            for m in range(3):
                shape_ref[m] = jnp.broadcast_to(turned[:, 24 + m:25 + m], (SLOTS, SLOTS))
            sums = [jnp.zeros((8, SLOTS), F32) for _ in range(6)]
            for g in range(4):
                rhs = jnp.concatenate(
                    [fb_ref[pl.ds(c, ROWS, stride=8), :].astype(BF16) for c in (2 * g, 2 * g + 1)], axis=1
                )
                q = jnp.maximum(jnp.dot(lhs, rhs, preferred_element_type=F32), 0.0)
                q = q * q
                part = [[jnp.zeros((8, SLOTS), F32) for _ in range(4)] for _ in range(2)]
                for i in range(16):
                    arm = [shape_ref[m, 8 * i:8 * i + 8, :] for m in range(3)]
                    for h in range(2):
                        v = q[8 * i:8 * i + 8, h * SLOTS:(h + 1) * SLOTS]
                        part[h][0] = part[h][0] + v
                        for m in range(3):
                            part[h][1 + m] = part[h][1 + m] + v * arm[m]
                for h in range(2):
                    c = 2 * g + h
                    pr = list_ref[c:c + 1, :]
                    gap = [side_ref[8 * m + c:8 * m + c + 1, :] for m in range(3)]
                    push = [v * pr for v in part[h]]
                    for m in range(3):
                        total = push[1 + m] + gap[m] * push[0]
                        react_ref[m, c] = react_ref[m, c] + total
                        sums[m] = sums[m] + total
                        u, v = (m + 1) % 3, (m + 2) % 3
                        sums[3 + m] = sums[3 + m] + (push[1 + u] * gap[v] - push[1 + v] * gap[u])
            for r in range(6):
                sums_ref[t, r:r + 1, :] = jnp.sum(sums[r], axis=0, keepdims=True)

        return carry

    lax.fori_loop(0, slots, one, 0)
    for m in range(3):
        force_ref[m] = jnp.sum(react_ref[m], axis=1)
    load_ref[...] = jnp.sum(sums_ref[...], axis=2)


def accel_kernel(own_ref, near_ref, coord_ref, left_ref, mid_ref, right_ref, force_ref, out_ref, press_ref, col_ref, line_ref):
    press_ref[0:16, :] = left_ref[16:32, :]
    press_ref[16:48, :] = mid_ref[...]
    press_ref[48:64, :] = right_ref[0:16, :]
    turned = mid_ref[...].T
    for a in range(2):
        for e in range(2):
            for f in range(2):
                r = (a * 4 + 1 + e) * 4 + 1 + f
                col_ref[4 * a + 2 * e + f] = jnp.broadcast_to(turned[:, r:r + 1], (SLOTS, SLOTS))
    steps = [(dx, dy, dz) for dx in (-1, 0, 1) for dy in (-1, 0, 1) for dz in (-1, 0, 1)]
    lane = lax.broadcasted_iota(jnp.int32, (32, SLOTS), 1)

    def cell(c, carry):
        a, e, f = c // 4, c // 2 % 2, c % 2
        w = ((a + 1) * 6 + e + 2) * 6 + f + 2
        v = ((a + 1) * 4 + e + 1) * 4 + f + 1
        r = (a * 4 + 1 + e) * 4 + 1 + f
        for chunk in range(4):
            lhs = own_ref[r, chunk * 32:(chunk + 1) * 32, :]
            pi = col_ref[c, chunk * 32:(chunk + 1) * 32, :]
            acc = [jnp.zeros((32, SLOTS), F32) for _ in range(4)]
            for g in range(0, 27, 2):
                pair = steps[g:g + 2]
                rhs = [near_ref[w + (d[0] * 6 + d[1]) * 6 + d[2]] for d in pair]
                rhs = jnp.concatenate(rhs, axis=1) if len(rhs) == 2 else rhs[0]
                q = jnp.maximum(jnp.dot(lhs, rhs, preferred_element_type=F32), 0.0)
                q = q * q
                for h, d in enumerate(pair):
                    pj = press_ref[pl.ds(v + (d[0] * 4 + d[1]) * 4 + d[2], 1), :]
                    at = w + (d[0] * 6 + d[1]) * 6 + d[2]
                    weight = q[:, h * SLOTS:(h + 1) * SLOTS] * (pi + pj)
                    acc[0] = acc[0] + weight
                    for m in range(3):
                        acc[1 + m] = acc[1 + m] + weight * coord_ref[at, m:m + 1, :]
            line = jnp.zeros((32, SLOTS), F32)
            for s in range(4):
                line = jnp.where(lane == s, jnp.sum(acc[s], axis=1, keepdims=True), line)
            line_ref[chunk * 32:(chunk + 1) * 32, :] = line
        rows = line_ref[...].T
        live = coord_ref[w, 0:1, :] < 32.0
        for m in range(3):
            own = coord_ref[w, m:m + 1, :] * rows[0:1, :] - rows[1 + m:2 + m, :]
            own = jnp.where(live, own * (12.0 / SLOTS), 0.0)
            out_ref[m, a, e, pl.ds(f, 1), :] = own - force_ref[m, pl.ds(c, 1), :]
        return carry

    lax.fori_loop(0, 8, cell, 0)


def gather_kernel(slot_ref, got_ref, out_ref, pick_ref):
    bodies = out_ref.shape[1]
    pick_ref[...] = jnp.zeros_like(pick_ref)
    for b in range(bodies):
        pick_ref[b:b + 1, 0:8] = got_ref[pl.ds(slot_ref[b], 1), :]
    out_ref[...] = pick_ref[...].T[0:6, 0:bodies] / BODY_PARTS


def vmem():
    return pl.BlockSpec(memory_space=pltpu.VMEM)


def smem():
    return pl.BlockSpec(memory_space=pltpu.SMEM)


def params():
    return pltpu.CompilerParams(vmem_limit_bytes=56 << 20)


def both_ways(value, axis):
    count = lax.axis_size(axis)
    ups = [(i, i + 1) for i in range(count - 1)]
    downs = [(i + 1, i) for i in range(count - 1)]
    return lax.ppermute(value, axis, ups), lax.ppermute(value, axis, downs)


def shaped(*dims, dtype=F32):
    return jax.ShapeDtypeStruct(dims, dtype)


def local(fluid_pos, fluid_count, body_shape, body_anchor, body_dest, body_cell):
    groups = lax.axis_size("gx")
    bodies = body_shape.shape[1]
    slots = groups * CAPACITY
    pos, send, slot_of = pl.pallas_call(
        pack_kernel,
        out_shape=(shaped(3, 8, SLOTS), shaped(slots, 4, SLOTS), shaped(bodies, dtype=jnp.int32)),
        in_specs=[vmem(), smem(), vmem(), vmem(), smem(), vmem()],
        out_specs=(vmem(), vmem(), smem()),
        scratch_shapes=[pltpu.VMEM((bodies, SLOTS), F32), pltpu.SMEM((groups,), jnp.int32)],
        compiler_params=params(),
        name="pack",
    )(fluid_pos, fluid_count, body_shape, body_anchor, body_dest, body_cell)
    recv = lax.all_to_all(send.reshape(groups, CAPACITY, 4, SLOTS), "gx", 0, 0, tiled=True).reshape(slots, 4, SLOTS)
    low, high = both_ways(pos, "body")
    line = jnp.stack([low, pos, high])
    low, high = both_ways(line, "yz")
    sheet = jnp.stack([low, line, high]).reshape(9, 3, 8, SLOTS)
    left, right = both_ways(sheet, "gx")
    rho, press, near, coord, own = pl.pallas_call(
        density_kernel,
        out_shape=(
            shaped(2, 2, 2, SLOTS),
            shaped(32, SLOTS),
            shaped(144, ROWS, SLOTS, dtype=BF16),
            shaped(144, 8, SLOTS),
            shaped(32, SLOTS, ROWS, dtype=BF16),
        ),
        in_specs=[vmem()] * 3,
        out_specs=(vmem(),) * 5,
        scratch_shapes=[
            pltpu.VMEM((ROWS * 8, SLOTS), F32),
            pltpu.VMEM((9, ROWS * 8, SLOTS), F32),
            pltpu.VMEM((64, SLOTS), F32),
            pltpu.VMEM((32, SLOTS), F32),
            pltpu.VMEM((SLOTS, SLOTS), F32),
        ],
        compiler_params=params(),
        name="density",
    )(left, sheet, right)
    press_left, press_right = both_ways(press, "gx")
    force, load = pl.pallas_call(
        body_kernel,
        out_shape=(shaped(3, 8, SLOTS), shaped(slots, 8)),
        in_specs=[pl.BlockSpec(memory_space=pl.ANY), vmem(), vmem()],
        out_specs=(vmem(), vmem()),
        scratch_shapes=[
            pltpu.VMEM((slots, 4, SLOTS), F32),
            pltpu.VMEM((8, SLOTS), F32),
            pltpu.VMEM((ROWS * slots, SLOTS), F32),
            pltpu.VMEM((ROWS * 8, SLOTS), F32),
            pltpu.VMEM((24, SLOTS), F32),
            pltpu.VMEM((3, SLOTS, SLOTS), F32),
            pltpu.VMEM((3, 8, 8, SLOTS), F32),
            pltpu.VMEM((slots, 8, SLOTS), F32),
            pltpu.SemaphoreType.DMA,
        ],
        compiler_params=params(),
        name="bodies",
    )(recv, pos, press)
    got = lax.all_to_all(load.reshape(groups, CAPACITY, 8), "gx", 0, 0, tiled=True).reshape(slots, 8)
    accel = pl.pallas_call(
        accel_kernel,
        out_shape=shaped(3, 2, 2, 2, SLOTS),
        in_specs=[vmem()] * 7,
        out_specs=vmem(),
        scratch_shapes=[
            pltpu.VMEM((64, SLOTS), F32),
            pltpu.VMEM((8, SLOTS, SLOTS), F32),
            pltpu.VMEM((SLOTS, SLOTS), F32),
        ],
        compiler_params=params(),
        name="accel",
    )(own, near, coord, press_left, press, press_right, force)
    body_load = pl.pallas_call(
        gather_kernel,
        out_shape=shaped(6, bodies),
        in_specs=[smem(), vmem()],
        out_specs=vmem(),
        scratch_shapes=[pltpu.VMEM((SLOTS, SLOTS), F32)],
        compiler_params=params(),
        name="collect",
    )(slot_of, got)
    return rho, accel, body_load


def solution(mesh):
    in_specs = (
        P(None, "gx", "yz", "body", None),
        P("gx", "yz", "body"),
        P(None, ("gx", "yz", "body"), None),
        P(None, ("gx", "yz", "body"), None),
        P(("gx", "yz", "body"), None),
        P(("gx", "yz", "body"), None),
    )
    out_specs = (
        P("gx", "yz", "body", None),
        P(None, "gx", "yz", "body", None),
        P(None, ("gx", "yz", "body")),
    )
    return jax.shard_map(local, mesh=mesh, in_specs=in_specs, out_specs=out_specs, check_vma=False)
```

time: 215 us -> 118 us (0.55)
  the two profiles are of different devices: /device:TPU:19 before, /device:TPU:31 now
where the time goes in v1:
time: 118 us; the launch traced here: 117 us
  starting transfers between devices  53.3 us (45%)
  Pallas kernels  49.3 us (42%)
  local copies, waits for them, and re-layouts  7.92 us (7%)
  waiting for transfers between devices  5.09 us (4%)
    ppermute x8, starting transfers between devices, both_ways(): return (lax.ppermute(value, axis, ups), lax.ppermute(value, axis, downs))  22 us
    pallas_call x1, Pallas kernels, local(): pl.pallas_call(density_kernel, out_shape=(shaped(2, 2, 2, SLOTS), shaped(...  19.4 us
    all_to_all x1, starting transfers between devices, local(): lax.all_to_all(load.reshape(groups, CAPACITY, 8), 'gx', 0, 0, tiled=True)  18.2 us
    pallas_call x1, Pallas kernels, local(): pl.pallas_call(body_kernel, out_shape=(shaped(3, 8, SLOTS), shaped(slots,...  16.6 us
    all_to_all x1, starting transfers between devices, local(): lax.all_to_all(send.reshape(groups, CAPACITY, 4, SLOTS), 'gx', 0, 0, tile...  13 us
    pallas_call x1, Pallas kernels, local(): pl.pallas_call(accel_kernel, out_shape=shaped(3, 2, 2, 2, SLOTS), in_spec...  10.1 us
    unnamed x15, local copies, waits for them, and re-layouts  5.94 us
    ppermute x8, waiting for transfers between devices, both_ways(): return (lax.ppermute(value, axis, ups), lax.ppermute(value, axis, downs))  5.08 us
  transfers between devices with their start and end apart: 10, of which 3 were waited for; matrix products, arithmetic and copies ran while one was open for 1% of the time, Pallas kernels for 39%

profile of v1, /device:TPU:31, one launch (start us, length us, event | category | flops | bytes accessed | tf_op | source)
XLA Modules:
  0.0 117.1 jit_solution(3061154857000863319)
XLA Ops:
  0.6 1.3 %copy.13.dest_ref = s32[24,1]{1,0:T(8,128)} copy(s32[24,1]{0,1:T(1,128)} %param.10) | data formatting | bytes 192 | tf_op args[4]
  2.0 1.4 %copy.14.cell_ref = s32[24,8]{1,0:T(8,128)} copy(s32[24,8]{0,1:T(8,128)} %param.11) | data formatting | bytes 1536 | tf_op args[5]
  3.3 1.4 %copy.12.anchor_ref = f32[3,24,8]{2,1,0:T(8,128)} copy(f32[3,24,8]{1,2,0:T(8,128)} %param.9) | data formatting | bytes 4608 | tf_op args[3]
  4.7 1.8 %pack.1 = (f32[3,8,128]{2,1,0:T(8,128)}, f32[48,4,128]{2,1,0:T(4,128)}, s32[24]{0:T(128)}) custom-call(f32[3,2,2,2,128]{4,3,2,1,0:T(2,128)} %pos_ref.1, s32[2,2,2]{2,1,0:T(2,128)} %count_ref.1, f32[3,24,128]{2,1,0:T(8,128)} %shape_ref.1, f32[3,24,8]{2,1,0:T(8,128)} %copy.12.anchor_ref, s32[24,1]{1,0:T(8,128)} %copy.13.dest_ref, s32[24,8]{1,0:T(8,128)} %copy.14.cell_ref), custom_call_target="tpu_custom_call" | custom-call | tf_op jit(solution)/shard_map/pack/pallas_call | solution.py:335
  6.5 2.5 %collective-permute-start.1 = (f32[3,8,128]{2,1,0:T(8,128)}, f32[3,8,128]{2,1,0:T(8,128)S(1)}, u32[]{:S(2)}, u32[]{:S(2)}) collective-permute-start(f32[3,8,128]{2,1,0:T(8,128)} %get-tuple-element.13.pos_ref), channel_id=1, source_target_pairs={{1,0},{2,1},{3,2},{5,4},{6,5},{7,6},{9,8},{10,9},{11,10},{13,12},{... | collective-permute-start | bytes 36872 | tf_op jit(solution)/shard_map/ppermute | solution.py:324
  9.0 1.3 %collective-permute-start = (f32[3,8,128]{2,1,0:T(8,128)}, f32[3,8,128]{2,1,0:T(8,128)S(1)}, u32[]{:S(2)}, u32[]{:S(2)}) collective-permute-start(f32[3,8,128]{2,1,0:T(8,128)} %get-tuple-element.13.pos_ref), channel_id=1, source_target_pairs={{0,1},{1,2},{2,3},{4,5},{5,6},{6,7},{8,9},{9,10},{10,11},{12,13},{... | collective-permute-start | bytes 36872 | tf_op jit(solution)/shard_map/ppermute | solution.py:324
  10.3 0.0 collective-permute-done.1
  10.3 3.3 %collective-permute-done = f32[3,8,128]{2,1,0:T(8,128)S(1)} collective-permute-done((f32[3,8,128]{2,1,0:T(8,128)}, f32[3,8,128]{2,1,0:T(8,128)S(1)}, u32[]{:S(2)}, u32[]{:S(2)}) %collective-permute-start) | collective-permute-done | bytes 12320 | tf_op jit(solution)/shard_map/ppermute | solution.py:324
  13.6 0.7 fusion
  14.3 2.1 %collective-permute-start.3 = (f32[3,3,8,128]{3,2,1,0:T(8,128)S(1)}, f32[3,3,8,128]{3,2,1,0:T(8,128)S(1)}, u32[]{:S(2)}, u32[]{:S(2)}) collective-permute-start(f32[3,3,8,128]{3,2,1,0:T(8,128)S(1)} %get-tuple-element.24), channel_id=1, source_target_pairs={{4,0},{8,4},{12,8},{16,12},{20,16},{24,20},{28,24},{5,1},{9,5},{13... | collective-permute-start | bytes 110600 | tf_op jit(solution)/shard_map/ppermute | solution.py:324
  16.4 4.4 %collective-permute-start.2 = (f32[3,3,8,128]{3,2,1,0:T(8,128)S(1)}, f32[3,3,8,128]{3,2,1,0:T(8,128)S(1)}, u32[]{:S(2)}, u32[]{:S(2)}) collective-permute-start(f32[3,3,8,128]{3,2,1,0:T(8,128)S(1)} %get-tuple-element.24), channel_id=1, source_target_pairs={{0,4},{4,8},{8,12},{12,16},{16,20},{20,24},{24,28},{1,5},{5,9},{9,... | collective-permute-start | bytes 110600 | tf_op jit(solution)/shard_map/ppermute | solution.py:324
  20.8 13.0 %all-to-all-start = ((f32[16,3,4,128]{3,2,1,0:T(4,128)}), f32[16,3,4,128]{3,2,1,0:T(4,128)S(1)}, u32[]{:S(2)}, u32[]{:S(2)}) async-start(f32[16,3,4,128]{3,2,1,0:T(4,128)} %bitcast.14), calls=%async_computation | async-start | bytes 196608 | tf_op jit(solution)/shard_map/all_to_all | solution.py:344
  33.8 0.0 collective-permute-done.3
  33.8 0.0 collective-permute-done.2
  33.9 2.0 %collective-permute-start.5 = (f32[9,3,8,128]{3,2,1,0:T(8,128)S(1)}, f32[9,3,8,128]{3,2,1,0:T(8,128)S(1)}, u32[]{:S(2)}, u32[]{:S(2)}) collective-permute-start(f32[9,3,8,128]{3,2,1,0:T(8,128)S(1)} %bitcast.10), channel_id=1, source_target_pairs={{32,0},{64,32},{96,64},{128,96},{160,128},{192,160},{224,192},{256... | collective-permute-start | bytes 331784 | tf_op jit(solution)/shard_map/ppermute | solution.py:324
  35.9 3.5 %collective-permute-start.4 = (f32[9,3,8,128]{3,2,1,0:T(8,128)S(1)}, f32[9,3,8,128]{3,2,1,0:T(8,128)S(1)}, u32[]{:S(2)}, u32[]{:S(2)}) collective-permute-start(f32[9,3,8,128]{3,2,1,0:T(8,128)S(1)} %bitcast.11), channel_id=1, source_target_pairs={{0,32},{32,64},{64,96},{96,128},{128,160},{160,192},{192,224},{224... | collective-permute-start | bytes 331784 | tf_op jit(solution)/shard_map/ppermute | solution.py:324
  39.5 1.0 collective-permute-done.5.right_ref
  40.5 0.7 collective-permute-done.4.left_ref
  41.2 0.6 copy-done.3
  41.8 19.4 %density.1 = (f32[2,2,2,128]{3,2,1,0:T(2,128)}, f32[32,128]{1,0:T(8,128)}, bf16[144,32,128]{2,1,0:T(8,128)(2,1)}, f32[144,8,128]{2,1,0:T(8,128)}, bf16[32,128,32]{2,1,0:T(8,128)(2,1)}) custom-call(f32[9,3,8,128]{3,2,1,0:T(8,128)} %copy-done.3, f32[9,3,8,128]{3,2,1,0:T(8,128)} %bitcast.12, f32[9,3,8,128]{3,2,1,0:T(8,128)} %copy-done.2), custom_call_target="tpu_custom_call" | custom-call | tf_op jit(solution)/shard_map/density/pallas_call | solution.py:350
  61.3 1.9 %collective-permute-start.7 = (f32[32,128]{1,0:T(8,128)}, f32[32,128]{1,0:T(8,128)S(1)}, u32[]{:S(2)}, u32[]{:S(2)}) collective-permute-start(f32[32,128]{1,0:T(8,128)} %get-tuple-element.18.press_ref.mid_ref), channel_id=1, source_target_pairs={{32,0},{64,32},{96,64},{128,96},{160,128},{192,160},{224,192},{256... | collective-permute-start | bytes 49160 | tf_op jit(solution)/shard_map/ppermute | solution.py:324
  63.2 4.3 %collective-permute-start.6 = (f32[32,128]{1,0:T(8,128)}, f32[32,128]{1,0:T(8,128)S(1)}, u32[]{:S(2)}, u32[]{:S(2)}) collective-permute-start(f32[32,128]{1,0:T(8,128)} %get-tuple-element.18.press_ref.mid_ref), channel_id=1, source_target_pairs={{0,32},{32,64},{64,96},{96,128},{128,160},{160,192},{192,224},{224... | collective-permute-start | bytes 49160 | tf_op jit(solution)/shard_map/ppermute | solution.py:324
  67.6 0.6 copy-done.1
  68.2 16.6 %bodies.1 = (f32[3,8,128]{2,1,0:T(8,128)}, f32[48,8]{1,0:T(8,128)}) custom-call(f32[48,4,128]{2,1,0:T(4,128)} %bitcast.13, f32[3,8,128]{2,1,0:T(8,128)} %get-tuple-element.13.pos_ref, f32[32,128]{1,0:T(8,128)} %get-tuple-element.18.press_ref.mid_ref), custom_call_target="tpu_custom_call" | custom-call | tf_op jit(solution)/shard_map/bodies/pallas_call | solution.py:372
  84.7 1.4 %reshape.24 = f32[16,3,8]{2,1,0:T(4,128)} reshape(f32[48,8]{1,0:T(8,128)} %get-tuple-element.22) | data formatting | bytes 3072 | tf_op jit(solution)/shard_map/reshape | solution.py:391
  86.1 18.2 %all-to-all-start.1 = ((f32[16,3,8]{2,1,0:T(4,128)}), f32[16,3,8]{2,1,0:T(4,128)S(1)}, u32[]{:S(2)}, u32[]{:S(2)}) async-start(f32[16,3,8]{2,1,0:T(4,128)} %reshape.24), calls=%async_computation.1 | async-start | bytes 65536 | tf_op jit(solution)/shard_map/all_to_all | solution.py:391
  104.3 0.0 collective-permute-done.6.left_ref
  104.3 0.6 copy-done.4
  104.9 0.0 copy-done.5
  104.9 10.1 %accel.1 = f32[3,2,2,2,128]{4,3,2,1,0:T(2,128)} custom-call(bf16[32,128,32]{2,1,0:T(8,128)(2,1)} %get-tuple-element.15.own_ref, bf16[144,32,128]{2,1,0:T(8,128)(2,1)} %get-tuple-element.16.near_ref, f32[144,8,128]{2,1,0:T(8,128)} %get-tuple-element.17.coord_ref, f32[32,128]{1,0:T(8,128)} %copy-done.5, f32[32,128]{1,0:T(8,128)} %get-tuple-element.18.press_ref.mid_ref, ...), custom_call_target="tpu_custom_call" | custom-call | tf_op jit(solution)/shard_map/accel/pallas_call | solution.py:392
  115.1 0.6 reshape.25.got_ref
  115.7 1.4 %collect.1 = f32[6,24]{1,0:T(8,128)} custom-call(s32[24]{0:T(128)} %get-tuple-element.21.slot_ref, f32[48,8]{1,0:T(8,128)} %reshape.25.got_ref), custom_call_target="tpu_custom_call" | custom-call | tf_op jit(solution)/shard_map/collect/pallas_call | solution.py:405
  (12 shorter events, 0.0 us)
Async XLA Ops:
  6.5 3.8 %collective-permute-start.1 = (f32[3,8,128]{2,1,0:T(8,128)}, f32[3,8,128]{2,1,0:T(8,128)S(1)}, u32[]{:S(2)}, u32[]{:S(2)}) collective-permute-start(f32[3,8,128]{2,1,0:T(8,128)} %get-tuple-element.13.pos_ref), channel_id=1, source_target_pairs={{1,0},{2,1},{3,2},{5,4},{6,5},{7,6},{9,8},{10,9},{11,10},{13,12},{... | collective-permute-start | bytes 36872 | tf_op jit(solution)/shard_map/ppermute | solution.py:324
  9.0 4.6 %collective-permute-start = (f32[3,8,128]{2,1,0:T(8,128)}, f32[3,8,128]{2,1,0:T(8,128)S(1)}, u32[]{:S(2)}, u32[]{:S(2)}) collective-permute-start(f32[3,8,128]{2,1,0:T(8,128)} %get-tuple-element.13.pos_ref), channel_id=1, source_target_pairs={{0,1},{1,2},{2,3},{4,5},{5,6},{6,7},{8,9},{9,10},{10,11},{12,13},{... | collective-permute-start | bytes 36872 | tf_op jit(solution)/shard_map/ppermute | solution.py:324
  14.3 19.5 %collective-permute-start.3 = (f32[3,3,8,128]{3,2,1,0:T(8,128)S(1)}, f32[3,3,8,128]{3,2,1,0:T(8,128)S(1)}, u32[]{:S(2)}, u32[]{:S(2)}) collective-permute-start(f32[3,3,8,128]{3,2,1,0:T(8,128)S(1)} %get-tuple-element.24), channel_id=1, source_target_pairs={{4,0},{8,4},{12,8},{16,12},{20,16},{24,20},{28,24},{5,1},{9,5},{13... | collective-permute-start | bytes 110600 | tf_op jit(solution)/shard_map/ppermute | solution.py:324
  16.4 17.4 %collective-permute-start.2 = (f32[3,3,8,128]{3,2,1,0:T(8,128)S(1)}, f32[3,3,8,128]{3,2,1,0:T(8,128)S(1)}, u32[]{:S(2)}, u32[]{:S(2)}) collective-permute-start(f32[3,3,8,128]{3,2,1,0:T(8,128)S(1)} %get-tuple-element.24), channel_id=1, source_target_pairs={{0,4},{4,8},{8,12},{12,16},{16,20},{20,24},{24,28},{1,5},{5,9},{9,... | collective-permute-start | bytes 110600 | tf_op jit(solution)/shard_map/ppermute | solution.py:324
  20.8 46.7 %all-to-all-start = ((f32[16,3,4,128]{3,2,1,0:T(4,128)}), f32[16,3,4,128]{3,2,1,0:T(4,128)S(1)}, u32[]{:S(2)}, u32[]{:S(2)}) async-start(f32[16,3,4,128]{3,2,1,0:T(4,128)} %bitcast.14), calls=%async_computation | async-start | bytes 196608 | tf_op jit(solution)/shard_map/all_to_all | solution.py:344
  33.9 7.3 %copy-start = (f32[3,3,3,8,128]{4,3,2,1,0:T(8,128)}, f32[3,3,3,8,128]{4,3,2,1,0:T(8,128)S(1)}, u32[]{:S(2)}) copy-start(f32[3,3,3,8,128]{4,3,2,1,0:T(8,128)S(1)} %pad_maximum_fusion) | copy-start | bytes 331780
  33.9 6.6 %collective-permute-start.5 = (f32[9,3,8,128]{3,2,1,0:T(8,128)S(1)}, f32[9,3,8,128]{3,2,1,0:T(8,128)S(1)}, u32[]{:S(2)}, u32[]{:S(2)}) collective-permute-start(f32[9,3,8,128]{3,2,1,0:T(8,128)S(1)} %bitcast.10), channel_id=1, source_target_pairs={{32,0},{64,32},{96,64},{128,96},{160,128},{192,160},{224,192},{256... | collective-permute-start | bytes 331784 | tf_op jit(solution)/shard_map/ppermute | solution.py:324
  35.9 5.3 %collective-permute-start.4 = (f32[9,3,8,128]{3,2,1,0:T(8,128)S(1)}, f32[9,3,8,128]{3,2,1,0:T(8,128)S(1)}, u32[]{:S(2)}, u32[]{:S(2)}) collective-permute-start(f32[9,3,8,128]{3,2,1,0:T(8,128)S(1)} %bitcast.11), channel_id=1, source_target_pairs={{0,32},{32,64},{64,96},{96,128},{128,160},{160,192},{192,224},{224... | collective-permute-start | bytes 331784 | tf_op jit(solution)/shard_map/ppermute | solution.py:324
  40.4 0.7 copy-start.2
  41.2 0.6 copy-start.3
  61.3 43.0 %collective-permute-start.7 = (f32[32,128]{1,0:T(8,128)}, f32[32,128]{1,0:T(8,128)S(1)}, u32[]{:S(2)}, u32[]{:S(2)}) collective-permute-start(f32[32,128]{1,0:T(8,128)} %get-tuple-element.18.press_ref.mid_ref), channel_id=1, source_target_pairs={{32,0},{64,32},{96,64},{128,96},{160,128},{192,160},{224,192},{256... | collective-permute-start | bytes 49160 | tf_op jit(solution)/shard_map/ppermute | solution.py:324
  63.2 41.1 %collective-permute-start.6 = (f32[32,128]{1,0:T(8,128)}, f32[32,128]{1,0:T(8,128)S(1)}, u32[]{:S(2)}, u32[]{:S(2)}) collective-permute-start(f32[32,128]{1,0:T(8,128)} %get-tuple-element.18.press_ref.mid_ref), channel_id=1, source_target_pairs={{0,32},{32,64},{64,96},{96,128},{128,160},{160,192},{192,224},{224... | collective-permute-start | bytes 49160 | tf_op jit(solution)/shard_map/ppermute | solution.py:324
  67.5 0.6 copy-start.1
  86.1 29.0 %all-to-all-start.1 = ((f32[16,3,8]{2,1,0:T(4,128)}), f32[16,3,8]{2,1,0:T(4,128)S(1)}, u32[]{:S(2)}, u32[]{:S(2)}) async-start(f32[16,3,8]{2,1,0:T(4,128)} %reshape.24), calls=%async_computation.1 | async-start | bytes 65536 | tf_op jit(solution)/shard_map/all_to_all | solution.py:391
  104.3 0.6 copy-start.4
  104.3 0.6 copy-start.5

commit v2 on v1

v2 whole, which is shorter than its diff:
```python
import jax
import jax.numpy as jnp
from jax import lax
from jax.experimental import pallas as pl
from jax.experimental.pallas import tpu as pltpu
from jax.sharding import PartitionSpec as P

SLOTS = 128
BODY_PARTS = 128
CAPACITY = 3
FAR = 64.0
TOGETHER = 4
ROWS = 32
F32 = jnp.float32
BF16 = jnp.bfloat16


def split3(v):
    high = v.astype(BF16).astype(F32)
    rest = v - high
    mid = rest.astype(BF16).astype(F32)
    return high, mid, rest - mid


def near_rows(coords):
    rows = []
    norm = 0.0
    for v in coords:
        h, m, l = split3(v)
        rows += [h, m, h, l, h, m]
        norm = norm + v * v
    one = jnp.ones_like(norm)
    return rows + list(split3(-norm)) + [one, one, one]


def own_rows(coords):
    rows = []
    norm = 0.0
    for v in coords:
        h, m, l = split3(2.0 * v)
        rows += [h, h, m, h, l, m]
        norm = norm + v * v
    one = jnp.ones_like(norm)
    return rows + [one, one, one] + list(split3(1.0 - norm))


def place_kernel(pos_ref, count_ref, out_ref):
    lane = lax.broadcasted_iota(jnp.int32, (2, SLOTS), 1)
    row = lax.broadcasted_iota(jnp.int32, (2, SLOTS), 0)
    for a in range(2):
        for e in range(2):
            count = jnp.where(row == 0, count_ref[a, e, 0], count_ref[a, e, 1])
            live = lane < count
            base = 4 * a + 2 * e
            out_ref[0, base:base + 2, :] = jnp.where(live, pos_ref[0, a, e], FAR)
            out_ref[1, base:base + 2, :] = pos_ref[1, a, e]
            out_ref[2, base:base + 2, :] = pos_ref[2, a, e]


def pack_kernel(shape_ref, anchor_ref, dest_ref, cell_ref, send_ref, slot_ref, extra_ref, tally_ref):
    bodies = shape_ref.shape[1]
    groups = tally_ref.shape[0]
    send_ref[...] = jnp.zeros_like(send_ref)
    extra_ref[...] = jnp.zeros_like(extra_ref)
    first = cell_ref[0:1, :]
    for m in range(3):
        rows = [anchor_ref[m, k:k + 1, :] for k in range(8)]
        for bit in (1, 2, 4):
            flip = (first & bit) > 0
            rows = [jnp.where(flip, rows[k ^ bit], rows[k]) for k in range(8)]
        for k in range(8):
            extra_ref[8 * m + k:8 * m + k + 1, 0:bodies] = rows[k]
    extra_ref[24:32, :] = jnp.ones((8, SLOTS), F32)
    extra_ref[...] = extra_ref[...].T
    for g in range(groups):
        tally_ref[g] = 0
    for b in range(bodies):
        dest = dest_ref[0, b]
        rank = tally_ref[dest]
        tally_ref[dest] = rank + 1
        slot_ref[b] = dest * 8 + rank
        slot = dest * CAPACITY + rank
        send_ref[slot, 0:3, :] = shape_ref[:, b, :]
        send_ref[slot, 3:4, :] = extra_ref[b:b + 1, :]


def density_kernel(left_ref, mid_ref, right_ref, rho_ref, press_ref, near_out, coord_out, own_out, near_ref, coord_ref, own_ref, fb_ref, fa_ref, fr_ref, live_ref, col_ref):
    index = [lax.axis_index(n) for n in ("gx", "yz", "body")]
    size = [lax.axis_size(n) for n in ("gx", "yz", "body")]
    sub = lax.broadcasted_iota(jnp.int32, (8, SLOTS), 0)
    part = [sub // 4, sub // 2 % 2, sub % 2]
    fb_ref[...] = jnp.zeros_like(fb_ref)
    fa_ref[...] = jnp.zeros_like(fa_ref)
    fr_ref[...] = jnp.zeros_like(fr_ref)

    def block(t, carry):
        by = t // 3
        bz = t % 3
        ny = index[1] + by - 1
        nz = index[2] + bz - 1
        inside = (ny >= 0) & (ny < size[1]) & (nz >= 0) & (nz < size[2])
        off_y = (part[1] + 2 * by - 3).astype(F32)
        off_z = (part[2] + 2 * bz - 3).astype(F32)
        for kind in range(2):
            if kind == 0:
                raw = [mid_ref[t, m] for m in range(3)]
                wx = part[0] + 1
                ok = jnp.full((8, SLOTS), inside)
            else:
                raw = [jnp.where(sub >= 4, left_ref[t, m], right_ref[t, m]) for m in range(3)]
                wx = 3 - 3 * part[0]
                ok = jnp.where(sub >= 4, index[0], size[0] - 1 - index[0]) > 0
                ok = ok & inside
            coords = [
                jnp.where(ok, raw[0], FAR) + (wx - 2).astype(F32),
                raw[1] + off_y,
                raw[2] + off_z,
            ]
            for r, v in enumerate(near_rows(coords)):
                fb_ref[8 * r:8 * r + 8, :] = v
            for m in range(3):
                fr_ref[8 * m:8 * m + 8, :] = coords[m]
            if kind == 0:
                for r, v in enumerate(own_rows(coords)):
                    fa_ref[t, 8 * r:8 * r + 8, :] = v
            for c in range(8):
                a, e, f = c // 4, c // 2 % 2, c % 2
                at_x = 1 + a if kind == 0 else 3 - 3 * a
                w = (at_x * 6 + 2 * by + e) * 6 + 2 * bz + f
                near_ref[w] = fb_ref[pl.ds(c, ROWS, stride=8), :].astype(BF16)
                coord_ref[w] = fr_ref[pl.ds(c, 8, stride=8), :]
        return carry

    lax.fori_loop(0, 9, block, 0)

    def turn(r, carry):
        wy = r // 4 % 4 + 1
        wz = r % 4 + 1
        t = wy // 2 * 3 + wz // 2
        c = r // 16 * 4 + wy % 2 * 2 + wz % 2
        own_ref[r] = fa_ref[t, pl.ds(c, ROWS, stride=8), :].T.astype(BF16)
        w = ((r // 16 + 1) * 6 + wy) * 6 + wz
        live_ref[pl.ds(r, 1), :] = coord_ref[w, 0:1, :]
        return carry

    lax.fori_loop(0, 32, turn, 0, unroll=16)
    for i in range(16):
        w = ((i // 4) * 6 + i % 4 + 1) * 6 + 1
        near_out[4 * i:4 * i + 4] = near_ref[w:w + 4]
        coord_out[4 * i:4 * i + 4] = coord_ref[w:w + 4]
    for a in range(2):
        for e in range(2):
            r = (a * 4 + 1 + e) * 4 + 1
            own_out[4 * a + 2 * e:4 * a + 2 * e + 2] = own_ref[r:r + 2]
    col_ref[...] = jnp.zeros_like(col_ref)
    lane = lax.broadcasted_iota(jnp.int32, (SLOTS, SLOTS), 1)

    def cell(r, carry):
        w = ((r // 16 + 1) * 6 + r // 4 % 4 + 1) * 6 + r % 4 + 1
        lhs = own_ref[r]
        acc = jnp.zeros((SLOTS, SLOTS), F32)
        steps = [(dx * 6 + dy) * 6 + dz for dx in (-1, 0, 1) for dy in (-1, 0, 1) for dz in (-1, 0, 1)]
        for g in range(0, 27, 2):
            pair = steps[g:g + 2]
            rhs = [near_ref[w + s] for s in pair]
            rhs = jnp.concatenate(rhs, axis=1) if len(rhs) == 2 else rhs[0]
            q = jnp.maximum(jnp.dot(lhs, rhs, preferred_element_type=F32), 0.0)
            q = q * q * q
            for h in range(len(pair)):
                acc = acc + q[:, h * SLOTS:(h + 1) * SLOTS]
        total = jnp.sum(acc, axis=1, keepdims=True)
        col_ref[...] = jnp.where(lane == r, total, col_ref[...])
        return carry

    lax.fori_loop(0, 32, cell, 0, unroll=8)
    live = live_ref[...] < 32.0
    density = jnp.where(live, col_ref[...].T[0:32, :] / (SLOTS / 2.0), 0.0)
    safe = jnp.where(live, density, 1.0)
    press_ref[...] = jnp.where(live, (density - 1.0) / (safe * safe), 0.0)
    for a in range(2):
        for e in range(2):
            r = (a * 4 + 1 + e) * 4 + 1
            rho_ref[a, e] = density[r:r + 2, :]


def body_kernel(recv_ref, pos_ref, press_ref, force_ref, load_ref, list_ref, fa_ref, used_ref, anchor_ref, near_ref, side_ref, arm_ref, react_ref, sums_ref, pick_ref, order_ref, sem):
    slots = recv_ref.shape[0]
    blank = jnp.zeros((8, SLOTS), F32)
    near_ref[...] = jnp.zeros_like(near_ref)
    react_ref[...] = jnp.zeros_like(react_ref)
    sums_ref[...] = jnp.zeros_like(sums_ref)
    fa_ref[27 * slots:, :] = jnp.zeros((5 * slots, SLOTS), F32)
    extras = jnp.concatenate([recv_ref[:, 3, :], jnp.zeros((SLOTS - slots, SLOTS), F32)], axis=0).T
    used_ref[...] = extras[24:32, :]
    down = pltpu.make_async_copy(used_ref, pick_ref, sem)
    down.start()
    shapes = [recv_ref[:, m, :] for m in range(3)]
    for r, v in enumerate(own_rows(shapes) + shapes):
        fa_ref[r * slots:(r + 1) * slots, :] = v
    for t in range(slots):
        for m in range(3):
            anchor_ref[t, 8 * m:8 * m + 8, :] = jnp.broadcast_to(extras[8 * m:8 * m + 8, t:t + 1], (8, SLOTS))
    press = jnp.concatenate([press_ref[(a * 4 + 1 + e) * 4 + 1:(a * 4 + 1 + e) * 4 + 3, :] for a in range(2) for e in range(2)], axis=0)
    list_ref[...] = press * (24.0 / SLOTS)
    down.wait()
    busy = jnp.int32(0)
    spare = jnp.int32(0)
    for t in range(slots):
        order_ref[busy] = t
        flag = pick_ref[0, t] > 0.0
        spare = jnp.where(flag, spare, t)
        busy = busy + flag.astype(jnp.int32)
    for n in range(TOGETHER - 1):
        order_ref[busy + n] = spare
    coords = [pos_ref[m] for m in range(3)]

    def one(t, n):
        gaps = [coords[m] - anchor_ref[t, 8 * m:8 * m + 8, :] for m in range(3)]
        for r, v in enumerate(near_rows(gaps)):
            near_ref[n, 8 * r:8 * r + 8, :] = v
        for m in range(3):
            side_ref[n, 8 * m:8 * m + 8, :] = -gaps[m]
        side_ref[n, 24:32, :] = list_ref[...] * pick_ref[0, t]
        turned = fa_ref[pl.ds(t, ROWS, stride=slots), :].T
        lhs = turned.astype(BF16)
        for m in range(3):
            arm_ref[n, m] = jnp.broadcast_to(turned[:, 24 + m:25 + m], (SLOTS, SLOTS))
        sums = [blank] * 6
        reacts = []
        for g in range(4):
            rhs = jnp.concatenate(
                [near_ref[n, pl.ds(c, ROWS, stride=8), :].astype(BF16) for c in (2 * g, 2 * g + 1)], axis=1
            )
            q = jnp.maximum(jnp.dot(lhs, rhs, preferred_element_type=F32), 0.0)
            q = q * q
            part = [[blank] * 4 for _ in range(2)]
            for i in range(16):
                arm = [arm_ref[n, m, 8 * i:8 * i + 8, :] for m in range(3)]
                for h in range(2):
                    v = q[8 * i:8 * i + 8, h * SLOTS:(h + 1) * SLOTS]
                    part[h][0] = part[h][0] + v
                    for m in range(3):
                        part[h][1 + m] = part[h][1 + m] + v * arm[m]
            for h in range(2):
                c = 2 * g + h
                pr = side_ref[n, 24 + c:25 + c, :]
                gap = [side_ref[n, 8 * m + c:8 * m + c + 1, :] for m in range(3)]
                push = [v * pr for v in part[h]]
                for m in range(3):
                    total = push[1 + m] + gap[m] * push[0]
                    reacts.append(total)
                    sums[m] = sums[m] + total
                    u, v = (m + 1) % 3, (m + 2) % 3
                    sums[3 + m] = sums[3 + m] + (push[1 + u] * gap[v] - push[1 + v] * gap[u])
        return reacts, sums

    def step(i, carry):
        picked = [order_ref[TOGETHER * i + n] for n in range(TOGETHER)]
        done = [one(t, n) for n, t in enumerate(picked)]
        for r in range(24):
            react_ref[r] = react_ref[r] + sum(d[0][r] for d in done)
        for t, d in zip(picked, done):
            for r in range(6):
                sums_ref[t, r:r + 1, :] = jnp.sum(d[1][r], axis=0, keepdims=True)
        return carry

    lax.fori_loop(0, (busy + TOGETHER - 1) // TOGETHER, step, 0)
    for r in range(24):
        force_ref[r % 3, r // 3:r // 3 + 1, :] = jnp.sum(react_ref[r], axis=0, keepdims=True)
    total = jnp.sum(sums_ref[...], axis=2)
    load_ref[...] = jnp.zeros_like(load_ref)
    for g in range(slots // CAPACITY):
        load_ref[g, 0:CAPACITY, 0:8] = total[CAPACITY * g:CAPACITY * g + CAPACITY, :]


def accel_kernel(own_ref, near_ref, coord_ref, left_ref, mid_ref, right_ref, force_ref, out_ref, press_ref, col_ref, line_ref):
    press_ref[0:16, :] = left_ref[16:32, :]
    press_ref[16:48, :] = mid_ref[...]
    press_ref[48:64, :] = right_ref[0:16, :]
    turned = mid_ref[...].T
    for a in range(2):
        for e in range(2):
            for f in range(2):
                r = (a * 4 + 1 + e) * 4 + 1 + f
                col_ref[4 * a + 2 * e + f] = jnp.broadcast_to(turned[:, r:r + 1], (SLOTS, SLOTS))
    steps = [(dx * 4 + dy) * 4 + dz for dx in (-1, 0, 1) for dy in (-1, 0, 1) for dz in (-1, 0, 1)]
    lane = lax.broadcasted_iota(jnp.int32, (32, SLOTS), 1)

    def cell(c, carry):
        a, e, f = c // 4, c // 2 % 2, c % 2
        w = ((a + 1) * 4 + e + 1) * 4 + f + 1

        def chunk(n):
            lhs = own_ref[c, n * 32:(n + 1) * 32, :]
            pi = col_ref[c, n * 32:(n + 1) * 32, :]
            acc = [jnp.zeros((32, SLOTS), F32) for _ in range(4)]
            for g in range(0, 27, 2):
                pair = steps[g:g + 2]
                rhs = [near_ref[w + s] for s in pair]
                rhs = jnp.concatenate(rhs, axis=1) if len(rhs) == 2 else rhs[0]
                q = jnp.maximum(jnp.dot(lhs, rhs, preferred_element_type=F32), 0.0)
                q = q * q
                for h, s in enumerate(pair):
                    weight = q[:, h * SLOTS:(h + 1) * SLOTS] * (pi + press_ref[pl.ds(w + s, 1), :])
                    acc[0] = acc[0] + weight
                    for m in range(3):
                        acc[1 + m] = acc[1 + m] + weight * coord_ref[w + s, m:m + 1, :]
            line = jnp.zeros((32, SLOTS), F32)
            for s in range(4):
                line = jnp.where(lane == s, jnp.sum(acc[s], axis=1, keepdims=True), line)
            line_ref[n * 32:(n + 1) * 32, :] = line

        for n in range(4):
            chunk(n)
        rows = line_ref[...].T
        live = coord_ref[w, 0:1, :] < 32.0
        for m in range(3):
            own = coord_ref[w, m:m + 1, :] * rows[0:1, :] - rows[1 + m:2 + m, :]
            own = jnp.where(live, own * (12.0 / SLOTS), 0.0)
            out_ref[m, a, e, pl.ds(f, 1), :] = own - force_ref[m, pl.ds(c, 1), :]
        return carry

    lax.fori_loop(0, 8, cell, 0, unroll=4)


def gather_kernel(slot_ref, got_ref, out_ref, pick_ref):
    bodies = out_ref.shape[1]
    pick_ref[...] = jnp.zeros_like(pick_ref)
    for b in range(bodies):
        place = slot_ref[b]
        pick_ref[b:b + 1, :] = got_ref[place // 8, pl.ds(place % 8, 1), :]
    out_ref[...] = pick_ref[...].T[0:6, 0:bodies] / BODY_PARTS


def vmem():
    return pl.BlockSpec(memory_space=pltpu.VMEM)


def smem():
    return pl.BlockSpec(memory_space=pltpu.SMEM)


def params():
    return pltpu.CompilerParams(vmem_limit_bytes=56 << 20)


def held(*values):
    return [pltpu.with_memory_space_constraint(v, pltpu.VMEM) for v in values]


def inner(*dims, dtype=F32):
    return pltpu.VMEM(dims, dtype)


def cost(giga):
    return pl.CostEstimate(flops=giga * 10**9 // 10, transcendentals=0, bytes_accessed=1 << 18)


def both_ways(value, axis):
    count = lax.axis_size(axis)
    ups = [(i, i + 1) for i in range(count - 1)]
    downs = [(i + 1, i) for i in range(count - 1)]
    return lax.ppermute(value, axis, ups), lax.ppermute(value, axis, downs)


def shaped(*dims, dtype=F32):
    return jax.ShapeDtypeStruct(dims, dtype)


def local(fluid_pos, fluid_count, body_shape, body_anchor, body_dest, body_cell):
    groups = lax.axis_size("gx")
    bodies = body_shape.shape[1]
    slots = groups * CAPACITY
    pos = pl.pallas_call(
        place_kernel,
        out_shape=inner(3, 8, SLOTS),
        in_specs=[vmem(), smem()],
        out_specs=vmem(),
        compiler_params=params(),
        name="place",
    )(fluid_pos, fluid_count)
    send, slot_of = pl.pallas_call(
        pack_kernel,
        out_shape=(inner(slots, 4, SLOTS), shaped(bodies, dtype=jnp.int32)),
        in_specs=[vmem(), vmem(), smem(), vmem()],
        out_specs=(vmem(), smem()),
        scratch_shapes=[pltpu.VMEM((SLOTS, SLOTS), F32), pltpu.SMEM((groups,), jnp.int32)],
        compiler_params=params(),
        cost_estimate=cost(4),
        name="pack",
    )(body_shape, jnp.swapaxes(body_anchor, 1, 2), body_dest.reshape(1, bodies), body_cell.T)
    low, high = both_ways(pos, "body")
    low, high, send = lax.optimization_barrier((low, high, send))
    recv = lax.all_to_all(send.reshape(groups, CAPACITY, 4, SLOTS), "gx", 0, 0, tiled=True).reshape(slots, 4, SLOTS)
    line = jnp.stack([low, pos, high])
    low, high = both_ways(line, "yz")
    sheet = jnp.stack([low, line, high]).reshape(9, 3, 8, SLOTS)
    left, right = both_ways(sheet, "gx")
    rho, press, near, coord, own = pl.pallas_call(
        density_kernel,
        out_shape=(
            shaped(2, 2, 2, SLOTS),
            inner(32, SLOTS),
            inner(64, ROWS, SLOTS, dtype=BF16),
            inner(64, 8, SLOTS),
            inner(8, SLOTS, ROWS, dtype=BF16),
        ),
        in_specs=[vmem()] * 3,
        out_specs=(vmem(),) * 5,
        scratch_shapes=[
            pltpu.VMEM((144, ROWS, SLOTS), BF16),
            pltpu.VMEM((144, 8, SLOTS), F32),
            pltpu.VMEM((32, SLOTS, ROWS), BF16),
            pltpu.VMEM((ROWS * 8, SLOTS), F32),
            pltpu.VMEM((9, ROWS * 8, SLOTS), F32),
            pltpu.VMEM((64, SLOTS), F32),
            pltpu.VMEM((32, SLOTS), F32),
            pltpu.VMEM((SLOTS, SLOTS), F32),
        ],
        compiler_params=params(),
        cost_estimate=cost(60),
        name="density",
    )(*held(left, sheet, right))
    press_left, press_right = both_ways(press, "gx")
    force, load = pl.pallas_call(
        body_kernel,
        out_shape=(inner(3, 8, SLOTS), inner(groups, 8, SLOTS)),
        in_specs=[vmem(), vmem(), vmem()],
        out_specs=(vmem(), vmem()),
        scratch_shapes=[
            pltpu.VMEM((8, SLOTS), F32),
            pltpu.VMEM((ROWS * slots, SLOTS), F32),
            pltpu.VMEM((8, SLOTS), F32),
            pltpu.VMEM((slots, 24, SLOTS), F32),
            pltpu.VMEM((TOGETHER, ROWS * 8, SLOTS), F32),
            pltpu.VMEM((TOGETHER, 32, SLOTS), F32),
            pltpu.VMEM((TOGETHER, 3, SLOTS, SLOTS), F32),
            pltpu.VMEM((24, 8, SLOTS), F32),
            pltpu.VMEM((slots, 8, SLOTS), F32),
            pltpu.SMEM((8, SLOTS), F32),
            pltpu.SMEM((slots + TOGETHER,), jnp.int32),
            pltpu.SemaphoreType.DMA,
        ],
        compiler_params=params(),
        cost_estimate=cost(60),
        name="bodies",
    )(*held(recv, pos, press))
    got = lax.all_to_all(load, "gx", 0, 0, tiled=True)
    accel = pl.pallas_call(
        accel_kernel,
        out_shape=shaped(3, 2, 2, 2, SLOTS),
        in_specs=[vmem()] * 7,
        out_specs=vmem(),
        scratch_shapes=[
            pltpu.VMEM((64, SLOTS), F32),
            pltpu.VMEM((8, SLOTS, SLOTS), F32),
            pltpu.VMEM((SLOTS, SLOTS), F32),
        ],
        compiler_params=params(),
        cost_estimate=cost(40),
        name="accel",
    )(*held(own, near, coord, press_left, press, press_right, force))
    body_load = pl.pallas_call(
        gather_kernel,
        out_shape=shaped(6, bodies),
        in_specs=[smem(), vmem()],
        out_specs=vmem(),
        scratch_shapes=[pltpu.VMEM((SLOTS, SLOTS), F32)],
        compiler_params=params(),
        cost_estimate=cost(1),
        name="collect",
    )(slot_of, *held(got))
    return rho, accel, body_load


def solution(mesh):
    in_specs = (
        P(None, "gx", "yz", "body", None),
        P("gx", "yz", "body"),
        P(None, ("gx", "yz", "body"), None),
        P(None, ("gx", "yz", "body"), None),
        P(("gx", "yz", "body"), None),
        P(("gx", "yz", "body"), None),
    )
    out_specs = (
        P("gx", "yz", "body", None),
        P(None, "gx", "yz", "body", None),
        P(None, ("gx", "yz", "body")),
    )
    return jax.shard_map(local, mesh=mesh, in_specs=in_specs, out_specs=out_specs, check_vma=False)
```

time: 118 us -> 79.2 us (0.67)
  the two profiles are of different devices: /device:TPU:31 before, /device:TPU:39 now
where the time goes in v2:
time: 79.2 us; the launch traced here: 78.6 us
  starting transfers between devices  44.4 us (56%)
  Pallas kernels  28.5 us (36%)
  waiting for transfers between devices  4.91 us (6%)
    ppermute x8, starting transfers between devices, both_ways(): return (lax.ppermute(value, axis, ups), lax.ppermute(value, axis, downs))  23.9 us
    all_to_all x1, starting transfers between devices, local(): got = lax.all_to_all(load, 'gx', 0, 0, tiled=True)  11 us
    pallas_call x1, Pallas kernels, local(): pl.pallas_call(density_kernel, out_shape=(shaped(2, 2, 2, SLOTS), inner(3...  10.8 us
    all_to_all x1, starting transfers between devices, local(): lax.all_to_all(send.reshape(groups, CAPACITY, 4, SLOTS), 'gx', 0, 0, tile...  9.54 us
    pallas_call x1, Pallas kernels, local(): pl.pallas_call(accel_kernel, out_shape=shaped(3, 2, 2, 2, SLOTS), in_spec...  7.13 us
    pallas_call x1, Pallas kernels, local(): pl.pallas_call(body_kernel, out_shape=(inner(3, 8, SLOTS), inner(groups,...  6.62 us
    ppermute x8, waiting for transfers between devices, both_ways(): return (lax.ppermute(value, axis, ups), lax.ppermute(value, axis, downs))  4.24 us
    pallas_call x1, Pallas kernels, local(): pl.pallas_call(pack_kernel, out_shape=(inner(slots, 4, SLOTS), shaped(bod...  1.59 us
  transfers between devices with their start and end apart: 10, of which 3 were waited for; matrix products, arithmetic and copies ran while one was open for 0% of the time, Pallas kernels for 33%

profile of v2, /device:TPU:39, one launch (start us, length us, event | category | flops | bytes accessed | tf_op | source)
XLA Modules:
  0.0 78.6 jit_solution(12610853754809489625)
XLA Ops:
  0.6 0.8 %place.1.pos_ref = f32[3,8,128]{2,1,0:T(8,128)S(1)} custom-call(f32[3,2,2,2,128]{4,3,2,1,0:T(2,128)} %pos_ref.1, s32[2,2,2]{2,1,0:T(2,128)} %count_ref.1), custom_call_target="tpu_custom_call" | custom-call | tf_op jit(solution)/shard_map/place/pallas_call | solution.py:374
  1.5 2.5 %collective-permute-start.1 = (f32[3,8,128]{2,1,0:T(8,128)S(1)}, f32[3,8,128]{2,1,0:T(8,128)S(1)}, u32[]{:S(2)}, u32[]{:S(2)}) collective-permute-start(f32[3,8,128]{2,1,0:T(8,128)S(1)} %place.1.pos_ref), channel_id=1, source_target_pairs={{1,0},{2,1},{3,2},{5,4},{6,5},{7,6},{9,8},{10,9},{11,10},{13,12},{... | collective-permute-start | bytes 36872 | tf_op jit(solution)/shard_map/ppermute | solution.py:363
  3.9 1.3 %collective-permute-start = (f32[3,8,128]{2,1,0:T(8,128)S(1)}, f32[3,8,128]{2,1,0:T(8,128)S(1)}, u32[]{:S(2)}, u32[]{:S(2)}) collective-permute-start(f32[3,8,128]{2,1,0:T(8,128)S(1)} %place.1.pos_ref), channel_id=1, source_target_pairs={{0,1},{1,2},{2,3},{4,5},{5,6},{6,7},{8,9},{9,10},{10,11},{12,13},{... | collective-permute-start | bytes 36872 | tf_op jit(solution)/shard_map/ppermute | solution.py:363
  5.2 1.6 %pack.1 = (f32[48,4,128]{2,1,0:T(4,128)}, s32[24]{0:T(128)}) custom-call(f32[3,24,128]{2,1,0:T(8,128)} %shape_ref.1, f32[3,8,24]{2,1,0:T(8,128)} %bitcast.22, s32[1,24]{1,0:T(1,128)} %bitcast.24, s32[8,24]{1,0:T(8,128)} %bitcast.23), custom_call_target="tpu_custom_call" | custom-call | flops 400000000 | bytes 262144 | tf_op jit(solution)/shard_map/pack/pallas_call | solution.py:382
  6.8 0.0 collective-permute-done.1
  6.8 1.5 %collective-permute-done = f32[3,8,128]{2,1,0:T(8,128)S(1)} collective-permute-done((f32[3,8,128]{2,1,0:T(8,128)S(1)}, f32[3,8,128]{2,1,0:T(8,128)S(1)}, u32[]{:S(2)}, u32[]{:S(2)}) %collective-permute-start) | collective-permute-done | bytes 12320 | tf_op jit(solution)/shard_map/ppermute | solution.py:363
  8.4 2.1 %collective-permute-start.3 = (f32[3,3,8,128]{3,2,1,0:T(8,128)S(1)}, f32[3,3,8,128]{3,2,1,0:T(8,128)S(1)}, u32[]{:S(2)}, u32[]{:S(2)}) collective-permute-start(f32[3,3,8,128]{3,2,1,0:T(8,128)S(1)} %get-tuple-element.28), channel_id=1, source_target_pairs={{4,0},{8,4},{12,8},{16,12},{20,16},{24,20},{28,24},{5,1},{9,5},{13... | collective-permute-start | bytes 110600 | tf_op jit(solution)/shard_map/ppermute | solution.py:363
  10.4 3.2 %collective-permute-start.2 = (f32[3,3,8,128]{3,2,1,0:T(8,128)S(1)}, f32[3,3,8,128]{3,2,1,0:T(8,128)S(1)}, u32[]{:S(2)}, u32[]{:S(2)}) collective-permute-start(f32[3,3,8,128]{3,2,1,0:T(8,128)S(1)} %get-tuple-element.28), channel_id=1, source_target_pairs={{0,4},{4,8},{8,12},{12,16},{16,20},{20,24},{24,28},{1,5},{5,9},{9,... | collective-permute-start | bytes 110600 | tf_op jit(solution)/shard_map/ppermute | solution.py:363
  13.7 0.0 collective-permute-done.3
  13.7 2.7 %collective-permute-done.2 = f32[3,3,8,128]{3,2,1,0:T(8,128)S(1)} collective-permute-done((f32[3,3,8,128]{3,2,1,0:T(8,128)S(1)}, f32[3,3,8,128]{3,2,1,0:T(8,128)S(1)}, u32[]{:S(2)}, u32[]{:S(2)}) %collective-permute-start.2) | collective-permute-done | bytes 36896 | tf_op jit(solution)/shard_map/ppermute | solution.py:363
  16.4 5.4 %collective-permute-start.5 = (f32[9,3,8,128]{3,2,1,0:T(8,128)S(1)}, f32[9,3,8,128]{3,2,1,0:T(8,128)S(1)}, u32[]{:S(2)}, u32[]{:S(2)}) collective-permute-start(f32[9,3,8,128]{3,2,1,0:T(8,128)S(1)} %bitcast.13), channel_id=1, source_target_pairs={{32,0},{64,32},{96,64},{128,96},{160,128},{192,160},{224,192},{256... | collective-permute-start | bytes 331784 | tf_op jit(solution)/shard_map/ppermute | solution.py:363
  21.8 3.9 %collective-permute-start.4 = (f32[9,3,8,128]{3,2,1,0:T(8,128)S(1)}, f32[9,3,8,128]{3,2,1,0:T(8,128)S(1)}, u32[]{:S(2)}, u32[]{:S(2)}) collective-permute-start(f32[9,3,8,128]{3,2,1,0:T(8,128)S(1)} %bitcast.14), channel_id=1, source_target_pairs={{0,32},{32,64},{64,96},{96,128},{128,160},{160,192},{192,224},{224... | collective-permute-start | bytes 331784 | tf_op jit(solution)/shard_map/ppermute | solution.py:363
  25.7 9.5 %all-to-all-start = ((f32[16,3,4,128]{3,2,1,0:T(4,128)}), f32[16,3,4,128]{3,2,1,0:T(4,128)S(1)}, u32[]{:S(2)}, u32[]{:S(2)}) async-start(f32[16,3,4,128]{3,2,1,0:T(4,128)} %bitcast.10), calls=%async_computation | async-start | bytes 196608 | tf_op jit(solution)/shard_map/all_to_all | solution.py:394
  35.3 0.0 collective-permute-done.5.right_ref
  35.3 0.0 collective-permute-done.4.left_ref
  35.3 10.8 %density.1 = (f32[2,2,2,128]{3,2,1,0:T(2,128)}, f32[32,128]{1,0:T(8,128)S(1)}, bf16[64,32,128]{2,1,0:T(8,128)(2,1)S(1)}, f32[64,8,128]{2,1,0:T(8,128)S(1)}, bf16[8,128,32]{2,1,0:T(8,128)(2,1)S(1)}) custom-call(f32[9,3,8,128]{3,2,1,0:T(8,128)S(1)} %collective-permute-done.4.left_ref, f32[9,3,8,128]{3,2,1,0:T(8,128)S(1)} %bitcast.15, ...), custom_call_target="tpu_custom_call" | custom-call | flops 6000000000 | bytes 262144 | tf_op jit(solution)/shard_map/density/pallas_call | solution.py:399
  46.1 2.0 %collective-permute-start.7 = (f32[32,128]{1,0:T(8,128)S(1)}, f32[32,128]{1,0:T(8,128)S(1)}, u32[]{:S(2)}, u32[]{:S(2)}) collective-permute-start(f32[32,128]{1,0:T(8,128)S(1)} %get-tuple-element.22.press_ref.mid_ref), channel_id=1, source_target_pairs={{32,0},{64,32},{96,64},{128,96},{160,128},{192,160},{224,192},{256... | collective-permute-start | bytes 49160 | tf_op jit(solution)/shard_map/ppermute | solution.py:363
  48.2 3.5 %collective-permute-start.6 = (f32[32,128]{1,0:T(8,128)S(1)}, f32[32,128]{1,0:T(8,128)S(1)}, u32[]{:S(2)}, u32[]{:S(2)}) collective-permute-start(f32[32,128]{1,0:T(8,128)S(1)} %get-tuple-element.22.press_ref.mid_ref), channel_id=1, source_target_pairs={{0,32},{32,64},{64,96},{96,128},{128,160},{160,192},{192,224},{224... | collective-permute-start | bytes 49160 | tf_op jit(solution)/shard_map/ppermute | solution.py:363
  51.7 0.0 all-to-all-done
  51.7 6.6 %bodies.1 = (f32[3,8,128]{2,1,0:T(8,128)S(1)}, f32[16,8,128]{2,1,0:T(8,128)}) custom-call(f32[48,4,128]{2,1,0:T(4,128)S(1)} %bitcast.16, f32[3,8,128]{2,1,0:T(8,128)S(1)} %place.1.pos_ref, f32[32,128]{1,0:T(8,128)S(1)} %get-tuple-element.22.press_ref.mid_ref), custom_call_target="tpu_custom_call" | custom-call | flops 6000000000 | bytes 262144 | tf_op jit(solution)/shard_map/bodies/pallas_call | solution.py:425
  58.3 11.0 %all-to-all-start.1 = ((f32[16,8,128]{2,1,0:T(8,128)}), f32[16,8,128]{2,1,0:T(8,128)S(1)}, u32[]{:S(2)}, u32[]{:S(2)}) async-start(f32[16,8,128]{2,1,0:T(8,128)} %get-tuple-element.26), calls=%async_computation.1 | async-start | bytes 131072 | tf_op jit(solution)/shard_map/all_to_all | solution.py:448
  69.3 0.0 collective-permute-done.7.right_ref
  69.3 0.0 collective-permute-done.6.left_ref
  69.3 7.1 %accel.1 = f32[3,2,2,2,128]{4,3,2,1,0:T(2,128)} custom-call(bf16[8,128,32]{2,1,0:T(8,128)(2,1)S(1)} %get-tuple-element.19.own_ref, bf16[64,32,128]{2,1,0:T(8,128)(2,1)S(1)} %get-tuple-element.20.near_ref, f32[64,8,128]{2,1,0:T(8,128)S(1)} %get-tuple-element.21.coord_ref, f32[32,128]{1,0:T(8,128)S(1)} %collective-permute-done.6.left_ref, ...), custom_call_target="tpu_custom_call" | custom-call | flops 4000000000 | bytes 262144 | tf_op jit(solution)/shard_map/accel/pallas_call | solution.py:449
  76.5 0.7 all-to-all-done.1.got_ref
  77.1 1.5 %collect.1 = f32[6,24]{1,0:T(8,128)} custom-call(s32[24]{0:T(128)} %get-tuple-element.25.slot_ref, f32[16,8,128]{2,1,0:T(8,128)S(1)} %all-to-all-done.1.got_ref), custom_call_target="tpu_custom_call" | custom-call | flops 100000000 | bytes 262144 | tf_op jit(solution)/shard_map/collect/pallas_call | solution.py:463
  (2 shorter events, 0.0 us)
Async XLA Ops:
  1.5 5.4 %collective-permute-start.1 = (f32[3,8,128]{2,1,0:T(8,128)S(1)}, f32[3,8,128]{2,1,0:T(8,128)S(1)}, u32[]{:S(2)}, u32[]{:S(2)}) collective-permute-start(f32[3,8,128]{2,1,0:T(8,128)S(1)} %place.1.pos_ref), channel_id=1, source_target_pairs={{1,0},{2,1},{3,2},{5,4},{6,5},{7,6},{9,8},{10,9},{11,10},{13,12},{... | collective-permute-start | bytes 36872 | tf_op jit(solution)/shard_map/ppermute | solution.py:363
  3.9 4.4 %collective-permute-start = (f32[3,8,128]{2,1,0:T(8,128)S(1)}, f32[3,8,128]{2,1,0:T(8,128)S(1)}, u32[]{:S(2)}, u32[]{:S(2)}) collective-permute-start(f32[3,8,128]{2,1,0:T(8,128)S(1)} %place.1.pos_ref), channel_id=1, source_target_pairs={{0,1},{1,2},{2,3},{4,5},{5,6},{6,7},{8,9},{9,10},{10,11},{12,13},{... | collective-permute-start | bytes 36872 | tf_op jit(solution)/shard_map/ppermute | solution.py:363
  8.4 5.3 %collective-permute-start.3 = (f32[3,3,8,128]{3,2,1,0:T(8,128)S(1)}, f32[3,3,8,128]{3,2,1,0:T(8,128)S(1)}, u32[]{:S(2)}, u32[]{:S(2)}) collective-permute-start(f32[3,3,8,128]{3,2,1,0:T(8,128)S(1)} %get-tuple-element.28), channel_id=1, source_target_pairs={{4,0},{8,4},{12,8},{16,12},{20,16},{24,20},{28,24},{5,1},{9,5},{13... | collective-permute-start | bytes 110600 | tf_op jit(solution)/shard_map/ppermute | solution.py:363
  10.4 5.9 %collective-permute-start.2 = (f32[3,3,8,128]{3,2,1,0:T(8,128)S(1)}, f32[3,3,8,128]{3,2,1,0:T(8,128)S(1)}, u32[]{:S(2)}, u32[]{:S(2)}) collective-permute-start(f32[3,3,8,128]{3,2,1,0:T(8,128)S(1)} %get-tuple-element.28), channel_id=1, source_target_pairs={{0,4},{4,8},{8,12},{12,16},{16,20},{20,24},{24,28},{1,5},{5,9},{9,... | collective-permute-start | bytes 110600 | tf_op jit(solution)/shard_map/ppermute | solution.py:363
  16.4 18.9 %collective-permute-start.5 = (f32[9,3,8,128]{3,2,1,0:T(8,128)S(1)}, f32[9,3,8,128]{3,2,1,0:T(8,128)S(1)}, u32[]{:S(2)}, u32[]{:S(2)}) collective-permute-start(f32[9,3,8,128]{3,2,1,0:T(8,128)S(1)} %bitcast.13), channel_id=1, source_target_pairs={{32,0},{64,32},{96,64},{128,96},{160,128},{192,160},{224,192},{256... | collective-permute-start | bytes 331784 | tf_op jit(solution)/shard_map/ppermute | solution.py:363
  21.8 13.5 %collective-permute-start.4 = (f32[9,3,8,128]{3,2,1,0:T(8,128)S(1)}, f32[9,3,8,128]{3,2,1,0:T(8,128)S(1)}, u32[]{:S(2)}, u32[]{:S(2)}) collective-permute-start(f32[9,3,8,128]{3,2,1,0:T(8,128)S(1)} %bitcast.14), channel_id=1, source_target_pairs={{0,32},{32,64},{64,96},{96,128},{128,160},{160,192},{192,224},{224... | collective-permute-start | bytes 331784 | tf_op jit(solution)/shard_map/ppermute | solution.py:363
  25.7 26.0 %all-to-all-start = ((f32[16,3,4,128]{3,2,1,0:T(4,128)}), f32[16,3,4,128]{3,2,1,0:T(4,128)S(1)}, u32[]{:S(2)}, u32[]{:S(2)}) async-start(f32[16,3,4,128]{3,2,1,0:T(4,128)} %bitcast.10), calls=%async_computation | async-start | bytes 196608 | tf_op jit(solution)/shard_map/all_to_all | solution.py:394
  46.1 23.2 %collective-permute-start.7 = (f32[32,128]{1,0:T(8,128)S(1)}, f32[32,128]{1,0:T(8,128)S(1)}, u32[]{:S(2)}, u32[]{:S(2)}) collective-permute-start(f32[32,128]{1,0:T(8,128)S(1)} %get-tuple-element.22.press_ref.mid_ref), channel_id=1, source_target_pairs={{32,0},{64,32},{96,64},{128,96},{160,128},{192,160},{224,192},{256... | collective-permute-start | bytes 49160 | tf_op jit(solution)/shard_map/ppermute | solution.py:363
  48.2 21.2 %collective-permute-start.6 = (f32[32,128]{1,0:T(8,128)S(1)}, f32[32,128]{1,0:T(8,128)S(1)}, u32[]{:S(2)}, u32[]{:S(2)}) collective-permute-start(f32[32,128]{1,0:T(8,128)S(1)} %get-tuple-element.22.press_ref.mid_ref), channel_id=1, source_target_pairs={{0,32},{32,64},{64,96},{96,128},{128,160},{160,192},{192,224},{224... | collective-permute-start | bytes 49160 | tf_op jit(solution)/shard_map/ppermute | solution.py:363
  58.3 18.8 %all-to-all-start.1 = ((f32[16,8,128]{2,1,0:T(8,128)}), f32[16,8,128]{2,1,0:T(8,128)S(1)}, u32[]{:S(2)}, u32[]{:S(2)}) async-start(f32[16,8,128]{2,1,0:T(8,128)} %get-tuple-element.26), calls=%async_computation.1 | async-start | bytes 131072 | tf_op jit(solution)/shard_map/all_to_all | solution.py:448

commit v3 on v2

--- a/solution.py
+++ b/solution.py
@@ -84,51 +84,44 @@
         send_ref[slot, 3:4, :] = extra_ref[b:b + 1, :]
 
 
-def density_kernel(left_ref, mid_ref, right_ref, rho_ref, press_ref, near_out, coord_out, own_out, near_ref, coord_ref, own_ref, fb_ref, fa_ref, fr_ref, live_ref, col_ref):
-    index = [lax.axis_index(n) for n in ("gx", "yz", "body")]
-    size = [lax.axis_size(n) for n in ("gx", "yz", "body")]
+def inside_of(by, bz):
+    ny = lax.axis_index("yz") + by - 1
+    nz = lax.axis_index("body") + bz - 1
+    return (ny >= 0) & (ny < lax.axis_size("yz")) & (nz >= 0) & (nz < lax.axis_size("body"))
+
+
+def block_of(t):
+    by = jnp.where(lax.axis_index("yz") % 2 == 1, t // 3, 2 - t // 3)
+    bz = jnp.where(lax.axis_index("body") % 2 == 1, t % 3, 2 - t % 3)
+    return by, bz
+
+
+def centre_kernel(mid_ref, near_ref, coord_ref, own_ref, live_ref, col_ref, fb_ref, fa_ref, fr_ref):
     sub = lax.broadcasted_iota(jnp.int32, (8, SLOTS), 0)
     part = [sub // 4, sub // 2 % 2, sub % 2]
-    fb_ref[...] = jnp.zeros_like(fb_ref)
-    fa_ref[...] = jnp.zeros_like(fa_ref)
-    fr_ref[...] = jnp.zeros_like(fr_ref)
+    for ref in (fb_ref, fr_ref):
+        ref[...] = jnp.zeros_like(ref)
+    fa_ref[:, 192:, :] = jnp.zeros((9, 64, SLOTS), F32)
 
     def block(t, carry):
-        by = t // 3
-        bz = t % 3
-        ny = index[1] + by - 1
-        nz = index[2] + bz - 1
-        inside = (ny >= 0) & (ny < size[1]) & (nz >= 0) & (nz < size[2])
-        off_y = (part[1] + 2 * by - 3).astype(F32)
-        off_z = (part[2] + 2 * bz - 3).astype(F32)
-        for kind in range(2):
-            if kind == 0:
-                raw = [mid_ref[t, m] for m in range(3)]
-                wx = part[0] + 1
-                ok = jnp.full((8, SLOTS), inside)
-            else:
-                raw = [jnp.where(sub >= 4, left_ref[t, m], right_ref[t, m]) for m in range(3)]
-                wx = 3 - 3 * part[0]
-                ok = jnp.where(sub >= 4, index[0], size[0] - 1 - index[0]) > 0
-                ok = ok & inside
-            coords = [
-                jnp.where(ok, raw[0], FAR) + (wx - 2).astype(F32),
-                raw[1] + off_y,
-                raw[2] + off_z,
-            ]
-            for r, v in enumerate(near_rows(coords)):
-                fb_ref[8 * r:8 * r + 8, :] = v
-            for m in range(3):
-                fr_ref[8 * m:8 * m + 8, :] = coords[m]
-            if kind == 0:
-                for r, v in enumerate(own_rows(coords)):
-                    fa_ref[t, 8 * r:8 * r + 8, :] = v
-            for c in range(8):
-                a, e, f = c // 4, c // 2 % 2, c % 2
-                at_x = 1 + a if kind == 0 else 3 - 3 * a
-                w = (at_x * 6 + 2 * by + e) * 6 + 2 * bz + f
-                near_ref[w] = fb_ref[pl.ds(c, ROWS, stride=8), :].astype(BF16)
-                coord_ref[w] = fr_ref[pl.ds(c, 8, stride=8), :]
+        by, bz = block_of(t)
+        inside = jnp.full((8, SLOTS), inside_of(by, bz))
+        coords = [
+            jnp.where(inside, mid_ref[t, 0], FAR) + (part[0] - 1).astype(F32),
+            mid_ref[t, 1] + (part[1] + 2 * by - 3).astype(F32),
+            mid_ref[t, 2] + (part[2] + 2 * bz - 3).astype(F32),
+        ]
+        for r, v in enumerate(near_rows(coords)):
+            fb_ref[8 * r:8 * r + 8, :] = v
+        for m in range(3):
+            fr_ref[8 * m:8 * m + 8, :] = coords[m]
+        for r, v in enumerate(own_rows(coords)):
+            fa_ref[by * 3 + bz, 8 * r:8 * r + 8, :] = v
+        for c in range(8):
+            a, e, f = c // 4, c // 2 % 2, c % 2
+            w = (a * 6 + 2 * by + e) * 6 + 2 * bz + f
+            near_ref[w] = fb_ref[pl.ds(c, ROWS, stride=8), :].astype(BF16)
+            coord_ref[w] = fr_ref[pl.ds(c, 8, stride=8), :]
         return carry
 
     lax.fori_loop(0, 9, block, 0)
@@ -139,40 +132,83 @@
         t = wy // 2 * 3 + wz // 2
         c = r // 16 * 4 + wy % 2 * 2 + wz % 2
         own_ref[r] = fa_ref[t, pl.ds(c, ROWS, stride=8), :].T.astype(BF16)
-        w = ((r // 16 + 1) * 6 + wy) * 6 + wz
-        live_ref[pl.ds(r, 1), :] = coord_ref[w, 0:1, :]
+        live_ref[pl.ds(r, 1), :] = coord_ref[(r // 16 * 6 + wy) * 6 + wz, 0:1, :]
         return carry
 
     lax.fori_loop(0, 32, turn, 0, unroll=16)
+    col_ref[...] = jnp.zeros_like(col_ref)
+    steps = [36 * x + 6 * dy + dz for x in (0, 1) for dy in (-1, 0, 1) for dz in (-1, 0, 1)]
+
+    def cell(r, carry):
+        add_tiles(col_ref, r, own_ref, near_ref, (r // 4 % 4 + 1) * 6 + r % 4 + 1, steps)
+        return carry
+
+    lax.fori_loop(0, 32, cell, 0, unroll=8)
+
+
+def add_tiles(col_ref, r, own_ref, near_ref, base, steps):
+    lane = lax.broadcasted_iota(jnp.int32, (SLOTS, SLOTS), 1)
+    lhs = own_ref[r]
+    acc = jnp.zeros((SLOTS, SLOTS), F32)
+    for g in range(0, len(steps), 2):
+        rhs = [near_ref[base + s] for s in steps[g:g + 2]]
+        q = jnp.concatenate(rhs, axis=1) if len(rhs) == 2 else rhs[0]
+        q = jnp.maximum(jnp.dot(lhs, q, preferred_element_type=F32), 0.0)
+        q = q * q * q
+        for h in range(len(rhs)):
+            acc = acc + q[:, h * SLOTS:(h + 1) * SLOTS]
+    total = jnp.sum(acc, axis=1, keepdims=True)
+    col_ref[...] = jnp.where(lane == r, col_ref[...] + total, col_ref[...])
+
+
+def side_kernel(left_ref, right_ref, near_mid, coord_mid, own_ref, live_ref, part_ref, rho_ref, press_ref, near_out, coord_out, own_out, near_ref, coord_ref, fb_ref, fr_ref, col_ref):
+    sub = lax.broadcasted_iota(jnp.int32, (8, SLOTS), 0)
+    part = [sub // 4, sub // 2 % 2, sub % 2]
+    for ref in (fb_ref, fr_ref):
+        ref[...] = jnp.zeros_like(ref)
+    gx = lax.axis_index("gx")
+    beside = jnp.where(sub >= 4, gx, lax.axis_size("gx") - 1 - gx) > 0
+
+    def block(t, carry):
+        by, bz = block_of(t)
+        inside = jnp.full((8, SLOTS), inside_of(by, bz)) & beside
+        raw = [jnp.where(sub >= 4, left_ref[t, m], right_ref[t, m]) for m in range(3)]
+        coords = [
+            jnp.where(inside, raw[0], FAR) + (1 - 3 * part[0]).astype(F32),
+            raw[1] + (part[1] + 2 * by - 3).astype(F32),
+            raw[2] + (part[2] + 2 * bz - 3).astype(F32),
+        ]
+        for r, v in enumerate(near_rows(coords)):
+            fb_ref[8 * r:8 * r + 8, :] = v
+        for m in range(3):
+            fr_ref[8 * m:8 * m + 8, :] = coords[m]
+        for c in range(8):
+            a, e, f = c // 4, c // 2 % 2, c % 2
+            w = ((1 - a) * 6 + 2 * by + e) * 6 + 2 * bz + f
+            near_ref[w] = fb_ref[pl.ds(c, ROWS, stride=8), :].astype(BF16)
+            coord_ref[w] = fr_ref[pl.ds(c, 8, stride=8), :]
+        return carry
+
+    lax.fori_loop(0, 9, block, 0)
+    col_ref[...] = part_ref[...]
+    steps = [6 * dy + dz for dy in (-1, 0, 1) for dz in (-1, 0, 1)]
+
+    def cell(r, carry):
+        add_tiles(col_ref, r, own_ref, near_ref, r // 16 * 36 + (r // 4 % 4 + 1) * 6 + r % 4 + 1, steps)
+        return carry
+
+    lax.fori_loop(0, 32, cell, 0, unroll=8)
     for i in range(16):
-        w = ((i // 4) * 6 + i % 4 + 1) * 6 + 1
-        near_out[4 * i:4 * i + 4] = near_ref[w:w + 4]
-        coord_out[4 * i:4 * i + 4] = coord_ref[w:w + 4]
+        x, y = i // 4, i % 4
+        w = (y + 1) * 6 + 1
+        near, coord = ((near_ref, coord_ref) if x in (0, 3) else (near_mid, coord_mid))
+        w = w + (36 if x >= 2 else 0)
+        near_out[4 * i:4 * i + 4] = near[w:w + 4]
+        coord_out[4 * i:4 * i + 4] = coord[w:w + 4]
     for a in range(2):
         for e in range(2):
             r = (a * 4 + 1 + e) * 4 + 1
             own_out[4 * a + 2 * e:4 * a + 2 * e + 2] = own_ref[r:r + 2]
-    col_ref[...] = jnp.zeros_like(col_ref)
-    lane = lax.broadcasted_iota(jnp.int32, (SLOTS, SLOTS), 1)
-
-    def cell(r, carry):
-        w = ((r // 16 + 1) * 6 + r // 4 % 4 + 1) * 6 + r % 4 + 1
-        lhs = own_ref[r]
-        acc = jnp.zeros((SLOTS, SLOTS), F32)
-        steps = [(dx * 6 + dy) * 6 + dz for dx in (-1, 0, 1) for dy in (-1, 0, 1) for dz in (-1, 0, 1)]
-        for g in range(0, 27, 2):
-            pair = steps[g:g + 2]
-            rhs = [near_ref[w + s] for s in pair]
-            rhs = jnp.concatenate(rhs, axis=1) if len(rhs) == 2 else rhs[0]
-            q = jnp.maximum(jnp.dot(lhs, rhs, preferred_element_type=F32), 0.0)
-            q = q * q * q
-            for h in range(len(pair)):
-                acc = acc + q[:, h * SLOTS:(h + 1) * SLOTS]
-        total = jnp.sum(acc, axis=1, keepdims=True)
-        col_ref[...] = jnp.where(lane == r, total, col_ref[...])
-        return carry
-
-    lax.fori_loop(0, 32, cell, 0, unroll=8)
     live = live_ref[...] < 32.0
     density = jnp.where(live, col_ref[...].T[0:32, :] / (SLOTS / 2.0), 0.0)
     safe = jnp.where(live, density, 1.0)
@@ -356,11 +392,18 @@
     return pl.CostEstimate(flops=giga * 10**9 // 10, transcendentals=0, bytes_accessed=1 << 18)
 
 
-def both_ways(value, axis):
+def shift_ways(value, axis):
     count = lax.axis_size(axis)
     ups = [(i, i + 1) for i in range(count - 1)]
     downs = [(i + 1, i) for i in range(count - 1)]
     return lax.ppermute(value, axis, ups), lax.ppermute(value, axis, downs)
+
+
+def swap_ways(value, axis):
+    count = lax.axis_size(axis)
+    inner_pairs = [(i, i ^ 1) for i in range(count)]
+    outer_pairs = [(i, (i + 1 ^ 1) - 1) for i in range(1, count - 1)]
+    return lax.ppermute(value, axis, inner_pairs), lax.ppermute(value, axis, outer_pairs)
 
 
 def shaped(*dims, dtype=F32):
@@ -389,15 +432,35 @@
         cost_estimate=cost(4),
         name="pack",
     )(body_shape, jnp.swapaxes(body_anchor, 1, 2), body_dest.reshape(1, bodies), body_cell.T)
-    low, high = both_ways(pos, "body")
+    low, high = swap_ways(pos, "body")
     low, high, send = lax.optimization_barrier((low, high, send))
     recv = lax.all_to_all(send.reshape(groups, CAPACITY, 4, SLOTS), "gx", 0, 0, tiled=True).reshape(slots, 4, SLOTS)
     line = jnp.stack([low, pos, high])
-    low, high = both_ways(line, "yz")
+    low, high = swap_ways(line, "yz")
     sheet = jnp.stack([low, line, high]).reshape(9, 3, 8, SLOTS)
-    left, right = both_ways(sheet, "gx")
+    left, right = shift_ways(sheet, "gx")
+    near_mid, coord_mid, own_all, live, partial = pl.pallas_call(
+        centre_kernel,
+        out_shape=(
+            inner(72, ROWS, SLOTS, dtype=BF16),
+            inner(72, 8, SLOTS),
+            inner(32, SLOTS, ROWS, dtype=BF16),
+            inner(32, SLOTS),
+            inner(SLOTS, SLOTS),
+        ),
+        in_specs=[vmem()],
+        out_specs=(vmem(),) * 5,
+        scratch_shapes=[
+            pltpu.VMEM((ROWS * 8, SLOTS), F32),
+            pltpu.VMEM((9, ROWS * 8, SLOTS), F32),
+            pltpu.VMEM((64, SLOTS), F32),
+        ],
+        compiler_params=params(),
+        cost_estimate=cost(60),
+        name="centre",
+    )(*held(sheet))
     rho, press, near, coord, own = pl.pallas_call(
-        density_kernel,
+        side_kernel,
         out_shape=(
             shaped(2, 2, 2, SLOTS),
             inner(32, SLOTS),
@@ -405,23 +468,20 @@
             inner(64, 8, SLOTS),
             inner(8, SLOTS, ROWS, dtype=BF16),
         ),
-        in_specs=[vmem()] * 3,
+        in_specs=[vmem()] * 7,
         out_specs=(vmem(),) * 5,
         scratch_shapes=[
-            pltpu.VMEM((144, ROWS, SLOTS), BF16),
-            pltpu.VMEM((144, 8, SLOTS), F32),
-            pltpu.VMEM((32, SLOTS, ROWS), BF16),
+            pltpu.VMEM((72, ROWS, SLOTS), BF16),
+            pltpu.VMEM((72, 8, SLOTS), F32),
             pltpu.VMEM((ROWS * 8, SLOTS), F32),
-            pltpu.VMEM((9, ROWS * 8, SLOTS), F32),
             pltpu.VMEM((64, SLOTS), F32),
-            pltpu.VMEM((32, SLOTS), F32),
             pltpu.VMEM((SLOTS, SLOTS), F32),
         ],
         compiler_params=params(),
         cost_estimate=cost(60),
-        name="density",
-    )(*held(left, sheet, right))
-    press_left, press_right = both_ways(press, "gx")
+        name="sides",
+    )(*held(left, right, near_mid, coord_mid, own_all, live, partial))
+    press_left, press_right = shift_ways(press, "gx")
     force, load = pl.pallas_call(
         body_kernel,
         out_shape=(inner(3, 8, SLOTS), inner(groups, 8, SLOTS)),

time: 79.2 us -> 80 us (1.010)
  the two profiles are of different devices: /device:TPU:39 before, /device:TPU:19 now
where the time goes in v3:
time: 80 us; the launch traced here: 79.4 us
  starting transfers between devices  42.8 us (54%)
  Pallas kernels  34.3 us (43%)
  waiting for transfers between devices  1.49 us (2%)
    all_to_all x1, starting transfers between devices, local(): lax.all_to_all(send.reshape(groups, CAPACITY, 4, SLOTS), 'gx', 0, 0, tile...  13 us
    ppermute x4, starting transfers between devices, shift_ways(): return (lax.ppermute(value, axis, ups), lax.ppermute(value, axis, downs))  11.1 us
    pallas_call x1, Pallas kernels, local(): pl.pallas_call(body_kernel, out_shape=(inner(3, 8, SLOTS), inner(groups,...  11 us
    pallas_call x1, Pallas kernels, local(): pl.pallas_call(centre_kernel, out_shape=(inner(72, ROWS, SLOTS, dtype=BF1...  7.48 us
    ppermute x2, starting transfers between devices, swap_ways(): lax.ppermute(value, axis, inner_pairs)  7.46 us
    pallas_call x1, Pallas kernels, local(): pl.pallas_call(accel_kernel, out_shape=shaped(3, 2, 2, 2, SLOTS), in_spec...  7.23 us
    all_to_all x1, starting transfers between devices, local(): got = lax.all_to_all(load, 'gx', 0, 0, tiled=True)  6.08 us
    ppermute x2, starting transfers between devices, swap_ways(): lax.ppermute(value, axis, outer_pairs)  5.19 us
  transfers between devices with their start and end apart: 10, of which 2 were waited for; matrix products, arithmetic and copies ran while one was open for 0% of the time, Pallas kernels for 40%

profile of v3, /device:TPU:19, one launch (start us, length us, event | category | flops | bytes accessed | tf_op | source)
XLA Modules:
  0.0 79.4 jit_solution(16128167844077327876)
XLA Ops:
  0.6 0.8 %place.1.pos_ref = f32[3,8,128]{2,1,0:T(8,128)S(1)} custom-call(f32[3,2,2,2,128]{4,3,2,1,0:T(2,128)} %pos_ref.1, s32[2,2,2]{2,1,0:T(2,128)} %count_ref.1), custom_call_target="tpu_custom_call" | custom-call | tf_op jit(solution)/shard_map/place/pallas_call | solution.py:417
  1.5 3.1 %collective-permute-start.1 = (f32[3,8,128]{2,1,0:T(8,128)S(1)}, f32[3,8,128]{2,1,0:T(8,128)S(1)}, u32[]{:S(2)}, u32[]{:S(2)}) collective-permute-start(f32[3,8,128]{2,1,0:T(8,128)S(1)} %place.1.pos_ref), channel_id=1, source_target_pairs={{1,2},{2,1},{5,6},{6,5},{9,10},{10,9},{13,14},{14,13},{17,18},{18,... | collective-permute-start | bytes 36872 | tf_op jit(solution)/shard_map/ppermute | solution.py:406
  4.6 1.9 %collective-permute-start = (f32[3,8,128]{2,1,0:T(8,128)S(1)}, f32[3,8,128]{2,1,0:T(8,128)S(1)}, u32[]{:S(2)}, u32[]{:S(2)}) collective-permute-start(f32[3,8,128]{2,1,0:T(8,128)S(1)} %place.1.pos_ref), channel_id=1, source_target_pairs={{0,1},{1,0},{2,3},{3,2},{4,5},{5,4},{6,7},{7,6},{8,9},{9,8},{10,11... | collective-permute-start | bytes 36872 | tf_op jit(solution)/shard_map/ppermute | solution.py:406
  6.5 1.6 %pack.1 = (f32[48,4,128]{2,1,0:T(4,128)}, s32[24]{0:T(128)}) custom-call(f32[3,24,128]{2,1,0:T(8,128)} %shape_ref.1, f32[3,8,24]{2,1,0:T(8,128)} %bitcast.22, s32[1,24]{1,0:T(1,128)} %bitcast.24, s32[8,24]{1,0:T(8,128)} %bitcast.23), custom_call_target="tpu_custom_call" | custom-call | flops 400000000 | bytes 262144 | tf_op jit(solution)/shard_map/pack/pallas_call | solution.py:425
  8.1 0.0 collective-permute-done.1
  8.1 0.9 %collective-permute-done = f32[3,8,128]{2,1,0:T(8,128)S(1)} collective-permute-done((f32[3,8,128]{2,1,0:T(8,128)S(1)}, f32[3,8,128]{2,1,0:T(8,128)S(1)}, u32[]{:S(2)}, u32[]{:S(2)}) %collective-permute-start) | collective-permute-done | bytes 12320 | tf_op jit(solution)/shard_map/ppermute | solution.py:406
  9.0 2.1 %collective-permute-start.3 = (f32[3,3,8,128]{3,2,1,0:T(8,128)S(1)}, f32[3,3,8,128]{3,2,1,0:T(8,128)S(1)}, u32[]{:S(2)}, u32[]{:S(2)}) collective-permute-start(f32[3,3,8,128]{3,2,1,0:T(8,128)S(1)} %get-tuple-element.38), channel_id=1, source_target_pairs={{4,8},{8,4},{12,16},{16,12},{20,24},{24,20},{5,9},{9,5},{13,17},{1... | collective-permute-start | bytes 110600 | tf_op jit(solution)/shard_map/ppermute | solution.py:406
  11.1 5.5 %collective-permute-start.2 = (f32[3,3,8,128]{3,2,1,0:T(8,128)S(1)}, f32[3,3,8,128]{3,2,1,0:T(8,128)S(1)}, u32[]{:S(2)}, u32[]{:S(2)}) collective-permute-start(f32[3,3,8,128]{3,2,1,0:T(8,128)S(1)} %get-tuple-element.38), channel_id=1, source_target_pairs={{0,4},{4,0},{8,12},{12,8},{16,20},{20,16},{24,28},{28,24},{1,5},{5... | collective-permute-start | bytes 110600 | tf_op jit(solution)/shard_map/ppermute | solution.py:406
  16.7 13.0 %all-to-all-start = ((f32[16,3,4,128]{3,2,1,0:T(4,128)}), f32[16,3,4,128]{3,2,1,0:T(4,128)S(1)}, u32[]{:S(2)}, u32[]{:S(2)}) async-start(f32[16,3,4,128]{3,2,1,0:T(4,128)} %bitcast.10), calls=%async_computation | async-start | bytes 196608 | tf_op jit(solution)/shard_map/all_to_all | solution.py:437
  29.7 0.0 collective-permute-done.3
  29.7 0.0 collective-permute-done.2
  29.7 2.0 %collective-permute-start.5 = (f32[9,3,8,128]{3,2,1,0:T(8,128)S(1)}, f32[9,3,8,128]{3,2,1,0:T(8,128)S(1)}, u32[]{:S(2)}, u32[]{:S(2)}) collective-permute-start(f32[9,3,8,128]{3,2,1,0:T(8,128)S(1)} %bitcast.13), channel_id=1, source_target_pairs={{32,0},{64,32},{96,64},{128,96},{160,128},{192,160},{224,192},{256... | collective-permute-start | bytes 331784 | tf_op jit(solution)/shard_map/ppermute | solution.py:399
  31.7 3.5 %collective-permute-start.4 = (f32[9,3,8,128]{3,2,1,0:T(8,128)S(1)}, f32[9,3,8,128]{3,2,1,0:T(8,128)S(1)}, u32[]{:S(2)}, u32[]{:S(2)}) collective-permute-start(f32[9,3,8,128]{3,2,1,0:T(8,128)S(1)} %bitcast.14), channel_id=1, source_target_pairs={{0,32},{32,64},{64,96},{96,128},{128,160},{160,192},{192,224},{224... | collective-permute-start | bytes 331784 | tf_op jit(solution)/shard_map/ppermute | solution.py:399
  35.3 7.5 %centre.1 = (bf16[72,32,128]{2,1,0:T(8,128)(2,1)S(1)}, f32[72,8,128]{2,1,0:T(8,128)S(1)}, bf16[32,128,32]{2,1,0:T(8,128)(2,1)S(1)}, f32[32,128]{1,0:T(8,128)S(1)}, f32[128,128]{1,0:T(8,128)S(1)}) custom-call(f32[9,3,8,128]{3,2,1,0:T(8,128)S(1)} %bitcast.15), custom_call_target="tpu_custom_call" | custom-call | flops 6000000000 | bytes 262144 | tf_op jit(solution)/shard_map/centre/pallas_call | solution.py:442
  42.8 0.0 collective-permute-done.5.right_ref
  42.8 0.0 collective-permute-done.4.left_ref
  42.8 4.7 %sides.1 = (f32[2,2,2,128]{3,2,1,0:T(2,128)}, f32[32,128]{1,0:T(8,128)S(1)}, bf16[64,32,128]{2,1,0:T(8,128)(2,1)S(1)}, f32[64,8,128]{2,1,0:T(8,128)S(1)}, bf16[8,128,32]{2,1,0:T(8,128)(2,1)S(1)}) custom-call(f32[9,3,8,128]{3,2,1,0:T(8,128)S(1)} %collective-permute-done.4.left_ref, f32[9,3,8,128]{3,2,1,0:T(8,128)S(1)} %collective-permute-done.5.right_ref, ...), custom_call_target="tpu_custom_call" | custom-call | flops 6000000000 | bytes 262144 | tf_op jit(solution)/shard_map/sides/pallas_call | solution.py:462
  47.5 1.9 %collective-permute-start.7 = (f32[32,128]{1,0:T(8,128)S(1)}, f32[32,128]{1,0:T(8,128)S(1)}, u32[]{:S(2)}, u32[]{:S(2)}) collective-permute-start(f32[32,128]{1,0:T(8,128)S(1)} %get-tuple-element.32.press_ref.mid_ref), channel_id=1, source_target_pairs={{32,0},{64,32},{96,64},{128,96},{160,128},{192,160},{224,192},{256... | collective-permute-start | bytes 49160 | tf_op jit(solution)/shard_map/ppermute | solution.py:399
  49.4 3.6 %collective-permute-start.6 = (f32[32,128]{1,0:T(8,128)S(1)}, f32[32,128]{1,0:T(8,128)S(1)}, u32[]{:S(2)}, u32[]{:S(2)}) collective-permute-start(f32[32,128]{1,0:T(8,128)S(1)} %get-tuple-element.32.press_ref.mid_ref), channel_id=1, source_target_pairs={{0,32},{32,64},{64,96},{96,128},{128,160},{160,192},{192,224},{224... | collective-permute-start | bytes 49160 | tf_op jit(solution)/shard_map/ppermute | solution.py:399
  53.1 0.0 all-to-all-done
  53.1 11.0 %bodies.1 = (f32[3,8,128]{2,1,0:T(8,128)S(1)}, f32[16,8,128]{2,1,0:T(8,128)}) custom-call(f32[48,4,128]{2,1,0:T(4,128)S(1)} %bitcast.16, f32[3,8,128]{2,1,0:T(8,128)S(1)} %place.1.pos_ref, f32[32,128]{1,0:T(8,128)S(1)} %get-tuple-element.32.press_ref.mid_ref), custom_call_target="tpu_custom_call" | custom-call | flops 6000000000 | bytes 262144 | tf_op jit(solution)/shard_map/bodies/pallas_call | solution.py:485
  64.1 6.1 %all-to-all-start.1 = ((f32[16,8,128]{2,1,0:T(8,128)}), f32[16,8,128]{2,1,0:T(8,128)S(1)}, u32[]{:S(2)}, u32[]{:S(2)}) async-start(f32[16,8,128]{2,1,0:T(8,128)} %get-tuple-element.36), calls=%async_computation.1 | async-start | bytes 131072 | tf_op jit(solution)/shard_map/all_to_all | solution.py:508
  70.1 0.0 collective-permute-done.7.right_ref
  70.2 0.0 collective-permute-done.6.left_ref
  70.2 7.2 %accel.1 = f32[3,2,2,2,128]{4,3,2,1,0:T(2,128)} custom-call(bf16[8,128,32]{2,1,0:T(8,128)(2,1)S(1)} %get-tuple-element.29.own_ref, bf16[64,32,128]{2,1,0:T(8,128)(2,1)S(1)} %get-tuple-element.30.near_ref, f32[64,8,128]{2,1,0:T(8,128)S(1)} %get-tuple-element.31.coord_ref, f32[32,128]{1,0:T(8,128)S(1)} %collective-permute-done.6.left_ref, ...), custom_call_target="tpu_custom_call" | custom-call | flops 4000000000 | bytes 262144 | tf_op jit(solution)/shard_map/accel/pallas_call | solution.py:509
  77.4 0.6 all-to-all-done.1.got_ref
  78.0 1.5 %collect.1 = f32[6,24]{1,0:T(8,128)} custom-call(s32[24]{0:T(128)} %get-tuple-element.35.slot_ref, f32[16,8,128]{2,1,0:T(8,128)S(1)} %all-to-all-done.1.got_ref), custom_call_target="tpu_custom_call" | custom-call | flops 100000000 | bytes 262144 | tf_op jit(solution)/shard_map/collect/pallas_call | solution.py:523
  (2 shorter events, 0.0 us)
Async XLA Ops:
  1.5 6.7 %collective-permute-start.1 = (f32[3,8,128]{2,1,0:T(8,128)S(1)}, f32[3,8,128]{2,1,0:T(8,128)S(1)}, u32[]{:S(2)}, u32[]{:S(2)}) collective-permute-start(f32[3,8,128]{2,1,0:T(8,128)S(1)} %place.1.pos_ref), channel_id=1, source_target_pairs={{1,2},{2,1},{5,6},{6,5},{9,10},{10,9},{13,14},{14,13},{17,18},{18,... | collective-permute-start | bytes 36872 | tf_op jit(solution)/shard_map/ppermute | solution.py:406
  4.6 4.4 %collective-permute-start = (f32[3,8,128]{2,1,0:T(8,128)S(1)}, f32[3,8,128]{2,1,0:T(8,128)S(1)}, u32[]{:S(2)}, u32[]{:S(2)}) collective-permute-start(f32[3,8,128]{2,1,0:T(8,128)S(1)} %place.1.pos_ref), channel_id=1, source_target_pairs={{0,1},{1,0},{2,3},{3,2},{4,5},{5,4},{6,7},{7,6},{8,9},{9,8},{10,11... | collective-permute-start | bytes 36872 | tf_op jit(solution)/shard_map/ppermute | solution.py:406
  9.0 20.6 %collective-permute-start.3 = (f32[3,3,8,128]{3,2,1,0:T(8,128)S(1)}, f32[3,3,8,128]{3,2,1,0:T(8,128)S(1)}, u32[]{:S(2)}, u32[]{:S(2)}) collective-permute-start(f32[3,3,8,128]{3,2,1,0:T(8,128)S(1)} %get-tuple-element.38), channel_id=1, source_target_pairs={{4,8},{8,4},{12,16},{16,12},{20,24},{24,20},{5,9},{9,5},{13,17},{1... | collective-permute-start | bytes 110600 | tf_op jit(solution)/shard_map/ppermute | solution.py:406
  11.1 18.6 %collective-permute-start.2 = (f32[3,3,8,128]{3,2,1,0:T(8,128)S(1)}, f32[3,3,8,128]{3,2,1,0:T(8,128)S(1)}, u32[]{:S(2)}, u32[]{:S(2)}) collective-permute-start(f32[3,3,8,128]{3,2,1,0:T(8,128)S(1)} %get-tuple-element.38), channel_id=1, source_target_pairs={{0,4},{4,0},{8,12},{12,8},{16,20},{20,16},{24,28},{28,24},{1,5},{5... | collective-permute-start | bytes 110600 | tf_op jit(solution)/shard_map/ppermute | solution.py:406
  16.7 36.4 %all-to-all-start = ((f32[16,3,4,128]{3,2,1,0:T(4,128)}), f32[16,3,4,128]{3,2,1,0:T(4,128)S(1)}, u32[]{:S(2)}, u32[]{:S(2)}) async-start(f32[16,3,4,128]{3,2,1,0:T(4,128)} %bitcast.10), calls=%async_computation | async-start | bytes 196608 | tf_op jit(solution)/shard_map/all_to_all | solution.py:437
  29.7 13.1 %collective-permute-start.5 = (f32[9,3,8,128]{3,2,1,0:T(8,128)S(1)}, f32[9,3,8,128]{3,2,1,0:T(8,128)S(1)}, u32[]{:S(2)}, u32[]{:S(2)}) collective-permute-start(f32[9,3,8,128]{3,2,1,0:T(8,128)S(1)} %bitcast.13), channel_id=1, source_target_pairs={{32,0},{64,32},{96,64},{128,96},{160,128},{192,160},{224,192},{256... | collective-permute-start | bytes 331784 | tf_op jit(solution)/shard_map/ppermute | solution.py:399
  31.7 11.1 %collective-permute-start.4 = (f32[9,3,8,128]{3,2,1,0:T(8,128)S(1)}, f32[9,3,8,128]{3,2,1,0:T(8,128)S(1)}, u32[]{:S(2)}, u32[]{:S(2)}) collective-permute-start(f32[9,3,8,128]{3,2,1,0:T(8,128)S(1)} %bitcast.14), channel_id=1, source_target_pairs={{0,32},{32,64},{64,96},{96,128},{128,160},{160,192},{192,224},{224... | collective-permute-start | bytes 331784 | tf_op jit(solution)/shard_map/ppermute | solution.py:399
  47.5 22.6 %collective-permute-start.7 = (f32[32,128]{1,0:T(8,128)S(1)}, f32[32,128]{1,0:T(8,128)S(1)}, u32[]{:S(2)}, u32[]{:S(2)}) collective-permute-start(f32[32,128]{1,0:T(8,128)S(1)} %get-tuple-element.32.press_ref.mid_ref), channel_id=1, source_target_pairs={{32,0},{64,32},{96,64},{128,96},{160,128},{192,160},{224,192},{256... | collective-permute-start | bytes 49160 | tf_op jit(solution)/shard_map/ppermute | solution.py:399
  49.4 20.7 %collective-permute-start.6 = (f32[32,128]{1,0:T(8,128)S(1)}, f32[32,128]{1,0:T(8,128)S(1)}, u32[]{:S(2)}, u32[]{:S(2)}) collective-permute-start(f32[32,128]{1,0:T(8,128)S(1)} %get-tuple-element.32.press_ref.mid_ref), channel_id=1, source_target_pairs={{0,32},{32,64},{64,96},{96,128},{128,160},{160,192},{192,224},{224... | collective-permute-start | bytes 49160 | tf_op jit(solution)/shard_map/ppermute | solution.py:399
  64.1 13.9 %all-to-all-start.1 = ((f32[16,8,128]{2,1,0:T(8,128)}), f32[16,8,128]{2,1,0:T(8,128)S(1)}, u32[]{:S(2)}, u32[]{:S(2)}) async-start(f32[16,8,128]{2,1,0:T(8,128)} %get-tuple-element.36), calls=%async_computation.1 | async-start | bytes 131072 | tf_op jit(solution)/shard_map/all_to_all | solution.py:508

commit v4 on v2

--- a/solution.py
+++ b/solution.py
@@ -9,7 +9,7 @@
 BODY_PARTS = 128
 CAPACITY = 3
 FAR = 64.0
-TOGETHER = 4
+TOGETHER = 24
 ROWS = 32
 F32 = jnp.float32
 BF16 = jnp.bfloat16
@@ -172,7 +172,7 @@
         col_ref[...] = jnp.where(lane == r, total, col_ref[...])
         return carry
 
-    lax.fori_loop(0, 32, cell, 0, unroll=8)
+    lax.fori_loop(0, 32, cell, 0, unroll=16)
     live = live_ref[...] < 32.0
     density = jnp.where(live, col_ref[...].T[0:32, :] / (SLOTS / 2.0), 0.0)
     safe = jnp.where(live, density, 1.0)
@@ -183,35 +183,26 @@
             rho_ref[a, e] = density[r:r + 2, :]
 
 
-def body_kernel(recv_ref, pos_ref, press_ref, force_ref, load_ref, list_ref, fa_ref, used_ref, anchor_ref, near_ref, side_ref, arm_ref, react_ref, sums_ref, pick_ref, order_ref, sem):
+def body_kernel(recv_ref, pos_ref, press_ref, force_ref, load_ref, list_ref, fa_ref, anchor_ref, near_ref, side_ref, half_ref, arm_ref, sums_ref):
     slots = recv_ref.shape[0]
     blank = jnp.zeros((8, SLOTS), F32)
-    near_ref[...] = jnp.zeros_like(near_ref)
-    react_ref[...] = jnp.zeros_like(react_ref)
+    near_ref[:, 192:, :] = jnp.zeros((TOGETHER, 64, SLOTS), F32)
+    force_ref[...] = jnp.zeros_like(force_ref)
     sums_ref[...] = jnp.zeros_like(sums_ref)
-    fa_ref[27 * slots:, :] = jnp.zeros((5 * slots, SLOTS), F32)
+    fa_ref[24 * slots:, :] = jnp.zeros((8 * slots, SLOTS), F32)
     extras = jnp.concatenate([recv_ref[:, 3, :], jnp.zeros((SLOTS - slots, SLOTS), F32)], axis=0).T
-    used_ref[...] = extras[24:32, :]
-    down = pltpu.make_async_copy(used_ref, pick_ref, sem)
-    down.start()
     shapes = [recv_ref[:, m, :] for m in range(3)]
-    for r, v in enumerate(own_rows(shapes) + shapes):
+    for r, v in enumerate(own_rows(shapes)):
         fa_ref[r * slots:(r + 1) * slots, :] = v
+    pieces = [split3(v) for v in shapes]
+    arm_ref[7 * slots:, :] = jnp.zeros((9 * slots, SLOTS), F32)
+    for r, v in enumerate([jnp.ones_like(shapes[0])] + [p[0] for p in pieces] + [p[1] + p[2] for p in pieces]):
+        arm_ref[r * slots:(r + 1) * slots, :] = v
     for t in range(slots):
-        for m in range(3):
+        for m in range(4):
             anchor_ref[t, 8 * m:8 * m + 8, :] = jnp.broadcast_to(extras[8 * m:8 * m + 8, t:t + 1], (8, SLOTS))
     press = jnp.concatenate([press_ref[(a * 4 + 1 + e) * 4 + 1:(a * 4 + 1 + e) * 4 + 3, :] for a in range(2) for e in range(2)], axis=0)
     list_ref[...] = press * (24.0 / SLOTS)
-    down.wait()
-    busy = jnp.int32(0)
-    spare = jnp.int32(0)
-    for t in range(slots):
-        order_ref[busy] = t
-        flag = pick_ref[0, t] > 0.0
-        spare = jnp.where(flag, spare, t)
-        busy = busy + flag.astype(jnp.int32)
-    for n in range(TOGETHER - 1):
-        order_ref[busy + n] = spare
     coords = [pos_ref[m] for m in range(3)]
 
     def one(t, n):
@@ -220,53 +211,42 @@
             near_ref[n, 8 * r:8 * r + 8, :] = v
         for m in range(3):
             side_ref[n, 8 * m:8 * m + 8, :] = -gaps[m]
-        side_ref[n, 24:32, :] = list_ref[...] * pick_ref[0, t]
-        turned = fa_ref[pl.ds(t, ROWS, stride=slots), :].T
-        lhs = turned.astype(BF16)
-        for m in range(3):
-            arm_ref[n, m] = jnp.broadcast_to(turned[:, 24 + m:25 + m], (SLOTS, SLOTS))
-        sums = [blank] * 6
-        reacts = []
+        side_ref[n, 24:32, :] = list_ref[...] * anchor_ref[t, 24:32, :]
+        lhs = fa_ref[pl.ds(t, ROWS, stride=slots), :].T.astype(BF16)
+        arms = arm_ref[pl.ds(t, 16, stride=slots), :].astype(BF16)
         for g in range(4):
             rhs = jnp.concatenate(
                 [near_ref[n, pl.ds(c, ROWS, stride=8), :].astype(BF16) for c in (2 * g, 2 * g + 1)], axis=1
             )
             q = jnp.maximum(jnp.dot(lhs, rhs, preferred_element_type=F32), 0.0)
             q = q * q
-            part = [[blank] * 4 for _ in range(2)]
-            for i in range(16):
-                arm = [arm_ref[n, m, 8 * i:8 * i + 8, :] for m in range(3)]
-                for h in range(2):
-                    v = q[8 * i:8 * i + 8, h * SLOTS:(h + 1) * SLOTS]
-                    part[h][0] = part[h][0] + v
-                    for m in range(3):
-                        part[h][1 + m] = part[h][1 + m] + v * arm[m]
+            top = q.astype(BF16)
+            low = (q - top.astype(F32)).astype(BF16)
+            got = jnp.dot(arms, top, preferred_element_type=F32) + jnp.dot(arms, low, preferred_element_type=F32)
             for h in range(2):
-                c = 2 * g + h
-                pr = side_ref[n, 24 + c:25 + c, :]
-                gap = [side_ref[n, 8 * m + c:8 * m + c + 1, :] for m in range(3)]
-                push = [v * pr for v in part[h]]
-                for m in range(3):
-                    total = push[1 + m] + gap[m] * push[0]
-                    reacts.append(total)
-                    sums[m] = sums[m] + total
-                    u, v = (m + 1) % 3, (m + 2) % 3
-                    sums[3 + m] = sums[3 + m] + (push[1 + u] * gap[v] - push[1 + v] * gap[u])
-        return reacts, sums
+                half_ref[n, 16 * g + 8 * h:16 * g + 8 * h + 8, :] = got[0:8, h * SLOTS:(h + 1) * SLOTS]
+        rows = [half_ref[n, pl.ds(r, 8, stride=8), :] for r in range(7)]
+        factor = side_ref[n, 24:32, :]
+        push = [rows[0] * factor] + [(rows[1 + m] + rows[4 + m]) * factor for m in range(3)]
+        gap = [side_ref[n, 8 * m:8 * m + 8, :] for m in range(3)]
+        reacts = [push[1 + m] + gap[m] * push[0] for m in range(3)]
+        turns = []
+        for m in range(3):
+            u, v = (m + 1) % 3, (m + 2) % 3
+            turns.append(push[1 + u] * gap[v] - push[1 + v] * gap[u])
+        return reacts, reacts + turns
 
     def step(i, carry):
-        picked = [order_ref[TOGETHER * i + n] for n in range(TOGETHER)]
+        picked = [TOGETHER * i + n for n in range(TOGETHER)]
         done = [one(t, n) for n, t in enumerate(picked)]
-        for r in range(24):
-            react_ref[r] = react_ref[r] + sum(d[0][r] for d in done)
+        for m in range(3):
+            force_ref[m] = force_ref[m] + sum(d[0][m] for d in done)
         for t, d in zip(picked, done):
             for r in range(6):
                 sums_ref[t, r:r + 1, :] = jnp.sum(d[1][r], axis=0, keepdims=True)
         return carry
 
-    lax.fori_loop(0, (busy + TOGETHER - 1) // TOGETHER, step, 0)
-    for r in range(24):
-        force_ref[r % 3, r // 3:r // 3 + 1, :] = jnp.sum(react_ref[r], axis=0, keepdims=True)
+    lax.fori_loop(0, slots // TOGETHER, step, 0)
     total = jnp.sum(sums_ref[...], axis=2)
     load_ref[...] = jnp.zeros_like(load_ref)
     for g in range(slots // CAPACITY):
@@ -320,16 +300,15 @@
             out_ref[m, a, e, pl.ds(f, 1), :] = own - force_ref[m, pl.ds(c, 1), :]
         return carry
 
-    lax.fori_loop(0, 8, cell, 0, unroll=4)
+    lax.fori_loop(0, 8, cell, 0, unroll=8)
 
 
 def gather_kernel(slot_ref, got_ref, out_ref, pick_ref):
     bodies = out_ref.shape[1]
-    pick_ref[...] = jnp.zeros_like(pick_ref)
     for b in range(bodies):
         place = slot_ref[b]
         pick_ref[b:b + 1, :] = got_ref[place // 8, pl.ds(place % 8, 1), :]
-    out_ref[...] = pick_ref[...].T[0:6, 0:bodies] / BODY_PARTS
+    out_ref[...] = pick_ref[...].T[0:6, :] / BODY_PARTS
 
 
 def vmem():
@@ -430,16 +409,12 @@
         scratch_shapes=[
             pltpu.VMEM((8, SLOTS), F32),
             pltpu.VMEM((ROWS * slots, SLOTS), F32),
-            pltpu.VMEM((8, SLOTS), F32),
-            pltpu.VMEM((slots, 24, SLOTS), F32),
+            pltpu.VMEM((slots, 32, SLOTS), F32),
             pltpu.VMEM((TOGETHER, ROWS * 8, SLOTS), F32),
             pltpu.VMEM((TOGETHER, 32, SLOTS), F32),
-            pltpu.VMEM((TOGETHER, 3, SLOTS, SLOTS), F32),
-            pltpu.VMEM((24, 8, SLOTS), F32),
+            pltpu.VMEM((TOGETHER, 64, SLOTS), F32),
+            pltpu.VMEM((16 * slots, SLOTS), F32),
             pltpu.VMEM((slots, 8, SLOTS), F32),
-            pltpu.SMEM((8, SLOTS), F32),
-            pltpu.SMEM((slots + TOGETHER,), jnp.int32),
-            pltpu.SemaphoreType.DMA,
         ],
         compiler_params=params(),
         cost_estimate=cost(60),
@@ -465,7 +440,7 @@
         out_shape=shaped(6, bodies),
         in_specs=[smem(), vmem()],
         out_specs=vmem(),
-        scratch_shapes=[pltpu.VMEM((SLOTS, SLOTS), F32)],
+        scratch_shapes=[pltpu.VMEM((bodies, SLOTS), F32)],
         compiler_params=params(),
         cost_estimate=cost(1),
         name="collect",

time: 79.2 us -> 77.4 us (0.977)
  starting transfers between devices: 44.4 us -> 40.4 us
  Pallas kernels: 28.5 us -> 30.1 us
    all_to_all x1, starting transfers between devices: 11 us -> 6.98 us  [local(): got = lax.all_to_all(load, 'gx', 0, 0, tiled=True)]
    pallas_call x1, Pallas kernels: 6.62 us -> 9.26 us  [local(): pl.pallas_call(body_kernel, out_shape=(inner(3, 8, SLOTS), inner(groups,...]
  transfers between devices with their start and end apart: 10 -> 10, of which waited for: 3 -> 3; matrix products, arithmetic and copies ran while one was open for 0% -> 0% of each run, Pallas kernels for 33% -> 36%
where the time goes in v4:
time: 77.4 us; the launch traced here: 76.8 us
  starting transfers between devices  40.4 us (52%)
  Pallas kernels  30.1 us (39%)
  waiting for transfers between devices  5.43 us (7%)
    ppermute x8, starting transfers between devices, both_ways(): return (lax.ppermute(value, axis, ups), lax.ppermute(value, axis, downs))  23.9 us
    pallas_call x1, Pallas kernels, local(): pl.pallas_call(density_kernel, out_shape=(shaped(2, 2, 2, SLOTS), inner(3...  10.4 us
    all_to_all x1, starting transfers between devices, local(): lax.all_to_all(send.reshape(groups, CAPACITY, 4, SLOTS), 'gx', 0, 0, tile...  9.54 us
    pallas_call x1, Pallas kernels, local(): pl.pallas_call(body_kernel, out_shape=(inner(3, 8, SLOTS), inner(groups,...  9.26 us
    all_to_all x1, starting transfers between devices, local(): got = lax.all_to_all(load, 'gx', 0, 0, tiled=True)  6.98 us
    pallas_call x1, Pallas kernels, local(): pl.pallas_call(accel_kernel, out_shape=shaped(3, 2, 2, 2, SLOTS), in_spec...  6.61 us
    ppermute x8, waiting for transfers between devices, both_ways(): return (lax.ppermute(value, axis, ups), lax.ppermute(value, axis, downs))  4.24 us
    pallas_call x1, Pallas kernels, local(): pl.pallas_call(pack_kernel, out_shape=(inner(slots, 4, SLOTS), shaped(bod...  1.59 us
  transfers between devices with their start and end apart: 10, of which 3 were waited for; matrix products, arithmetic and copies ran while one was open for 0% of the time, Pallas kernels for 36%

profile of v4, /device:TPU:39, one launch (start us, length us, event | category | flops | bytes accessed | tf_op | source)
XLA Modules:
  0.0 76.8 jit_solution(3238613055831451862)
XLA Ops:
  0.6 0.8 %place.1.pos_ref = f32[3,8,128]{2,1,0:T(8,128)S(1)} custom-call(f32[3,2,2,2,128]{4,3,2,1,0:T(2,128)} %pos_ref.1, s32[2,2,2]{2,1,0:T(2,128)} %count_ref.1), custom_call_target="tpu_custom_call" | custom-call | tf_op jit(solution)/shard_map/place/pallas_call | solution.py:353
  1.5 2.5 %collective-permute-start.1 = (f32[3,8,128]{2,1,0:T(8,128)S(1)}, f32[3,8,128]{2,1,0:T(8,128)S(1)}, u32[]{:S(2)}, u32[]{:S(2)}) collective-permute-start(f32[3,8,128]{2,1,0:T(8,128)S(1)} %place.1.pos_ref), channel_id=1, source_target_pairs={{1,0},{2,1},{3,2},{5,4},{6,5},{7,6},{9,8},{10,9},{11,10},{13,12},{... | collective-permute-start | bytes 36872 | tf_op jit(solution)/shard_map/ppermute | solution.py:342
  3.9 1.3 %collective-permute-start = (f32[3,8,128]{2,1,0:T(8,128)S(1)}, f32[3,8,128]{2,1,0:T(8,128)S(1)}, u32[]{:S(2)}, u32[]{:S(2)}) collective-permute-start(f32[3,8,128]{2,1,0:T(8,128)S(1)} %place.1.pos_ref), channel_id=1, source_target_pairs={{0,1},{1,2},{2,3},{4,5},{5,6},{6,7},{8,9},{9,10},{10,11},{12,13},{... | collective-permute-start | bytes 36872 | tf_op jit(solution)/shard_map/ppermute | solution.py:342
  5.2 1.6 %pack.1 = (f32[48,4,128]{2,1,0:T(4,128)}, s32[24]{0:T(128)}) custom-call(f32[3,24,128]{2,1,0:T(8,128)} %shape_ref.1, f32[3,8,24]{2,1,0:T(8,128)} %bitcast.22, s32[1,24]{1,0:T(1,128)} %bitcast.24, s32[8,24]{1,0:T(8,128)} %bitcast.23), custom_call_target="tpu_custom_call" | custom-call | flops 400000000 | bytes 262144 | tf_op jit(solution)/shard_map/pack/pallas_call | solution.py:361
  6.8 0.0 collective-permute-done.1
  6.8 1.5 %collective-permute-done = f32[3,8,128]{2,1,0:T(8,128)S(1)} collective-permute-done((f32[3,8,128]{2,1,0:T(8,128)S(1)}, f32[3,8,128]{2,1,0:T(8,128)S(1)}, u32[]{:S(2)}, u32[]{:S(2)}) %collective-permute-start) | collective-permute-done | bytes 12320 | tf_op jit(solution)/shard_map/ppermute | solution.py:342
  8.4 2.1 %collective-permute-start.3 = (f32[3,3,8,128]{3,2,1,0:T(8,128)S(1)}, f32[3,3,8,128]{3,2,1,0:T(8,128)S(1)}, u32[]{:S(2)}, u32[]{:S(2)}) collective-permute-start(f32[3,3,8,128]{3,2,1,0:T(8,128)S(1)} %get-tuple-element.28), channel_id=1, source_target_pairs={{4,0},{8,4},{12,8},{16,12},{20,16},{24,20},{28,24},{5,1},{9,5},{13... | collective-permute-start | bytes 110600 | tf_op jit(solution)/shard_map/ppermute | solution.py:342
  10.4 3.2 %collective-permute-start.2 = (f32[3,3,8,128]{3,2,1,0:T(8,128)S(1)}, f32[3,3,8,128]{3,2,1,0:T(8,128)S(1)}, u32[]{:S(2)}, u32[]{:S(2)}) collective-permute-start(f32[3,3,8,128]{3,2,1,0:T(8,128)S(1)} %get-tuple-element.28), channel_id=1, source_target_pairs={{0,4},{4,8},{8,12},{12,16},{16,20},{20,24},{24,28},{1,5},{5,9},{9,... | collective-permute-start | bytes 110600 | tf_op jit(solution)/shard_map/ppermute | solution.py:342
  13.7 0.0 collective-permute-done.3
  13.7 2.7 %collective-permute-done.2 = f32[3,3,8,128]{3,2,1,0:T(8,128)S(1)} collective-permute-done((f32[3,3,8,128]{3,2,1,0:T(8,128)S(1)}, f32[3,3,8,128]{3,2,1,0:T(8,128)S(1)}, u32[]{:S(2)}, u32[]{:S(2)}) %collective-permute-start.2) | collective-permute-done | bytes 36896 | tf_op jit(solution)/shard_map/ppermute | solution.py:342
  16.4 5.4 %collective-permute-start.5 = (f32[9,3,8,128]{3,2,1,0:T(8,128)S(1)}, f32[9,3,8,128]{3,2,1,0:T(8,128)S(1)}, u32[]{:S(2)}, u32[]{:S(2)}) collective-permute-start(f32[9,3,8,128]{3,2,1,0:T(8,128)S(1)} %bitcast.13), channel_id=1, source_target_pairs={{32,0},{64,32},{96,64},{128,96},{160,128},{192,160},{224,192},{256... | collective-permute-start | bytes 331784 | tf_op jit(solution)/shard_map/ppermute | solution.py:342
  21.8 3.9 %collective-permute-start.4 = (f32[9,3,8,128]{3,2,1,0:T(8,128)S(1)}, f32[9,3,8,128]{3,2,1,0:T(8,128)S(1)}, u32[]{:S(2)}, u32[]{:S(2)}) collective-permute-start(f32[9,3,8,128]{3,2,1,0:T(8,128)S(1)} %bitcast.14), channel_id=1, source_target_pairs={{0,32},{32,64},{64,96},{96,128},{128,160},{160,192},{192,224},{224... | collective-permute-start | bytes 331784 | tf_op jit(solution)/shard_map/ppermute | solution.py:342
  25.7 9.5 %all-to-all-start = ((f32[16,3,4,128]{3,2,1,0:T(4,128)}), f32[16,3,4,128]{3,2,1,0:T(4,128)S(1)}, u32[]{:S(2)}, u32[]{:S(2)}) async-start(f32[16,3,4,128]{3,2,1,0:T(4,128)} %bitcast.10), calls=%async_computation | async-start | bytes 196608 | tf_op jit(solution)/shard_map/all_to_all | solution.py:373
  35.3 0.0 collective-permute-done.5.right_ref
  35.3 0.0 collective-permute-done.4.left_ref
  35.3 10.4 %density.1 = (f32[2,2,2,128]{3,2,1,0:T(2,128)}, f32[32,128]{1,0:T(8,128)S(1)}, bf16[64,32,128]{2,1,0:T(8,128)(2,1)S(1)}, f32[64,8,128]{2,1,0:T(8,128)S(1)}, bf16[8,128,32]{2,1,0:T(8,128)(2,1)S(1)}) custom-call(f32[9,3,8,128]{3,2,1,0:T(8,128)S(1)} %collective-permute-done.4.left_ref, f32[9,3,8,128]{3,2,1,0:T(8,128)S(1)} %bitcast.15, ...), custom_call_target="tpu_custom_call" | custom-call | flops 6000000000 | bytes 262144 | tf_op jit(solution)/shard_map/density/pallas_call | solution.py:378
  45.7 2.0 %collective-permute-start.7 = (f32[32,128]{1,0:T(8,128)S(1)}, f32[32,128]{1,0:T(8,128)S(1)}, u32[]{:S(2)}, u32[]{:S(2)}) collective-permute-start(f32[32,128]{1,0:T(8,128)S(1)} %get-tuple-element.22.press_ref.mid_ref), channel_id=1, source_target_pairs={{32,0},{64,32},{96,64},{128,96},{160,128},{192,160},{224,192},{256... | collective-permute-start | bytes 49160 | tf_op jit(solution)/shard_map/ppermute | solution.py:342
  47.7 3.6 %collective-permute-start.6 = (f32[32,128]{1,0:T(8,128)S(1)}, f32[32,128]{1,0:T(8,128)S(1)}, u32[]{:S(2)}, u32[]{:S(2)}) collective-permute-start(f32[32,128]{1,0:T(8,128)S(1)} %get-tuple-element.22.press_ref.mid_ref), channel_id=1, source_target_pairs={{0,32},{32,64},{64,96},{96,128},{128,160},{160,192},{192,224},{224... | collective-permute-start | bytes 49160 | tf_op jit(solution)/shard_map/ppermute | solution.py:342
  51.2 0.0 all-to-all-done
  51.3 9.3 %bodies.1 = (f32[3,8,128]{2,1,0:T(8,128)S(1)}, f32[16,8,128]{2,1,0:T(8,128)}) custom-call(f32[48,4,128]{2,1,0:T(4,128)S(1)} %bitcast.16, f32[3,8,128]{2,1,0:T(8,128)S(1)} %place.1.pos_ref, f32[32,128]{1,0:T(8,128)S(1)} %get-tuple-element.22.press_ref.mid_ref), custom_call_target="tpu_custom_call" | custom-call | flops 6000000000 | bytes 262144 | tf_op jit(solution)/shard_map/bodies/pallas_call | solution.py:404
  60.5 7.0 %all-to-all-start.1 = ((f32[16,8,128]{2,1,0:T(8,128)}), f32[16,8,128]{2,1,0:T(8,128)S(1)}, u32[]{:S(2)}, u32[]{:S(2)}) async-start(f32[16,8,128]{2,1,0:T(8,128)} %get-tuple-element.26), calls=%async_computation.1 | async-start | bytes 131072 | tf_op jit(solution)/shard_map/all_to_all | solution.py:423
  67.5 0.0 collective-permute-done.7.right_ref
  67.5 0.0 collective-permute-done.6.left_ref
  67.5 6.6 %accel.1 = f32[3,2,2,2,128]{4,3,2,1,0:T(2,128)} custom-call(bf16[8,128,32]{2,1,0:T(8,128)(2,1)S(1)} %get-tuple-element.19.own_ref, bf16[64,32,128]{2,1,0:T(8,128)(2,1)S(1)} %get-tuple-element.20.near_ref, f32[64,8,128]{2,1,0:T(8,128)S(1)} %get-tuple-element.21.coord_ref, f32[32,128]{1,0:T(8,128)S(1)} %collective-permute-done.6.left_ref, ...), custom_call_target="tpu_custom_call" | custom-call | flops 4000000000 | bytes 262144 | tf_op jit(solution)/shard_map/accel/pallas_call | solution.py:424
  74.1 1.2 %all-to-all-done.1.got_ref = f32[16,8,128]{2,1,0:T(8,128)S(1)} async-done(((f32[16,8,128]{2,1,0:T(8,128)}), f32[16,8,128]{2,1,0:T(8,128)S(1)}, u32[]{:S(2)}, u32[]{:S(2)}) %all-to-all-start.1) | async-done | bytes 65568 | tf_op jit(solution)/shard_map/all_to_all | solution.py:423
  75.3 1.5 %collect.1 = f32[6,24]{1,0:T(8,128)} custom-call(s32[24]{0:T(128)} %get-tuple-element.25.slot_ref, f32[16,8,128]{2,1,0:T(8,128)S(1)} %all-to-all-done.1.got_ref), custom_call_target="tpu_custom_call" | custom-call | flops 100000000 | bytes 262144 | tf_op jit(solution)/shard_map/collect/pallas_call | solution.py:438
  (2 shorter events, 0.0 us)
Async XLA Ops:
  1.5 5.4 %collective-permute-start.1 = (f32[3,8,128]{2,1,0:T(8,128)S(1)}, f32[3,8,128]{2,1,0:T(8,128)S(1)}, u32[]{:S(2)}, u32[]{:S(2)}) collective-permute-start(f32[3,8,128]{2,1,0:T(8,128)S(1)} %place.1.pos_ref), channel_id=1, source_target_pairs={{1,0},{2,1},{3,2},{5,4},{6,5},{7,6},{9,8},{10,9},{11,10},{13,12},{... | collective-permute-start | bytes 36872 | tf_op jit(solution)/shard_map/ppermute | solution.py:342
  3.9 4.4 %collective-permute-start = (f32[3,8,128]{2,1,0:T(8,128)S(1)}, f32[3,8,128]{2,1,0:T(8,128)S(1)}, u32[]{:S(2)}, u32[]{:S(2)}) collective-permute-start(f32[3,8,128]{2,1,0:T(8,128)S(1)} %place.1.pos_ref), channel_id=1, source_target_pairs={{0,1},{1,2},{2,3},{4,5},{5,6},{6,7},{8,9},{9,10},{10,11},{12,13},{... | collective-permute-start | bytes 36872 | tf_op jit(solution)/shard_map/ppermute | solution.py:342
  8.4 5.3 %collective-permute-start.3 = (f32[3,3,8,128]{3,2,1,0:T(8,128)S(1)}, f32[3,3,8,128]{3,2,1,0:T(8,128)S(1)}, u32[]{:S(2)}, u32[]{:S(2)}) collective-permute-start(f32[3,3,8,128]{3,2,1,0:T(8,128)S(1)} %get-tuple-element.28), channel_id=1, source_target_pairs={{4,0},{8,4},{12,8},{16,12},{20,16},{24,20},{28,24},{5,1},{9,5},{13... | collective-permute-start | bytes 110600 | tf_op jit(solution)/shard_map/ppermute | solution.py:342
  10.4 5.9 %collective-permute-start.2 = (f32[3,3,8,128]{3,2,1,0:T(8,128)S(1)}, f32[3,3,8,128]{3,2,1,0:T(8,128)S(1)}, u32[]{:S(2)}, u32[]{:S(2)}) collective-permute-start(f32[3,3,8,128]{3,2,1,0:T(8,128)S(1)} %get-tuple-element.28), channel_id=1, source_target_pairs={{0,4},{4,8},{8,12},{12,16},{16,20},{20,24},{24,28},{1,5},{5,9},{9,... | collective-permute-start | bytes 110600 | tf_op jit(solution)/shard_map/ppermute | solution.py:342
  16.4 18.9 %collective-permute-start.5 = (f32[9,3,8,128]{3,2,1,0:T(8,128)S(1)}, f32[9,3,8,128]{3,2,1,0:T(8,128)S(1)}, u32[]{:S(2)}, u32[]{:S(2)}) collective-permute-start(f32[9,3,8,128]{3,2,1,0:T(8,128)S(1)} %bitcast.13), channel_id=1, source_target_pairs={{32,0},{64,32},{96,64},{128,96},{160,128},{192,160},{224,192},{256... | collective-permute-start | bytes 331784 | tf_op jit(solution)/shard_map/ppermute | solution.py:342
  21.8 13.5 %collective-permute-start.4 = (f32[9,3,8,128]{3,2,1,0:T(8,128)S(1)}, f32[9,3,8,128]{3,2,1,0:T(8,128)S(1)}, u32[]{:S(2)}, u32[]{:S(2)}) collective-permute-start(f32[9,3,8,128]{3,2,1,0:T(8,128)S(1)} %bitcast.14), channel_id=1, source_target_pairs={{0,32},{32,64},{64,96},{96,128},{128,160},{160,192},{192,224},{224... | collective-permute-start | bytes 331784 | tf_op jit(solution)/shard_map/ppermute | solution.py:342
  25.7 25.5 %all-to-all-start = ((f32[16,3,4,128]{3,2,1,0:T(4,128)}), f32[16,3,4,128]{3,2,1,0:T(4,128)S(1)}, u32[]{:S(2)}, u32[]{:S(2)}) async-start(f32[16,3,4,128]{3,2,1,0:T(4,128)} %bitcast.10), calls=%async_computation | async-start | bytes 196608 | tf_op jit(solution)/shard_map/all_to_all | solution.py:373
  45.7 21.8 %collective-permute-start.7 = (f32[32,128]{1,0:T(8,128)S(1)}, f32[32,128]{1,0:T(8,128)S(1)}, u32[]{:S(2)}, u32[]{:S(2)}) collective-permute-start(f32[32,128]{1,0:T(8,128)S(1)} %get-tuple-element.22.press_ref.mid_ref), channel_id=1, source_target_pairs={{32,0},{64,32},{96,64},{128,96},{160,128},{192,160},{224,192},{256... | collective-permute-start | bytes 49160 | tf_op jit(solution)/shard_map/ppermute | solution.py:342
  47.7 19.8 %collective-permute-start.6 = (f32[32,128]{1,0:T(8,128)S(1)}, f32[32,128]{1,0:T(8,128)S(1)}, u32[]{:S(2)}, u32[]{:S(2)}) collective-permute-start(f32[32,128]{1,0:T(8,128)S(1)} %get-tuple-element.22.press_ref.mid_ref), channel_id=1, source_target_pairs={{0,32},{32,64},{64,96},{96,128},{128,160},{160,192},{192,224},{224... | collective-permute-start | bytes 49160 | tf_op jit(solution)/shard_map/ppermute | solution.py:342
  60.5 14.8 %all-to-all-start.1 = ((f32[16,8,128]{2,1,0:T(8,128)}), f32[16,8,128]{2,1,0:T(8,128)S(1)}, u32[]{:S(2)}, u32[]{:S(2)}) async-start(f32[16,8,128]{2,1,0:T(8,128)} %get-tuple-element.26), calls=%async_computation.1 | async-start | bytes 131072 | tf_op jit(solution)/shard_map/all_to_all | solution.py:423

commit v5 on v4

--- a/solution.py
+++ b/solution.py
@@ -84,6 +84,12 @@
         send_ref[slot, 3:4, :] = extra_ref[b:b + 1, :]
 
 
+def block_of(t):
+    by = jnp.where(lax.axis_index("yz") % 2 == 1, t // 3, 2 - t // 3)
+    bz = jnp.where(lax.axis_index("body") % 2 == 1, t % 3, 2 - t % 3)
+    return by, bz
+
+
 def density_kernel(left_ref, mid_ref, right_ref, rho_ref, press_ref, near_out, coord_out, own_out, near_ref, coord_ref, own_ref, fb_ref, fa_ref, fr_ref, live_ref, col_ref):
     index = [lax.axis_index(n) for n in ("gx", "yz", "body")]
     size = [lax.axis_size(n) for n in ("gx", "yz", "body")]
@@ -94,8 +100,7 @@
     fr_ref[...] = jnp.zeros_like(fr_ref)
 
     def block(t, carry):
-        by = t // 3
-        bz = t % 3
+        by, bz = block_of(t)
         ny = index[1] + by - 1
         nz = index[2] + bz - 1
         inside = (ny >= 0) & (ny < size[1]) & (nz >= 0) & (nz < size[2])
@@ -122,7 +127,7 @@
                 fr_ref[8 * m:8 * m + 8, :] = coords[m]
             if kind == 0:
                 for r, v in enumerate(own_rows(coords)):
-                    fa_ref[t, 8 * r:8 * r + 8, :] = v
+                    fa_ref[by * 3 + bz, 8 * r:8 * r + 8, :] = v
             for c in range(8):
                 a, e, f = c // 4, c // 2 % 2, c % 2
                 at_x = 1 + a if kind == 0 else 3 - 3 * a
@@ -342,6 +347,13 @@
     return lax.ppermute(value, axis, ups), lax.ppermute(value, axis, downs)
 
 
+def swap_ways(value, axis):
+    count = lax.axis_size(axis)
+    inner_pairs = [(i, i ^ 1) for i in range(count)]
+    outer_pairs = [(i, (i + 1 ^ 1) - 1) for i in range(1, count - 1)]
+    return lax.ppermute(value, axis, inner_pairs), lax.ppermute(value, axis, outer_pairs)
+
+
 def shaped(*dims, dtype=F32):
     return jax.ShapeDtypeStruct(dims, dtype)
 
@@ -368,11 +380,11 @@
         cost_estimate=cost(4),
         name="pack",
     )(body_shape, jnp.swapaxes(body_anchor, 1, 2), body_dest.reshape(1, bodies), body_cell.T)
-    low, high = both_ways(pos, "body")
+    low, high = swap_ways(pos, "body")
     low, high, send = lax.optimization_barrier((low, high, send))
     recv = lax.all_to_all(send.reshape(groups, CAPACITY, 4, SLOTS), "gx", 0, 0, tiled=True).reshape(slots, 4, SLOTS)
     line = jnp.stack([low, pos, high])
-    low, high = both_ways(line, "yz")
+    low, high = swap_ways(line, "yz")
     sheet = jnp.stack([low, line, high]).reshape(9, 3, 8, SLOTS)
     left, right = both_ways(sheet, "gx")
     rho, press, near, coord, own = pl.pallas_call(

time: 77.4 us -> 79.2 us (1.023)
  the two profiles are of different devices: /device:TPU:39 before, /device:TPU:27 now
where the time goes in v5:
time: 79.2 us; the launch traced here: 78.6 us
  starting transfers between devices  42.8 us (54%)
  Pallas kernels  30.2 us (38%)
  waiting for transfers between devices  4.87 us (6%)
    ppermute x4, starting transfers between devices, both_ways(): return (lax.ppermute(value, axis, ups), lax.ppermute(value, axis, downs))  14.9 us
    pallas_call x1, Pallas kernels, local(): pl.pallas_call(density_kernel, out_shape=(shaped(2, 2, 2, SLOTS), inner(3...  10.4 us
    all_to_all x1, starting transfers between devices, local(): lax.all_to_all(send.reshape(groups, CAPACITY, 4, SLOTS), 'gx', 0, 0, tile...  9.54 us
    pallas_call x1, Pallas kernels, local(): pl.pallas_call(body_kernel, out_shape=(inner(3, 8, SLOTS), inner(groups,...  9.26 us
    ppermute x2, starting transfers between devices, swap_ways(): lax.ppermute(value, axis, outer_pairs)  7.52 us
    all_to_all x1, starting transfers between devices, local(): got = lax.all_to_all(load, 'gx', 0, 0, tiled=True)  6.98 us
    pallas_call x1, Pallas kernels, local(): pl.pallas_call(accel_kernel, out_shape=shaped(3, 2, 2, 2, SLOTS), in_spec...  6.61 us
    ppermute x2, starting transfers between devices, swap_ways(): lax.ppermute(value, axis, inner_pairs)  3.84 us
  transfers between devices with their start and end apart: 10, of which 3 were waited for; matrix products, arithmetic and copies ran while one was open for 0% of the time, Pallas kernels for 35%

profile of v5, /device:TPU:27, one launch (start us, length us, event | category | flops | bytes accessed | tf_op | source)
XLA Modules:
  0.0 78.6 jit_solution(4353072998304057039)
XLA Ops:
  0.6 0.8 %place.1.pos_ref = f32[3,8,128]{2,1,0:T(8,128)S(1)} custom-call(f32[3,2,2,2,128]{4,3,2,1,0:T(2,128)} %pos_ref.1, s32[2,2,2]{2,1,0:T(2,128)} %count_ref.1), custom_call_target="tpu_custom_call" | custom-call | tf_op jit(solution)/shard_map/place/pallas_call | solution.py:365
  1.5 3.1 %collective-permute-start.1 = (f32[3,8,128]{2,1,0:T(8,128)S(1)}, f32[3,8,128]{2,1,0:T(8,128)S(1)}, u32[]{:S(2)}, u32[]{:S(2)}) collective-permute-start(f32[3,8,128]{2,1,0:T(8,128)S(1)} %place.1.pos_ref), channel_id=1, source_target_pairs={{1,2},{2,1},{5,6},{6,5},{9,10},{10,9},{13,14},{14,13},{17,18},{18,... | collective-permute-start | bytes 36872 | tf_op jit(solution)/shard_map/ppermute | solution.py:354
  4.6 1.9 %collective-permute-start = (f32[3,8,128]{2,1,0:T(8,128)S(1)}, f32[3,8,128]{2,1,0:T(8,128)S(1)}, u32[]{:S(2)}, u32[]{:S(2)}) collective-permute-start(f32[3,8,128]{2,1,0:T(8,128)S(1)} %place.1.pos_ref), channel_id=1, source_target_pairs={{0,1},{1,0},{2,3},{3,2},{4,5},{5,4},{6,7},{7,6},{8,9},{9,8},{10,11... | collective-permute-start | bytes 36872 | tf_op jit(solution)/shard_map/ppermute | solution.py:354
  6.5 1.6 %pack.1 = (f32[48,4,128]{2,1,0:T(4,128)}, s32[24]{0:T(128)}) custom-call(f32[3,24,128]{2,1,0:T(8,128)} %shape_ref.1, f32[3,8,24]{2,1,0:T(8,128)} %bitcast.22, s32[1,24]{1,0:T(1,128)} %bitcast.24, s32[8,24]{1,0:T(8,128)} %bitcast.23), custom_call_target="tpu_custom_call" | custom-call | flops 400000000 | bytes 262144 | tf_op jit(solution)/shard_map/pack/pallas_call | solution.py:373
  8.1 0.0 collective-permute-done.1
  8.1 0.9 %collective-permute-done = f32[3,8,128]{2,1,0:T(8,128)S(1)} collective-permute-done((f32[3,8,128]{2,1,0:T(8,128)S(1)}, f32[3,8,128]{2,1,0:T(8,128)S(1)}, u32[]{:S(2)}, u32[]{:S(2)}) %collective-permute-start) | collective-permute-done | bytes 12320 | tf_op jit(solution)/shard_map/ppermute | solution.py:354
  9.0 4.4 %collective-permute-start.3 = (f32[3,3,8,128]{3,2,1,0:T(8,128)S(1)}, f32[3,3,8,128]{3,2,1,0:T(8,128)S(1)}, u32[]{:S(2)}, u32[]{:S(2)}) collective-permute-start(f32[3,3,8,128]{3,2,1,0:T(8,128)S(1)} %get-tuple-element.28), channel_id=1, source_target_pairs={{4,8},{8,4},{12,16},{16,12},{20,24},{24,20},{5,9},{9,5},{13,17},{1... | collective-permute-start | bytes 110600 | tf_op jit(solution)/shard_map/ppermute | solution.py:354
  13.5 1.9 %collective-permute-start.2 = (f32[3,3,8,128]{3,2,1,0:T(8,128)S(1)}, f32[3,3,8,128]{3,2,1,0:T(8,128)S(1)}, u32[]{:S(2)}, u32[]{:S(2)}) collective-permute-start(f32[3,3,8,128]{3,2,1,0:T(8,128)S(1)} %get-tuple-element.28), channel_id=1, source_target_pairs={{0,4},{4,0},{8,12},{12,8},{16,20},{20,16},{24,28},{28,24},{1,5},{5... | collective-permute-start | bytes 110600 | tf_op jit(solution)/shard_map/ppermute | solution.py:354
  15.4 0.0 collective-permute-done.3
  15.4 2.8 %collective-permute-done.2 = f32[3,3,8,128]{3,2,1,0:T(8,128)S(1)} collective-permute-done((f32[3,3,8,128]{3,2,1,0:T(8,128)S(1)}, f32[3,3,8,128]{3,2,1,0:T(8,128)S(1)}, u32[]{:S(2)}, u32[]{:S(2)}) %collective-permute-start.2) | collective-permute-done | bytes 36896 | tf_op jit(solution)/shard_map/ppermute | solution.py:354
  18.2 5.4 %collective-permute-start.5 = (f32[9,3,8,128]{3,2,1,0:T(8,128)S(1)}, f32[9,3,8,128]{3,2,1,0:T(8,128)S(1)}, u32[]{:S(2)}, u32[]{:S(2)}) collective-permute-start(f32[9,3,8,128]{3,2,1,0:T(8,128)S(1)} %bitcast.13), channel_id=1, source_target_pairs={{32,0},{64,32},{96,64},{128,96},{160,128},{192,160},{224,192},{256... | collective-permute-start | bytes 331784 | tf_op jit(solution)/shard_map/ppermute | solution.py:347
  23.6 3.9 %collective-permute-start.4 = (f32[9,3,8,128]{3,2,1,0:T(8,128)S(1)}, f32[9,3,8,128]{3,2,1,0:T(8,128)S(1)}, u32[]{:S(2)}, u32[]{:S(2)}) collective-permute-start(f32[9,3,8,128]{3,2,1,0:T(8,128)S(1)} %bitcast.14), channel_id=1, source_target_pairs={{0,32},{32,64},{64,96},{96,128},{128,160},{160,192},{192,224},{224... | collective-permute-start | bytes 331784 | tf_op jit(solution)/shard_map/ppermute | solution.py:347
  27.5 9.5 %all-to-all-start = ((f32[16,3,4,128]{3,2,1,0:T(4,128)}), f32[16,3,4,128]{3,2,1,0:T(4,128)S(1)}, u32[]{:S(2)}, u32[]{:S(2)}) async-start(f32[16,3,4,128]{3,2,1,0:T(4,128)} %bitcast.10), calls=%async_computation | async-start | bytes 196608 | tf_op jit(solution)/shard_map/all_to_all | solution.py:385
  37.1 0.0 collective-permute-done.5.right_ref
  37.1 0.0 collective-permute-done.4.left_ref
  37.1 10.4 %density.1 = (f32[2,2,2,128]{3,2,1,0:T(2,128)}, f32[32,128]{1,0:T(8,128)S(1)}, bf16[64,32,128]{2,1,0:T(8,128)(2,1)S(1)}, f32[64,8,128]{2,1,0:T(8,128)S(1)}, bf16[8,128,32]{2,1,0:T(8,128)(2,1)S(1)}) custom-call(f32[9,3,8,128]{3,2,1,0:T(8,128)S(1)} %collective-permute-done.4.left_ref, f32[9,3,8,128]{3,2,1,0:T(8,128)S(1)} %bitcast.15, ...), custom_call_target="tpu_custom_call" | custom-call | flops 6000000000 | bytes 262144 | tf_op jit(solution)/shard_map/density/pallas_call | solution.py:390
  47.5 2.0 %collective-permute-start.7 = (f32[32,128]{1,0:T(8,128)S(1)}, f32[32,128]{1,0:T(8,128)S(1)}, u32[]{:S(2)}, u32[]{:S(2)}) collective-permute-start(f32[32,128]{1,0:T(8,128)S(1)} %get-tuple-element.22.press_ref.mid_ref), channel_id=1, source_target_pairs={{32,0},{64,32},{96,64},{128,96},{160,128},{192,160},{224,192},{256... | collective-permute-start | bytes 49160 | tf_op jit(solution)/shard_map/ppermute | solution.py:347
  49.5 3.5 %collective-permute-start.6 = (f32[32,128]{1,0:T(8,128)S(1)}, f32[32,128]{1,0:T(8,128)S(1)}, u32[]{:S(2)}, u32[]{:S(2)}) collective-permute-start(f32[32,128]{1,0:T(8,128)S(1)} %get-tuple-element.22.press_ref.mid_ref), channel_id=1, source_target_pairs={{0,32},{32,64},{64,96},{96,128},{128,160},{160,192},{192,224},{224... | collective-permute-start | bytes 49160 | tf_op jit(solution)/shard_map/ppermute | solution.py:347
  53.1 0.0 all-to-all-done
  53.1 9.3 %bodies.1 = (f32[3,8,128]{2,1,0:T(8,128)S(1)}, f32[16,8,128]{2,1,0:T(8,128)}) custom-call(f32[48,4,128]{2,1,0:T(4,128)S(1)} %bitcast.16, f32[3,8,128]{2,1,0:T(8,128)S(1)} %place.1.pos_ref, f32[32,128]{1,0:T(8,128)S(1)} %get-tuple-element.22.press_ref.mid_ref), custom_call_target="tpu_custom_call" | custom-call | flops 6000000000 | bytes 262144 | tf_op jit(solution)/shard_map/bodies/pallas_call | solution.py:416
  62.3 7.0 %all-to-all-start.1 = ((f32[16,8,128]{2,1,0:T(8,128)}), f32[16,8,128]{2,1,0:T(8,128)S(1)}, u32[]{:S(2)}, u32[]{:S(2)}) async-start(f32[16,8,128]{2,1,0:T(8,128)} %get-tuple-element.26), calls=%async_computation.1 | async-start | bytes 131072 | tf_op jit(solution)/shard_map/all_to_all | solution.py:435
  69.3 0.0 collective-permute-done.7.right_ref
  69.3 0.0 collective-permute-done.6.left_ref
  69.3 6.6 %accel.1 = f32[3,2,2,2,128]{4,3,2,1,0:T(2,128)} custom-call(bf16[8,128,32]{2,1,0:T(8,128)(2,1)S(1)} %get-tuple-element.19.own_ref, bf16[64,32,128]{2,1,0:T(8,128)(2,1)S(1)} %get-tuple-element.20.near_ref, f32[64,8,128]{2,1,0:T(8,128)S(1)} %get-tuple-element.21.coord_ref, f32[32,128]{1,0:T(8,128)S(1)} %collective-permute-done.6.left_ref, ...), custom_call_target="tpu_custom_call" | custom-call | flops 4000000000 | bytes 262144 | tf_op jit(solution)/shard_map/accel/pallas_call | solution.py:436
  75.9 1.2 %all-to-all-done.1.got_ref = f32[16,8,128]{2,1,0:T(8,128)S(1)} async-done(((f32[16,8,128]{2,1,0:T(8,128)}), f32[16,8,128]{2,1,0:T(8,128)S(1)}, u32[]{:S(2)}, u32[]{:S(2)}) %all-to-all-start.1) | async-done | bytes 65568 | tf_op jit(solution)/shard_map/all_to_all | solution.py:435
  77.1 1.5 %collect.1 = f32[6,24]{1,0:T(8,128)} custom-call(s32[24]{0:T(128)} %get-tuple-element.25.slot_ref, f32[16,8,128]{2,1,0:T(8,128)S(1)} %all-to-all-done.1.got_ref), custom_call_target="tpu_custom_call" | custom-call | flops 100000000 | bytes 262144 | tf_op jit(solution)/shard_map/collect/pallas_call | solution.py:450
  (2 shorter events, 0.0 us)
Async XLA Ops:
  1.5 6.7 %collective-permute-start.1 = (f32[3,8,128]{2,1,0:T(8,128)S(1)}, f32[3,8,128]{2,1,0:T(8,128)S(1)}, u32[]{:S(2)}, u32[]{:S(2)}) collective-permute-start(f32[3,8,128]{2,1,0:T(8,128)S(1)} %place.1.pos_ref), channel_id=1, source_target_pairs={{1,2},{2,1},{5,6},{6,5},{9,10},{10,9},{13,14},{14,13},{17,18},{18,... | collective-permute-start | bytes 36872 | tf_op jit(solution)/shard_map/ppermute | solution.py:354
  4.6 4.4 %collective-permute-start = (f32[3,8,128]{2,1,0:T(8,128)S(1)}, f32[3,8,128]{2,1,0:T(8,128)S(1)}, u32[]{:S(2)}, u32[]{:S(2)}) collective-permute-start(f32[3,8,128]{2,1,0:T(8,128)S(1)} %place.1.pos_ref), channel_id=1, source_target_pairs={{0,1},{1,0},{2,3},{3,2},{4,5},{5,4},{6,7},{7,6},{8,9},{9,8},{10,11... | collective-permute-start | bytes 36872 | tf_op jit(solution)/shard_map/ppermute | solution.py:354
  9.0 6.3 %collective-permute-start.3 = (f32[3,3,8,128]{3,2,1,0:T(8,128)S(1)}, f32[3,3,8,128]{3,2,1,0:T(8,128)S(1)}, u32[]{:S(2)}, u32[]{:S(2)}) collective-permute-start(f32[3,3,8,128]{3,2,1,0:T(8,128)S(1)} %get-tuple-element.28), channel_id=1, source_target_pairs={{4,8},{8,4},{12,16},{16,12},{20,24},{24,20},{5,9},{9,5},{13,17},{1... | collective-permute-start | bytes 110600 | tf_op jit(solution)/shard_map/ppermute | solution.py:354
  13.5 4.7 %collective-permute-start.2 = (f32[3,3,8,128]{3,2,1,0:T(8,128)S(1)}, f32[3,3,8,128]{3,2,1,0:T(8,128)S(1)}, u32[]{:S(2)}, u32[]{:S(2)}) collective-permute-start(f32[3,3,8,128]{3,2,1,0:T(8,128)S(1)} %get-tuple-element.28), channel_id=1, source_target_pairs={{0,4},{4,0},{8,12},{12,8},{16,20},{20,16},{24,28},{28,24},{1,5},{5... | collective-permute-start | bytes 110600 | tf_op jit(solution)/shard_map/ppermute | solution.py:354
  18.2 18.9 %collective-permute-start.5 = (f32[9,3,8,128]{3,2,1,0:T(8,128)S(1)}, f32[9,3,8,128]{3,2,1,0:T(8,128)S(1)}, u32[]{:S(2)}, u32[]{:S(2)}) collective-permute-start(f32[9,3,8,128]{3,2,1,0:T(8,128)S(1)} %bitcast.13), channel_id=1, source_target_pairs={{32,0},{64,32},{96,64},{128,96},{160,128},{192,160},{224,192},{256... | collective-permute-start | bytes 331784 | tf_op jit(solution)/shard_map/ppermute | solution.py:347
  23.6 13.5 %collective-permute-start.4 = (f32[9,3,8,128]{3,2,1,0:T(8,128)S(1)}, f32[9,3,8,128]{3,2,1,0:T(8,128)S(1)}, u32[]{:S(2)}, u32[]{:S(2)}) collective-permute-start(f32[9,3,8,128]{3,2,1,0:T(8,128)S(1)} %bitcast.14), channel_id=1, source_target_pairs={{0,32},{32,64},{64,96},{96,128},{128,160},{160,192},{192,224},{224... | collective-permute-start | bytes 331784 | tf_op jit(solution)/shard_map/ppermute | solution.py:347
  27.5 25.5 %all-to-all-start = ((f32[16,3,4,128]{3,2,1,0:T(4,128)}), f32[16,3,4,128]{3,2,1,0:T(4,128)S(1)}, u32[]{:S(2)}, u32[]{:S(2)}) async-start(f32[16,3,4,128]{3,2,1,0:T(4,128)} %bitcast.10), calls=%async_computation | async-start | bytes 196608 | tf_op jit(solution)/shard_map/all_to_all | solution.py:385
  47.5 21.8 %collective-permute-start.7 = (f32[32,128]{1,0:T(8,128)S(1)}, f32[32,128]{1,0:T(8,128)S(1)}, u32[]{:S(2)}, u32[]{:S(2)}) collective-permute-start(f32[32,128]{1,0:T(8,128)S(1)} %get-tuple-element.22.press_ref.mid_ref), channel_id=1, source_target_pairs={{32,0},{64,32},{96,64},{128,96},{160,128},{192,160},{224,192},{256... | collective-permute-start | bytes 49160 | tf_op jit(solution)/shard_map/ppermute | solution.py:347
  49.5 19.8 %collective-permute-start.6 = (f32[32,128]{1,0:T(8,128)S(1)}, f32[32,128]{1,0:T(8,128)S(1)}, u32[]{:S(2)}, u32[]{:S(2)}) collective-permute-start(f32[32,128]{1,0:T(8,128)S(1)} %get-tuple-element.22.press_ref.mid_ref), channel_id=1, source_target_pairs={{0,32},{32,64},{64,96},{96,128},{128,160},{160,192},{192,224},{224... | collective-permute-start | bytes 49160 | tf_op jit(solution)/shard_map/ppermute | solution.py:347
  62.3 14.8 %all-to-all-start.1 = ((f32[16,8,128]{2,1,0:T(8,128)}), f32[16,8,128]{2,1,0:T(8,128)S(1)}, u32[]{:S(2)}, u32[]{:S(2)}) async-start(f32[16,8,128]{2,1,0:T(8,128)} %get-tuple-element.26), calls=%async_computation.1 | async-start | bytes 131072 | tf_op jit(solution)/shard_map/all_to_all | solution.py:435

commit v6 on v4

--- a/solution.py
+++ b/solution.py
@@ -78,7 +78,7 @@
         dest = dest_ref[0, b]
         rank = tally_ref[dest]
         tally_ref[dest] = rank + 1
-        slot_ref[b] = dest * 8 + rank
+        slot_ref[b] = rank * groups + dest
         slot = dest * CAPACITY + rank
         send_ref[slot, 0:3, :] = shape_ref[:, b, :]
         send_ref[slot, 3:4, :] = extra_ref[b:b + 1, :]
@@ -183,7 +183,7 @@
             rho_ref[a, e] = density[r:r + 2, :]
 
 
-def body_kernel(recv_ref, pos_ref, press_ref, force_ref, load_ref, list_ref, fa_ref, anchor_ref, near_ref, side_ref, half_ref, arm_ref, sums_ref):
+def body_kernel(recv_ref, pos_ref, press_ref, force_ref, load_ref, list_ref, fa_ref, anchor_ref, near_ref, side_ref, half_ref, arm_ref, sums_ref, wide_ref):
     slots = recv_ref.shape[0]
     blank = jnp.zeros((8, SLOTS), F32)
     near_ref[:, 192:, :] = jnp.zeros((TOGETHER, 64, SLOTS), F32)
@@ -248,9 +248,14 @@
 
     lax.fori_loop(0, slots // TOGETHER, step, 0)
     total = jnp.sum(sums_ref[...], axis=2)
-    load_ref[...] = jnp.zeros_like(load_ref)
-    for g in range(slots // CAPACITY):
-        load_ref[g, 0:CAPACITY, 0:8] = total[CAPACITY * g:CAPACITY * g + CAPACITY, :]
+    groups = slots // CAPACITY
+    wide_ref[...] = jnp.concatenate([total, jnp.zeros((slots, SLOTS - 8), F32)], axis=1)
+    mixed = sum(
+        pltpu.roll(wide_ref[pl.ds(r, groups, stride=CAPACITY), :], 8 * r, 1) if r else wide_ref[pl.ds(0, groups, stride=CAPACITY), :]
+        for r in range(CAPACITY)
+    )
+    for g in range(groups):
+        load_ref[g] = mixed[g:g + 1, :]
 
 
 def accel_kernel(own_ref, near_ref, coord_ref, left_ref, mid_ref, right_ref, force_ref, out_ref, press_ref, col_ref, line_ref):
@@ -303,11 +308,15 @@
     lax.fori_loop(0, 8, cell, 0, unroll=8)
 
 
-def gather_kernel(slot_ref, got_ref, out_ref, pick_ref):
+def gather_kernel(slot_ref, got_ref, out_ref, pick_ref, roll_ref):
     bodies = out_ref.shape[1]
+    groups = got_ref.shape[0]
+    for g in range(groups):
+        roll_ref[g:g + 1, :] = got_ref[g]
+    for r in range(1, CAPACITY):
+        roll_ref[r * groups:(r + 1) * groups, :] = pltpu.roll(roll_ref[0:groups, :], SLOTS - 8 * r, 1)
     for b in range(bodies):
-        place = slot_ref[b]
-        pick_ref[b:b + 1, :] = got_ref[place // 8, pl.ds(place % 8, 1), :]
+        pick_ref[b:b + 1, :] = roll_ref[pl.ds(slot_ref[b], 1), :]
     out_ref[...] = pick_ref[...].T[0:6, :] / BODY_PARTS
 
 
@@ -403,7 +412,7 @@
     press_left, press_right = both_ways(press, "gx")
     force, load = pl.pallas_call(
         body_kernel,
-        out_shape=(inner(3, 8, SLOTS), inner(groups, 8, SLOTS)),
+        out_shape=(inner(3, 8, SLOTS), inner(groups, 1, SLOTS)),
         in_specs=[vmem(), vmem(), vmem()],
         out_specs=(vmem(), vmem()),
         scratch_shapes=[
@@ -415,6 +424,7 @@
             pltpu.VMEM((TOGETHER, 64, SLOTS), F32),
             pltpu.VMEM((16 * slots, SLOTS), F32),
             pltpu.VMEM((slots, 8, SLOTS), F32),
+            pltpu.VMEM((slots, SLOTS), F32),
         ],
         compiler_params=params(),
         cost_estimate=cost(60),
@@ -440,7 +450,7 @@
         out_shape=shaped(6, bodies),
         in_specs=[smem(), vmem()],
         out_specs=vmem(),
-        scratch_shapes=[pltpu.VMEM((bodies, SLOTS), F32)],
+        scratch_shapes=[pltpu.VMEM((bodies, SLOTS), F32), pltpu.VMEM((slots, SLOTS), F32)],
         compiler_params=params(),
         cost_estimate=cost(1),
         name="collect",

time: 77.4 us -> 76.6 us (0.990)
  waiting for transfers between devices: 5.43 us -> 4.64 us
    all_to_all x1, waiting for transfers between devices: 1.18 us -> 0.4 us  [local(): got = lax.all_to_all(load, 'gx', 0, 0, tiled=True)]
  transfers between devices with their start and end apart: 10 -> 10, of which waited for: 3 -> 3; matrix products, arithmetic and copies ran while one was open for 0% -> 0% of each run, Pallas kernels for 36% -> 37%
where the time goes in v6:
time: 76.6 us; the launch traced here: 76 us
  starting transfers between devices  40.4 us (53%)
  Pallas kernels  30.1 us (39%)
  waiting for transfers between devices  4.64 us (6%)
    ppermute x8, starting transfers between devices, both_ways(): return (lax.ppermute(value, axis, ups), lax.ppermute(value, axis, downs))  23.9 us
    pallas_call x1, Pallas kernels, local(): pl.pallas_call(density_kernel, out_shape=(shaped(2, 2, 2, SLOTS), inner(3...  10.4 us
    all_to_all x1, starting transfers between devices, local(): lax.all_to_all(send.reshape(groups, CAPACITY, 4, SLOTS), 'gx', 0, 0, tile...  9.54 us
    pallas_call x1, Pallas kernels, local(): pl.pallas_call(body_kernel, out_shape=(inner(3, 8, SLOTS), inner(groups,...  9.32 us
    all_to_all x1, starting transfers between devices, local(): got = lax.all_to_all(load, 'gx', 0, 0, tiled=True)  6.98 us
    pallas_call x1, Pallas kernels, local(): pl.pallas_call(accel_kernel, out_shape=shaped(3, 2, 2, 2, SLOTS), in_spec...  6.61 us
    ppermute x8, waiting for transfers between devices, both_ways(): return (lax.ppermute(value, axis, ups), lax.ppermute(value, axis, downs))  4.24 us
    pallas_call x1, Pallas kernels, local(): pl.pallas_call(pack_kernel, out_shape=(inner(slots, 4, SLOTS), shaped(bod...  1.59 us
  transfers between devices with their start and end apart: 10, of which 3 were waited for; matrix products, arithmetic and copies ran while one was open for 0% of the time, Pallas kernels for 37%

profile of v6, /device:TPU:39, one launch (start us, length us, event | category | flops | bytes accessed | tf_op | source)
XLA Modules:
  0.0 76.0 jit_solution(4410839303150686897)
XLA Ops:
  0.6 0.8 %place.1.pos_ref = f32[3,8,128]{2,1,0:T(8,128)S(1)} custom-call(f32[3,2,2,2,128]{4,3,2,1,0:T(2,128)} %pos_ref.1, s32[2,2,2]{2,1,0:T(2,128)} %count_ref.1), custom_call_target="tpu_custom_call" | custom-call | tf_op jit(solution)/shard_map/place/pallas_call | solution.py:362
  1.5 2.5 %collective-permute-start.1 = (f32[3,8,128]{2,1,0:T(8,128)S(1)}, f32[3,8,128]{2,1,0:T(8,128)S(1)}, u32[]{:S(2)}, u32[]{:S(2)}) collective-permute-start(f32[3,8,128]{2,1,0:T(8,128)S(1)} %place.1.pos_ref), channel_id=1, source_target_pairs={{1,0},{2,1},{3,2},{5,4},{6,5},{7,6},{9,8},{10,9},{11,10},{13,12},{... | collective-permute-start | bytes 36872 | tf_op jit(solution)/shard_map/ppermute | solution.py:351
  3.9 1.3 %collective-permute-start = (f32[3,8,128]{2,1,0:T(8,128)S(1)}, f32[3,8,128]{2,1,0:T(8,128)S(1)}, u32[]{:S(2)}, u32[]{:S(2)}) collective-permute-start(f32[3,8,128]{2,1,0:T(8,128)S(1)} %place.1.pos_ref), channel_id=1, source_target_pairs={{0,1},{1,2},{2,3},{4,5},{5,6},{6,7},{8,9},{9,10},{10,11},{12,13},{... | collective-permute-start | bytes 36872 | tf_op jit(solution)/shard_map/ppermute | solution.py:351
  5.2 1.6 %pack.1 = (f32[48,4,128]{2,1,0:T(4,128)}, s32[24]{0:T(128)}) custom-call(f32[3,24,128]{2,1,0:T(8,128)} %shape_ref.1, f32[3,8,24]{2,1,0:T(8,128)} %bitcast.22, s32[1,24]{1,0:T(1,128)} %bitcast.24, s32[8,24]{1,0:T(8,128)} %bitcast.23), custom_call_target="tpu_custom_call" | custom-call | flops 400000000 | bytes 262144 | tf_op jit(solution)/shard_map/pack/pallas_call | solution.py:370
  6.8 0.0 collective-permute-done.1
  6.8 1.5 %collective-permute-done = f32[3,8,128]{2,1,0:T(8,128)S(1)} collective-permute-done((f32[3,8,128]{2,1,0:T(8,128)S(1)}, f32[3,8,128]{2,1,0:T(8,128)S(1)}, u32[]{:S(2)}, u32[]{:S(2)}) %collective-permute-start) | collective-permute-done | bytes 12320 | tf_op jit(solution)/shard_map/ppermute | solution.py:351
  8.4 2.1 %collective-permute-start.3 = (f32[3,3,8,128]{3,2,1,0:T(8,128)S(1)}, f32[3,3,8,128]{3,2,1,0:T(8,128)S(1)}, u32[]{:S(2)}, u32[]{:S(2)}) collective-permute-start(f32[3,3,8,128]{3,2,1,0:T(8,128)S(1)} %get-tuple-element.28), channel_id=1, source_target_pairs={{4,0},{8,4},{12,8},{16,12},{20,16},{24,20},{28,24},{5,1},{9,5},{13... | collective-permute-start | bytes 110600 | tf_op jit(solution)/shard_map/ppermute | solution.py:351
  10.4 3.2 %collective-permute-start.2 = (f32[3,3,8,128]{3,2,1,0:T(8,128)S(1)}, f32[3,3,8,128]{3,2,1,0:T(8,128)S(1)}, u32[]{:S(2)}, u32[]{:S(2)}) collective-permute-start(f32[3,3,8,128]{3,2,1,0:T(8,128)S(1)} %get-tuple-element.28), channel_id=1, source_target_pairs={{0,4},{4,8},{8,12},{12,16},{16,20},{20,24},{24,28},{1,5},{5,9},{9,... | collective-permute-start | bytes 110600 | tf_op jit(solution)/shard_map/ppermute | solution.py:351
  13.7 0.0 collective-permute-done.3
  13.7 2.7 %collective-permute-done.2 = f32[3,3,8,128]{3,2,1,0:T(8,128)S(1)} collective-permute-done((f32[3,3,8,128]{3,2,1,0:T(8,128)S(1)}, f32[3,3,8,128]{3,2,1,0:T(8,128)S(1)}, u32[]{:S(2)}, u32[]{:S(2)}) %collective-permute-start.2) | collective-permute-done | bytes 36896 | tf_op jit(solution)/shard_map/ppermute | solution.py:351
  16.4 5.4 %collective-permute-start.5 = (f32[9,3,8,128]{3,2,1,0:T(8,128)S(1)}, f32[9,3,8,128]{3,2,1,0:T(8,128)S(1)}, u32[]{:S(2)}, u32[]{:S(2)}) collective-permute-start(f32[9,3,8,128]{3,2,1,0:T(8,128)S(1)} %bitcast.13), channel_id=1, source_target_pairs={{32,0},{64,32},{96,64},{128,96},{160,128},{192,160},{224,192},{256... | collective-permute-start | bytes 331784 | tf_op jit(solution)/shard_map/ppermute | solution.py:351
  21.8 3.9 %collective-permute-start.4 = (f32[9,3,8,128]{3,2,1,0:T(8,128)S(1)}, f32[9,3,8,128]{3,2,1,0:T(8,128)S(1)}, u32[]{:S(2)}, u32[]{:S(2)}) collective-permute-start(f32[9,3,8,128]{3,2,1,0:T(8,128)S(1)} %bitcast.14), channel_id=1, source_target_pairs={{0,32},{32,64},{64,96},{96,128},{128,160},{160,192},{192,224},{224... | collective-permute-start | bytes 331784 | tf_op jit(solution)/shard_map/ppermute | solution.py:351
  25.7 9.5 %all-to-all-start = ((f32[16,3,4,128]{3,2,1,0:T(4,128)}), f32[16,3,4,128]{3,2,1,0:T(4,128)S(1)}, u32[]{:S(2)}, u32[]{:S(2)}) async-start(f32[16,3,4,128]{3,2,1,0:T(4,128)} %bitcast.10), calls=%async_computation | async-start | bytes 196608 | tf_op jit(solution)/shard_map/all_to_all | solution.py:382
  35.3 0.0 collective-permute-done.5.right_ref
  35.3 0.0 collective-permute-done.4.left_ref
  35.3 10.4 %density.1 = (f32[2,2,2,128]{3,2,1,0:T(2,128)}, f32[32,128]{1,0:T(8,128)S(1)}, bf16[64,32,128]{2,1,0:T(8,128)(2,1)S(1)}, f32[64,8,128]{2,1,0:T(8,128)S(1)}, bf16[8,128,32]{2,1,0:T(8,128)(2,1)S(1)}) custom-call(f32[9,3,8,128]{3,2,1,0:T(8,128)S(1)} %collective-permute-done.4.left_ref, f32[9,3,8,128]{3,2,1,0:T(8,128)S(1)} %bitcast.15, ...), custom_call_target="tpu_custom_call" | custom-call | flops 6000000000 | bytes 262144 | tf_op jit(solution)/shard_map/density/pallas_call | solution.py:387
  45.7 2.0 %collective-permute-start.7 = (f32[32,128]{1,0:T(8,128)S(1)}, f32[32,128]{1,0:T(8,128)S(1)}, u32[]{:S(2)}, u32[]{:S(2)}) collective-permute-start(f32[32,128]{1,0:T(8,128)S(1)} %get-tuple-element.22.press_ref.mid_ref), channel_id=1, source_target_pairs={{32,0},{64,32},{96,64},{128,96},{160,128},{192,160},{224,192},{256... | collective-permute-start | bytes 49160 | tf_op jit(solution)/shard_map/ppermute | solution.py:351
  47.7 3.6 %collective-permute-start.6 = (f32[32,128]{1,0:T(8,128)S(1)}, f32[32,128]{1,0:T(8,128)S(1)}, u32[]{:S(2)}, u32[]{:S(2)}) collective-permute-start(f32[32,128]{1,0:T(8,128)S(1)} %get-tuple-element.22.press_ref.mid_ref), channel_id=1, source_target_pairs={{0,32},{32,64},{64,96},{96,128},{128,160},{160,192},{192,224},{224... | collective-permute-start | bytes 49160 | tf_op jit(solution)/shard_map/ppermute | solution.py:351
  51.2 0.0 all-to-all-done
  51.3 9.3 %bodies.1 = (f32[3,8,128]{2,1,0:T(8,128)S(1)}, f32[16,1,128]{2,1,0:T(1,128)}) custom-call(f32[48,4,128]{2,1,0:T(4,128)S(1)} %bitcast.16, f32[3,8,128]{2,1,0:T(8,128)S(1)} %place.1.pos_ref, f32[32,128]{1,0:T(8,128)S(1)} %get-tuple-element.22.press_ref.mid_ref), custom_call_target="tpu_custom_call" | custom-call | flops 6000000000 | bytes 262144 | tf_op jit(solution)/shard_map/bodies/pallas_call | solution.py:413
  60.6 7.0 %all-to-all-start.1 = ((f32[16,1,128]{2,1,0:T(1,128)}), f32[16,1,128]{2,1,0:T(1,128)S(1)}, u32[]{:S(2)}, u32[]{:S(2)}) async-start(f32[16,1,128]{2,1,0:T(1,128)} %get-tuple-element.26), calls=%async_computation.1 | async-start | bytes 16384 | tf_op jit(solution)/shard_map/all_to_all | solution.py:433
  67.6 0.0 collective-permute-done.7.right_ref
  67.6 0.0 collective-permute-done.6.left_ref
  67.6 6.6 %accel.1 = f32[3,2,2,2,128]{4,3,2,1,0:T(2,128)} custom-call(bf16[8,128,32]{2,1,0:T(8,128)(2,1)S(1)} %get-tuple-element.19.own_ref, bf16[64,32,128]{2,1,0:T(8,128)(2,1)S(1)} %get-tuple-element.20.near_ref, f32[64,8,128]{2,1,0:T(8,128)S(1)} %get-tuple-element.21.coord_ref, f32[32,128]{1,0:T(8,128)S(1)} %collective-permute-done.6.left_ref, ...), custom_call_target="tpu_custom_call" | custom-call | flops 4000000000 | bytes 262144 | tf_op jit(solution)/shard_map/accel/pallas_call | solution.py:434
  74.2 0.4 all-to-all-done.1.got_ref
  74.6 1.4 %collect.1 = f32[6,24]{1,0:T(8,128)} custom-call(s32[24]{0:T(128)} %get-tuple-element.25.slot_ref, f32[16,1,128]{2,1,0:T(1,128)S(1)} %all-to-all-done.1.got_ref), custom_call_target="tpu_custom_call" | custom-call | flops 100000000 | bytes 262144 | tf_op jit(solution)/shard_map/collect/pallas_call | solution.py:448
  (2 shorter events, 0.0 us)
Async XLA Ops:
  1.5 5.4 %collective-permute-start.1 = (f32[3,8,128]{2,1,0:T(8,128)S(1)}, f32[3,8,128]{2,1,0:T(8,128)S(1)}, u32[]{:S(2)}, u32[]{:S(2)}) collective-permute-start(f32[3,8,128]{2,1,0:T(8,128)S(1)} %place.1.pos_ref), channel_id=1, source_target_pairs={{1,0},{2,1},{3,2},{5,4},{6,5},{7,6},{9,8},{10,9},{11,10},{13,12},{... | collective-permute-start | bytes 36872 | tf_op jit(solution)/shard_map/ppermute | solution.py:351
  3.9 4.4 %collective-permute-start = (f32[3,8,128]{2,1,0:T(8,128)S(1)}, f32[3,8,128]{2,1,0:T(8,128)S(1)}, u32[]{:S(2)}, u32[]{:S(2)}) collective-permute-start(f32[3,8,128]{2,1,0:T(8,128)S(1)} %place.1.pos_ref), channel_id=1, source_target_pairs={{0,1},{1,2},{2,3},{4,5},{5,6},{6,7},{8,9},{9,10},{10,11},{12,13},{... | collective-permute-start | bytes 36872 | tf_op jit(solution)/shard_map/ppermute | solution.py:351
  8.4 5.3 %collective-permute-start.3 = (f32[3,3,8,128]{3,2,1,0:T(8,128)S(1)}, f32[3,3,8,128]{3,2,1,0:T(8,128)S(1)}, u32[]{:S(2)}, u32[]{:S(2)}) collective-permute-start(f32[3,3,8,128]{3,2,1,0:T(8,128)S(1)} %get-tuple-element.28), channel_id=1, source_target_pairs={{4,0},{8,4},{12,8},{16,12},{20,16},{24,20},{28,24},{5,1},{9,5},{13... | collective-permute-start | bytes 110600 | tf_op jit(solution)/shard_map/ppermute | solution.py:351
  10.4 5.9 %collective-permute-start.2 = (f32[3,3,8,128]{3,2,1,0:T(8,128)S(1)}, f32[3,3,8,128]{3,2,1,0:T(8,128)S(1)}, u32[]{:S(2)}, u32[]{:S(2)}) collective-permute-start(f32[3,3,8,128]{3,2,1,0:T(8,128)S(1)} %get-tuple-element.28), channel_id=1, source_target_pairs={{0,4},{4,8},{8,12},{12,16},{16,20},{20,24},{24,28},{1,5},{5,9},{9,... | collective-permute-start | bytes 110600 | tf_op jit(solution)/shard_map/ppermute | solution.py:351
  16.4 18.9 %collective-permute-start.5 = (f32[9,3,8,128]{3,2,1,0:T(8,128)S(1)}, f32[9,3,8,128]{3,2,1,0:T(8,128)S(1)}, u32[]{:S(2)}, u32[]{:S(2)}) collective-permute-start(f32[9,3,8,128]{3,2,1,0:T(8,128)S(1)} %bitcast.13), channel_id=1, source_target_pairs={{32,0},{64,32},{96,64},{128,96},{160,128},{192,160},{224,192},{256... | collective-permute-start | bytes 331784 | tf_op jit(solution)/shard_map/ppermute | solution.py:351
  21.8 13.5 %collective-permute-start.4 = (f32[9,3,8,128]{3,2,1,0:T(8,128)S(1)}, f32[9,3,8,128]{3,2,1,0:T(8,128)S(1)}, u32[]{:S(2)}, u32[]{:S(2)}) collective-permute-start(f32[9,3,8,128]{3,2,1,0:T(8,128)S(1)} %bitcast.14), channel_id=1, source_target_pairs={{0,32},{32,64},{64,96},{96,128},{128,160},{160,192},{192,224},{224... | collective-permute-start | bytes 331784 | tf_op jit(solution)/shard_map/ppermute | solution.py:351
  25.7 25.5 %all-to-all-start = ((f32[16,3,4,128]{3,2,1,0:T(4,128)}), f32[16,3,4,128]{3,2,1,0:T(4,128)S(1)}, u32[]{:S(2)}, u32[]{:S(2)}) async-start(f32[16,3,4,128]{3,2,1,0:T(4,128)} %bitcast.10), calls=%async_computation | async-start | bytes 196608 | tf_op jit(solution)/shard_map/all_to_all | solution.py:382
  45.7 21.9 %collective-permute-start.7 = (f32[32,128]{1,0:T(8,128)S(1)}, f32[32,128]{1,0:T(8,128)S(1)}, u32[]{:S(2)}, u32[]{:S(2)}) collective-permute-start(f32[32,128]{1,0:T(8,128)S(1)} %get-tuple-element.22.press_ref.mid_ref), channel_id=1, source_target_pairs={{32,0},{64,32},{96,64},{128,96},{160,128},{192,160},{224,192},{256... | collective-permute-start | bytes 49160 | tf_op jit(solution)/shard_map/ppermute | solution.py:351
  47.7 19.9 %collective-permute-start.6 = (f32[32,128]{1,0:T(8,128)S(1)}, f32[32,128]{1,0:T(8,128)S(1)}, u32[]{:S(2)}, u32[]{:S(2)}) collective-permute-start(f32[32,128]{1,0:T(8,128)S(1)} %get-tuple-element.22.press_ref.mid_ref), channel_id=1, source_target_pairs={{0,32},{32,64},{64,96},{96,128},{128,160},{160,192},{192,224},{224... | collective-permute-start | bytes 49160 | tf_op jit(solution)/shard_map/ppermute | solution.py:351
  60.6 14.0 %all-to-all-start.1 = ((f32[16,1,128]{2,1,0:T(1,128)}), f32[16,1,128]{2,1,0:T(1,128)S(1)}, u32[]{:S(2)}, u32[]{:S(2)}) async-start(f32[16,1,128]{2,1,0:T(1,128)} %get-tuple-element.26), calls=%async_computation.1 | async-start | bytes 16384 | tf_op jit(solution)/shard_map/all_to_all | solution.py:433
